TPU v7x, 768 devices: a whole 4x8x12 slice. The times are simulated.
768 devices in a mesh: pipe: 6 (over z_lo), seq: 32 (over y, z_hi, core), fsdp: 4 (over x).
Axes of the slice: x: 4, y: 8, z: 12 (z_hi: 2, z_lo: 6; z = z_hi * 6 + z_lo), core: 2. Of those that a mesh axis runs over, the one named last changes fastest.
Arguments:
- embedded: bfloat16 [4096, 2688], P('seq', 'fsdp'), may hold values from -6 to 6
- sent_forward: bfloat16 [6, 4096, 2688], P('pipe', 'seq', 'fsdp'), may hold values from -6 to 6
- stashed: bfloat16 [6, 4096, 2688], P('pipe', 'seq', 'fsdp'), may hold values from -6 to 6
- sent_backward: bfloat16 [6, 4096, 2688], P('pipe', 'seq', 'fsdp'), may hold values from -6 to 6
- loss_grad: bfloat16 [4096, 2688], P('seq', 'fsdp'), may hold values from -6 to 6
- norm_gain: float32 [6, 2688], P('pipe'), may hold values from 0.5 to 2
- w_query: bfloat16 [6, 2688, 2048], P('pipe', None, 'fsdp'), may hold values from -1 to 1
- w_key: bfloat16 [6, 2688, 1024], P('pipe', None, 'fsdp'), may hold values from -1 to 1
- value_projection: bfloat16 [6, 2688, 1024], P('pipe', None, 'fsdp'), may hold values from -0.125 to 0.125
- w_out: bfloat16 [6, 2048, 2688], P('pipe', 'fsdp'), may hold values from -0.125 to 0.125
- forward_docs: int32 [6, 4096], P('pipe'), may hold values from 0 to 3, never falling along the last dimension, each value on 1 to 2048 neighbouring positions
- backward_docs: int32 [6, 4096], P('pipe'), may hold values from 0 to 3, never falling along the last dimension, each value on 1 to 2048 neighbouring positions
Outputs:
- forward_out: bfloat16 [6, 4096, 2688], P('pipe', 'seq', 'fsdp')
- input_grad: bfloat16 [6, 4096, 2688], P('pipe', 'seq', 'fsdp')
Inputs may be any that keep to these rules, and one draw needn't show every extreme that they name: `forward_docs`: document numbers never fall along a sequence; every document is a run of 1 to 2048 tokens. `backward_docs`: document numbers never fall along a sequence; every document is a run of 1 to 2048 tokens.
All inputs are finite; a program needn't handle non-finite values.
Results may differ from a plain program's by a relative error of at most 0.015.
Values may be sent and summed in bfloat16 or wider, within the bound.
No kernel may reach another device: no remote copies, remote signals or barrier semaphores. Data moves between devices by JAX's collectives and lax.ppermute only.
A program may use at most 64 MiB of HBM per device.

v0:
```python
import jax
import jax.numpy as jnp
from jax import lax
from jax.sharding import PartitionSpec as P

QUERY_HEADS = 16
KEY_VALUE_HEADS = 8
HEAD_SIZE = 128
WINDOW_TOKENS = 512


def from_behind(value, axis, steps):
    count = lax.axis_size(axis)
    initial, last = (max(0, -steps), min(count, count - steps))
    return lax.ppermute(value, axis, [(source, source + steps) for source in range(initial, last)])


def normalize(rows_in, gain):
    value_rows = rows_in.astype(jnp.float32)
    row_scale_factor = lax.rsqrt(jnp.mean(value_rows * value_rows, axis=-1, keepdims=True) + 1e-06)
    return ((value_rows * row_scale_factor * gain).astype(jnp.bfloat16), row_scale_factor)


def block_probs(query_block, k_block, q_pos, k_pos, q_doc, k_doc):
    scores = jnp.einsum("qhgd,khd->hgqk", query_block, k_block, preferred_element_type=jnp.float32)
    scores = scores * HEAD_SIZE ** (-0.5)
    keep = (k_pos[None, :] <= q_pos[:, None]) & (q_pos[:, None] - k_pos[None, :] < WINDOW_TOKENS)
    keep = keep & (k_doc[None, :] == q_doc[:, None])
    scores = jnp.where(keep, scores, -1e30)
    top = jnp.max(scores, axis=-1, keepdims=True)
    expo = jnp.exp(scores - top)
    return expo / jnp.sum(expo, axis=-1, keepdims=True)


def near_rows(both, hops):
    pieces = [from_behind(both, "seq", distance) for distance in range(hops, 0, -1)]
    return jnp.concatenate(pieces + [both], 0)


def return_terms(terms, hops, length):
    total = jnp.zeros((length, terms.shape[1]), jnp.float32)
    for distance in range(1, hops + 1):
        piece = terms[(hops - distance) * length : (hops - distance + 1) * length]
        total = total + from_behind(piece.astype(jnp.bfloat16), "seq", -distance).astype(
            piece.dtype
        )
    return total


def contract_last(left, right):
    return lax.dot_general(
        left, right, (((1,), (1,)), ((), ())), preferred_element_type=jnp.float32
    )


def per_device(
    embedded,
    sent_forward,
    stashed,
    sent_backward,
    loss_grad,
    norm_gain,
    w_query,
    w_key,
    value_projection,
    w_out,
    forward_docs,
    backward_docs,
):
    length = embedded.shape[0]
    share = embedded.shape[1]
    section = lax.axis_index("pipe")
    sections = lax.axis_size("pipe")
    arrived = from_behind(sent_forward[0], "pipe", 1)
    incoming = jnp.where(section == 0, embedded, arrived)
    returned = from_behind(sent_backward[0], "pipe", -1)
    upstream = jnp.where(section == sections - 1, loss_grad, returned)
    x_full, stash_full, upstream_full = (
        lax.all_gather(incoming, "fsdp", axis=1, tiled=True),
        lax.all_gather(stashed[0], "fsdp", axis=1, tiled=True),
        lax.all_gather(upstream, "fsdp", axis=1, tiled=True),
    )
    gain = norm_gain[0]
    query_weight, key_weight, value_weight, out_weight = (
        w_query[0],
        w_key[0],
        value_projection[0],
        w_out[0],
    )
    h_forward, scale_forward = normalize(x_full, gain)
    h_backward, scale_backward = normalize(stash_full, gain)
    stacked = jnp.concatenate([h_forward, h_backward], 0)
    query_rows = jnp.dot(stacked, query_weight, preferred_element_type=jnp.float32).astype(
        jnp.bfloat16
    )
    key_rows = jnp.dot(stacked, key_weight, preferred_element_type=jnp.float32).astype(jnp.bfloat16)
    value_rows = jnp.dot(stacked, value_weight, preferred_element_type=jnp.float32).astype(
        jnp.bfloat16
    )
    key_cols = key_rows.shape[1]
    kv_heads = key_cols // HEAD_SIZE
    head_groups = QUERY_HEADS // KEY_VALUE_HEADS
    both = jnp.concatenate(
        [key_rows[:length], value_rows[:length], key_rows[length:], value_rows[length:]], 1
    )
    hops = min(WINDOW_TOKENS // length, lax.axis_size("seq") - 1)
    window_rows = near_rows(both, hops)
    span = (hops + 1) * length
    query_start = lax.axis_index("seq") * length
    q_pos = query_start + jnp.arange(length, dtype=jnp.int32)
    k_pos = query_start - hops * length + jnp.arange(span, dtype=jnp.int32)
    pad_ids = jnp.full((WINDOW_TOKENS,), -1, jnp.int32)
    docs_fwd = jnp.concatenate([pad_ids, forward_docs[0]])
    docs_bwd = jnp.concatenate([pad_ids, backward_docs[0]])
    k_start = query_start - hops * length + WINDOW_TOKENS
    q_fwd = query_rows[:length].reshape(length, kv_heads, head_groups, HEAD_SIZE)
    k_fwd = window_rows[:, :key_cols].reshape(span, kv_heads, HEAD_SIZE)
    v_fwd = window_rows[:, key_cols : 2 * key_cols].reshape(span, kv_heads, HEAD_SIZE)
    probs_fwd = block_probs(
        q_fwd,
        k_fwd,
        q_pos,
        k_pos,
        lax.dynamic_slice_in_dim(docs_fwd, query_start + WINDOW_TOKENS, length, 0),
        lax.dynamic_slice_in_dim(docs_fwd, k_start, span, 0),
    ).astype(jnp.bfloat16)
    attn_fwd = (
        jnp.einsum("hgqk,khd->qhgd", probs_fwd, v_fwd, preferred_element_type=jnp.float32)
        .reshape(length, -1)
        .astype(jnp.bfloat16)
    )
    partial_out = jnp.dot(attn_fwd, out_weight, preferred_element_type=jnp.float32)
    summed = lax.psum_scatter(
        partial_out.astype(jnp.bfloat16), "fsdp", scatter_dimension=1, tiled=True
    ).astype(jnp.float32)
    forward_out = (incoming.astype(jnp.float32) + summed).astype(jnp.bfloat16)
    q_bwd = query_rows[length:].reshape(length, kv_heads, head_groups, HEAD_SIZE)
    k_bwd = window_rows[:, 2 * key_cols : 3 * key_cols].reshape(span, kv_heads, HEAD_SIZE)
    v_bwd = window_rows[:, 3 * key_cols :].reshape(span, kv_heads, HEAD_SIZE)
    probs = block_probs(
        q_bwd,
        k_bwd,
        q_pos,
        k_pos,
        lax.dynamic_slice_in_dim(docs_bwd, query_start + WINDOW_TOKENS, length, 0),
        lax.dynamic_slice_in_dim(docs_bwd, k_start, span, 0),
    )
    probs_low = probs.astype(jnp.bfloat16)
    attention_gradient = (
        contract_last(upstream_full, out_weight)
        .astype(jnp.bfloat16)
        .reshape(length, kv_heads, head_groups, HEAD_SIZE)
    )
    dv_terms = jnp.einsum(
        "hgqk,qhgd->khd", probs_low, attention_gradient, preferred_element_type=jnp.float32
    )
    dp_block = jnp.einsum(
        "qhgd,khd->hgqk", attention_gradient, v_bwd, preferred_element_type=jnp.float32
    )
    delta = jnp.sum(probs * dp_block, axis=-1, keepdims=True)
    ds_block = (probs * (dp_block - delta)).astype(jnp.bfloat16)
    dq_local = (
        (
            jnp.einsum("hgqk,khd->qhgd", ds_block, k_bwd, preferred_element_type=jnp.float32)
            * HEAD_SIZE ** (-0.5)
        )
        .reshape(length, -1)
        .astype(jnp.bfloat16)
    )
    dk_terms = jnp.einsum(
        "hgqk,qhgd->khd", ds_block, q_bwd, preferred_element_type=jnp.float32
    ) * HEAD_SIZE ** (-0.5)
    kv_terms = jnp.concatenate(
        [dk_terms.reshape(span, key_cols), dv_terms.reshape(span, key_cols)], 1
    )
    owned = kv_terms[hops * length :] + return_terms(kv_terms, hops, length)
    dk_local = owned[:, :key_cols].astype(jnp.bfloat16)
    dv_local = owned[:, key_cols:].astype(jnp.bfloat16)
    d_norm = (
        contract_last(dq_local, query_weight)
        + contract_last(dk_local, key_weight)
        + contract_last(dv_local, value_weight)
    )
    feature_start = lax.axis_index("fsdp") * share
    d_whole = lax.psum(d_norm.astype(jnp.bfloat16), "fsdp").astype(jnp.float32)
    values_in = stash_full.astype(jnp.float32)
    row_mean = jnp.mean(values_in * gain * d_whole, axis=-1, keepdims=True)
    d_input = scale_backward * gain * d_whole - values_in * scale_backward**3 * row_mean
    d_input = lax.dynamic_slice_in_dim(d_input, feature_start, share, 1)
    input_grad = (upstream.astype(jnp.float32) + d_input).astype(jnp.bfloat16)
    return (forward_out[None], input_grad[None])


def solution(mesh):
    placed = (
        P("seq", "fsdp"),
        P("pipe", "seq", "fsdp"),
        P("pipe", "seq", "fsdp"),
        P("pipe", "seq", "fsdp"),
        P("seq", "fsdp"),
        P("pipe", None),
        P("pipe", None, "fsdp"),
        P("pipe", None, "fsdp"),
        P("pipe", None, "fsdp"),
        P("pipe", "fsdp", None),
        P("pipe", None),
        P("pipe", None),
    )
    return jax.shard_map(
        per_device,
        mesh=mesh,
        in_specs=placed,
        out_specs=(P("pipe", "seq", "fsdp"), P("pipe", "seq", "fsdp")),
        check_vma=False,
    )
```

profile of v0, /device:TPU:8, one launch (start us, length us, event | category | flops | bytes accessed | tf_op | source)
XLA Modules:
  0.0 252.7 jit_solution(18427499727909327280)
XLA Ops:
  7.2 5.2 %collective-permute-start = (bf16[128,672]{0,1:T(8,128)(2,1)}, bf16[128,672]{0,1:T(8,128)(2,1)}, u32[]{:S(2)}, u32[]{:S(2)}) collective-permute-start(bf16[128,672]{0,1:T(8,128)(2,1)} %bitcast.156), channel_id=1, source_target_pairs={{0,128},{128,256},{256,384},{384,512},{512,640},{1,129},{129,257},... | collective-permute-start | bytes 516104 | tf_op jit(solution)/shard_map/ppermute | solution.py:15
  12.5 1.3 collective-permute-start.5
  15.4 13.7 %all-gather = bf16[1,128,2688]{1,2,0:T(8,128)(2,1)S(1)} all-gather(bf16[1,128,672]{1,2,0:T(8,128)(2,1)} %param.14), channel_id=2, replica_groups=mesh['pipe'=6,'seq'=32,'fsdp'=4] {'fsdp'}, dimensions={2}, use_global_device_ids=true | all-gather | bytes 860160 | tf_op jit(solution)/shard_map/all_gather | solution.py:80
  32.2 13.6 %all_gather.9 = bf16[128,2688]{0,1:T(8,128)(2,1)S(1)} all-gather(bf16[128,672]{0,1:T(8,128)(2,1)S(1)} %broadcast_select_fusion.1), channel_id=1, replica_groups=mesh['pipe'=6,'seq'=32,'fsdp'=4] {'fsdp'}, dimensions={1}, use_global_device_ids=true | all-gather | bytes 860160 | tf_op jit(solution)/shard_map/all_gather | solution.py:79
  50.4 2.0 collective-permute-start.4
  52.4 14.8 %collective-permute-start.3 = (bf16[128,1024]{0,1:T(8,128)(2,1)}, bf16[128,1024]{0,1:T(8,128)(2,1)}, u32[]{:S(2)}, u32[]{:S(2)}) collective-permute-start(bf16[128,1024]{0,1:T(8,128)(2,1)} %pad_maximum_fusion.5), channel_id=1, source_target_pairs={{0,8},{4,12},{8,16},{12,20},{16,24},{20,28},{24,32},{28,36},{32,40... | collective-permute-start | bytes 786440 | tf_op jit(solution)/shard_map/ppermute | solution.py:15
  67.3 10.7 %collective-permute-start.2 = (bf16[128,1024]{0,1:T(8,128)(2,1)}, bf16[128,1024]{0,1:T(8,128)(2,1)}, u32[]{:S(2)}, u32[]{:S(2)}) collective-permute-start(bf16[128,1024]{0,1:T(8,128)(2,1)} %pad_maximum_fusion.5), channel_id=1, source_target_pairs={{0,12},{4,16},{8,20},{12,24},{16,28},{20,32},{24,36},{28,40},{32,4... | collective-permute-start | bytes 786440 | tf_op jit(solution)/shard_map/ppermute | solution.py:15
  78.0 3.5 %collective-permute-start.1 = (bf16[128,1024]{0,1:T(8,128)(2,1)}, bf16[128,1024]{0,1:T(8,128)(2,1)}, u32[]{:S(2)}, u32[]{:S(2)}) collective-permute-start(bf16[128,1024]{0,1:T(8,128)(2,1)} %pad_maximum_fusion.5), channel_id=1, source_target_pairs={{0,16},{4,20},{8,24},{12,28},{16,32},{20,36},{24,40},{28,44},{32,4... | collective-permute-start | bytes 786440 | tf_op jit(solution)/shard_map/ppermute | solution.py:15
  84.1 13.4 %all_gather.11 = bf16[128,2688]{0,1:T(8,128)(2,1)S(1)} all-gather(bf16[128,672]{0,1:T(8,128)(2,1)S(1)} %broadcast_select_fusion), channel_id=1, replica_groups=mesh['pipe'=6,'seq'=32,'fsdp'=4] {'fsdp'}, dimensions={1}, use_global_device_ids=true | all-gather | bytes 860160 | tf_op jit(solution)/shard_map/all_gather | solution.py:81
  97.5 1.7 fusion.39
  99.9 1.7 copy.49
  101.6 1.6 reshape.80
  103.2 1.7 copy.50
  110.2 2.7 %fusion.87 = (f32[2,2,128]{2,1,0:T(2,128)S(1)}, f32[2,2,128,640]{2,3,1,0:T(8,128)}) fusion(bf16[640,2,128,1]{0,2,3,1:T(8,128)(2,1)} %bitcast.138, bf16[128,2,2,128]{0,3,2,1:T(8,128)(2,1)} %bitcast.142, pred[128,640]{0,1:T(8,128)(4,1)} %get-tuple-element.18), kind=kOutput, calls=%fused_computation.114 | convolution fusion | flops 85197440 | bytes 1853440 | tf_op jit(solution)/shard_map/sub | solution.py:31
  112.9 2.9 %fusion.42 = f32[2,128,640,1]{2,1,3,0:T(8,128)} fusion(bf16[128,2,2,128]{0,3,2,1:T(8,128)(2,1)} %bitcast.150, f32[2,2,128]{2,1,0:T(2,128)S(1)} %get-tuple-element.22, bf16[640,2,128,1]{0,2,3,1:T(8,128)(2,1)} %bitcast.139, bf16[128,2,2,128]{0,3,2,1:T(8,128)(2,1)} %bitcast.143, pred[128,640]{0,1:T(8,128)(4,1)} %get-tuple-element.18), kind=kOutput, calls=%fused_computation.56 | convolution fusion | flops 169411712 | bytes 1329152 | tf_op jit(solution)/shard_map/hgqk,qhgd->khd/dot_general | solution.py:154
  115.8 2.0 multiply_reduce_fusion.2
  120.1 2.9 %collective-permute-start.6 = (bf16[128,512]{0,1:T(8,128)(2,1)S(1)}, bf16[128,512]{0,1:T(8,128)(2,1)S(1)}, u32[]{:S(2)}, u32[]{:S(2)}) collective-permute-start(bf16[128,512]{0,1:T(8,128)(2,1)S(1)} %get-tuple-element.6), channel_id=1, source_target_pairs={{4,0},{8,4},{12,8},{16,12},{20,16},{24,20},{28,24},{32,28},{36,32}... | collective-permute-start | bytes 393224 | tf_op jit(solution)/shard_map/ppermute | solution.py:15
  123.0 1.9 collective-permute-start.9
  124.9 1.9 collective-permute-start.8
  126.8 1.9 collective-permute-start.7
  130.8 6.9 %collective-permute-done.8 = bf16[128,512]{0,1:T(8,128)(2,1)S(1)} collective-permute-done((bf16[128,512]{0,1:T(8,128)(2,1)S(1)}, bf16[128,512]{0,1:T(8,128)(2,1)S(1)}, u32[]{:S(2)}, u32[]{:S(2)}) %collective-permute-start.8) | collective-permute-done | bytes 131104 | tf_op jit(solution)/shard_map/ppermute | solution.py:15
  137.8 8.1 %collective-permute-done.7 = bf16[128,512]{0,1:T(8,128)(2,1)S(1)} collective-permute-done((bf16[128,512]{0,1:T(8,128)(2,1)S(1)}, bf16[128,512]{0,1:T(8,128)(2,1)S(1)}, u32[]{:S(2)}, u32[]{:S(2)}) %collective-permute-start.7) | collective-permute-done | bytes 131104 | tf_op jit(solution)/shard_map/ppermute | solution.py:15
  147.4 1.4 fusion.2
  149.0 1.7 fusion.84
  150.7 2.7 %convolution_convert_fusion.1 = bf16[2,128,2,128]{3,1,2,0:T(8,128)(2,1)} fusion(bf16[640,2,128,1]{0,2,3,1:T(8,128)(2,1)} %bitcast.147, f32[2,2,128]{2,1,0:T(2,128)S(1)} %fusion.84, bf16[640,2,128,1]{0,2,3,1:T(8,128)(2,1)} %bitcast.146, pred[128,640]{0,1:T(8,128)(4,1)} %get-tuple-element.19, bf16[128,2,2,128]{3,2,1,0:T(2,128)(2,1)} %reshape.80), kind=kOutput, calls=%fused_computation.52 | convolution fusion | flops 169477248 | bytes 1001472 | tf_op jit(solution)/shard_map/hgqk,khd->qhgd/dot_general | solution.py:128
  153.3 3.9 %convolution_convert_fusion = bf16[128,2688]{0,1:T(8,128)(2,1)} fusion(bf16[128,512]{0,1:T(8,128)(2,1)} %bitcast.149, bf16[1,512,2688]{2,1,0:T(8,128)(2,1)} %param.21), kind=kOutput, calls=%fused_computation.5 | convolution fusion | flops 352665600 | bytes 3571712 | tf_op jit(solution)/shard_map/dot_general | solution.py:132
  157.3 1.2 bitcast_convert_fusion
  158.5 51.8 %all-reduce.4.cloned.1.call-done = bf16[128,2688]{0,1:T(8,128)(2,1)} async-done(((bf16[128,2688]{0,1:T(8,128)(2,1)}), bf16[128,2688]{0,1:T(8,128)(2,1)}) %all-reduce.4.cloned.1.call-update) | async-done | bytes 688144 | tf_op jit(solution)/shard_map/psum | solution.py:185
  210.3 1.3 convert_element_type.121
  212.0 1.8 fusion.53
  213.8 30.3 %reduce-scatter.2.cloned.1.call-done = bf16[128,672]{0,1:T(8,128)(2,1)} async-done(((bf16[128,2688]{0,1:T(8,128)(2,1)}), bf16[128,672]{0,1:T(8,128)(2,1)}) %reduce-scatter.2.cloned.1.call-update) | async-done | bytes 172048 | tf_op jit(solution)/shard_map/reduce_scatter | solution.py:133
  244.1 1.7 fusion.52
  (92 shorter events, 24.2 us)
Async XLA Ops:
  7.2 74.3 %copy-start = (bf16[1,2688,512]{2,1,0:T(8,128)(2,1)S(1)}, bf16[1,2688,512]{2,1,0:T(8,128)(2,1)}, u32[]{:S(2)}) copy-start(bf16[1,2688,512]{2,1,0:T(8,128)(2,1)} %param.18) | copy-start | bytes 8257540
  7.2 22.2 %copy-start.21 = (f32[1,2688]{1,0:T(1,128)S(1)}, f32[1,2688]{1,0:T(1,128)}, u32[]{:S(2)}) copy-start(f32[1,2688]{1,0:T(1,128)} %param.17) | copy-start | bytes 32260
  7.2 203.1 %all-reduce.4.cloned.1.call-start = ((), (), s32[]{:S(2)}) async-start(), calls=%async_computation.2 | async-start | bytes 1376256 | tf_op jit(solution)/shard_map/psum | solution.py:185
  7.2 23.3 %collective-permute-start = (bf16[128,672]{0,1:T(8,128)(2,1)}, bf16[128,672]{0,1:T(8,128)(2,1)}, u32[]{:S(2)}, u32[]{:S(2)}) collective-permute-start(bf16[128,672]{0,1:T(8,128)(2,1)} %bitcast.156), channel_id=1, source_target_pairs={{0,128},{128,256},{256,384},{384,512},{512,640},{1,129},{129,257},... | collective-permute-start | bytes 516104 | tf_op jit(solution)/shard_map/ppermute | solution.py:15
  12.5 70.0 %collective-permute-start.5 = (bf16[128,672]{0,1:T(8,128)(2,1)}, bf16[128,672]{0,1:T(8,128)(2,1)}, u32[]{:S(2)}, u32[]{:S(2)}) collective-permute-start(bf16[128,672]{0,1:T(8,128)(2,1)} %bitcast.157), channel_id=1, source_target_pairs={{128,0},{256,128},{384,256},{512,384},{640,512},{129,1},{257,129},... | collective-permute-start | bytes 516104 | tf_op jit(solution)/shard_map/ppermute | solution.py:15
  46.2 1.3 copy-start.9
  47.5 1.3 copy-start.7
  49.6 28.4 %copy-start.13 = (bf16[128,256]{0,1:T(8,128)(2,1)}, bf16[128,256]{0,1:T(8,128)(2,1)S(1)}, u32[]{:S(2)}) copy-start(bf16[128,256]{0,1:T(8,128)(2,1)S(1)} %get-tuple-element.13) | copy-start | bytes 196612
  49.6 28.4 %copy-start.15 = (bf16[128,256]{0,1:T(8,128)(2,1)}, bf16[128,256]{0,1:T(8,128)(2,1)S(1)}, u32[]{:S(2)}) copy-start(bf16[128,256]{0,1:T(8,128)(2,1)S(1)} %get-tuple-element.26) | copy-start | bytes 196612
  49.6 28.4 %copy-start.17 = (bf16[128,256]{0,1:T(8,128)(2,1)}, bf16[128,256]{0,1:T(8,128)(2,1)S(1)}, u32[]{:S(2)}) copy-start(bf16[128,256]{0,1:T(8,128)(2,1)S(1)} %get-tuple-element.27) | copy-start | bytes 196612
  50.4 32.1 %copy-start.20 = (bf16[128,672]{0,1:T(8,128)(2,1)S(1)}, bf16[128,672]{0,1:T(8,128)(2,1)}, u32[]{:S(2)}) copy-start(bf16[128,672]{0,1:T(8,128)(2,1)} %param.16) | copy-start | bytes 516100
  50.4 57.6 %collective-permute-start.4 = (bf16[128,1024]{0,1:T(8,128)(2,1)}, bf16[128,1024]{0,1:T(8,128)(2,1)}, u32[]{:S(2)}, u32[]{:S(2)}) collective-permute-start(bf16[128,1024]{0,1:T(8,128)(2,1)} %pad_maximum_fusion.5), channel_id=1, source_target_pairs={{0,4},{4,8},{8,12},{12,16},{16,20},{20,24},{24,28},{28,32},{32,36}... | collective-permute-start | bytes 786440 | tf_op jit(solution)/shard_map/ppermute | solution.py:15
  52.4 54.5 %collective-permute-start.3 = (bf16[128,1024]{0,1:T(8,128)(2,1)}, bf16[128,1024]{0,1:T(8,128)(2,1)}, u32[]{:S(2)}, u32[]{:S(2)}) collective-permute-start(bf16[128,1024]{0,1:T(8,128)(2,1)} %pad_maximum_fusion.5), channel_id=1, source_target_pairs={{0,8},{4,12},{8,16},{12,20},{16,24},{20,28},{24,32},{28,36},{32,40... | collective-permute-start | bytes 786440 | tf_op jit(solution)/shard_map/ppermute | solution.py:15
  67.3 38.6 %collective-permute-start.2 = (bf16[128,1024]{0,1:T(8,128)(2,1)}, bf16[128,1024]{0,1:T(8,128)(2,1)}, u32[]{:S(2)}, u32[]{:S(2)}) collective-permute-start(bf16[128,1024]{0,1:T(8,128)(2,1)} %pad_maximum_fusion.5), channel_id=1, source_target_pairs={{0,12},{4,16},{8,20},{12,24},{16,28},{20,32},{24,36},{28,40},{32,4... | collective-permute-start | bytes 786440 | tf_op jit(solution)/shard_map/ppermute | solution.py:15
  78.0 26.9 %collective-permute-start.1 = (bf16[128,1024]{0,1:T(8,128)(2,1)}, bf16[128,1024]{0,1:T(8,128)(2,1)}, u32[]{:S(2)}, u32[]{:S(2)}) collective-permute-start(bf16[128,1024]{0,1:T(8,128)(2,1)} %pad_maximum_fusion.5), channel_id=1, source_target_pairs={{0,16},{4,20},{8,24},{12,28},{16,32},{20,36},{24,40},{28,44},{32,4... | collective-permute-start | bytes 786440 | tf_op jit(solution)/shard_map/ppermute | solution.py:15
  81.5 16.0 %copy-start.1 = (bf16[1,512,2688]{2,1,0:T(8,128)(2,1)S(1)}, bf16[1,512,2688]{2,1,0:T(8,128)(2,1)}, u32[]{:S(2)}) copy-start(bf16[1,512,2688]{2,1,0:T(8,128)(2,1)} %param.21) | copy-start | bytes 8257540
  104.9 4.1 %copy-start.14 = (bf16[128,256]{0,1:T(8,128)(2,1)S(1)}, bf16[128,256]{0,1:T(8,128)(2,1)}, u32[]{:S(2)}) copy-start(bf16[128,256]{0,1:T(8,128)(2,1)} %copy-done.13) | copy-start | bytes 196612
  104.9 4.1 %copy-start.16 = (bf16[128,256]{0,1:T(8,128)(2,1)S(1)}, bf16[128,256]{0,1:T(8,128)(2,1)}, u32[]{:S(2)}) copy-start(bf16[128,256]{0,1:T(8,128)(2,1)} %copy-done.15) | copy-start | bytes 196612
  104.9 4.2 %copy-start.18 = (bf16[128,256]{0,1:T(8,128)(2,1)S(1)}, bf16[128,256]{0,1:T(8,128)(2,1)}, u32[]{:S(2)}) copy-start(bf16[128,256]{0,1:T(8,128)(2,1)} %copy-done.17) | copy-start | bytes 196612
  115.8 2.0 copy-start.11
  117.8 1.0 copy-start.12
  117.8 1.2 copy-start.19
  118.8 1.1 copy-start.3
  120.1 9.6 %collective-permute-start.6 = (bf16[128,512]{0,1:T(8,128)(2,1)S(1)}, bf16[128,512]{0,1:T(8,128)(2,1)S(1)}, u32[]{:S(2)}, u32[]{:S(2)}) collective-permute-start(bf16[128,512]{0,1:T(8,128)(2,1)S(1)} %get-tuple-element.6), channel_id=1, source_target_pairs={{4,0},{8,4},{12,8},{16,12},{20,16},{24,20},{28,24},{32,28},{36,32}... | collective-permute-start | bytes 393224 | tf_op jit(solution)/shard_map/ppermute | solution.py:15
  123.0 7.9 %collective-permute-start.9 = (bf16[128,512]{0,1:T(8,128)(2,1)S(1)}, bf16[128,512]{0,1:T(8,128)(2,1)S(1)}, u32[]{:S(2)}, u32[]{:S(2)}) collective-permute-start(bf16[128,512]{0,1:T(8,128)(2,1)S(1)} %get-tuple-element.7), channel_id=1, source_target_pairs={{16,0},{20,4},{24,8},{28,12},{32,16},{36,20},{40,24},{44,28},{48,3... | collective-permute-start | bytes 393224 | tf_op jit(solution)/shard_map/ppermute | solution.py:15
  124.9 12.9 %collective-permute-start.8 = (bf16[128,512]{0,1:T(8,128)(2,1)S(1)}, bf16[128,512]{0,1:T(8,128)(2,1)S(1)}, u32[]{:S(2)}, u32[]{:S(2)}) collective-permute-start(bf16[128,512]{0,1:T(8,128)(2,1)S(1)} %get-tuple-element.8), channel_id=1, source_target_pairs={{12,0},{16,4},{20,8},{24,12},{28,16},{32,20},{36,24},{40,28},{44,3... | collective-permute-start | bytes 393224 | tf_op jit(solution)/shard_map/ppermute | solution.py:15
  126.8 19.1 %collective-permute-start.7 = (bf16[128,512]{0,1:T(8,128)(2,1)S(1)}, bf16[128,512]{0,1:T(8,128)(2,1)S(1)}, u32[]{:S(2)}, u32[]{:S(2)}) collective-permute-start(bf16[128,512]{0,1:T(8,128)(2,1)S(1)} %get-tuple-element.9), channel_id=1, source_target_pairs={{8,0},{12,4},{16,8},{20,12},{24,16},{28,20},{32,24},{36,28},{40,32... | collective-permute-start | bytes 393224 | tf_op jit(solution)/shard_map/ppermute | solution.py:15
  129.6 16.4 %copy-start.8 = (bf16[1,2688,256]{2,1,0:T(8,128)(2,1)S(1)}, bf16[1,2688,256]{2,1,0:T(8,128)(2,1)}, u32[]{:S(2)}) copy-start(bf16[1,2688,256]{2,1,0:T(8,128)(2,1)} %param.19) | copy-start | bytes 4128772
  146.0 1.3 copy-start.10
  148.8 95.4 %reduce-scatter.2.cloned.1.call-start = ((), (), s32[]{:S(2)}) async-start(), calls=%async_computation.1 | async-start | bytes 860160 | tf_op jit(solution)/shard_map/reduce_scatter | solution.py:133
  210.3 1.3 copy-start.2
  210.3 1.8 copy-start.6
  (2 other events, 1.3 us)
Sparse Core Ops, SparseCore 0:
  148.9 61.3 all-reduce.3
  213.4 30.6 reduce-scatter.1
where the time goes:
time: 254 us; the launch traced here: 253 us
  waiting for transfers between devices  98.4 us (39%)
  starting transfers between devices  46.5 us (18%)
  blocking collectives  40.7 us (16%)
  matrix products  23.2 us (9%)
  local copies, waits for them, and re-layouts  17.7 us (7%)
  between operations  14.5 us (6%)
  other arithmetic  11.7 us (5%)
    psum x1, waiting for transfers between devices, per_device(): d_whole = lax.psum(d_norm.astype(jnp.bfloat16), 'fsdp').astype(jnp.float32)  51.8 us
    ppermute x10, starting transfers between devices, from_behind(): lax.ppermute(value, axis, [(source, source + steps) for source in range(i...  46.2 us
    reduce_scatter x1, waiting for transfers between devices, per_device(): lax.psum_scatter(partial_out.astype(jnp.bfloat16), 'fsdp', scatter_dimens...  30.3 us
    ppermute x10, waiting for transfers between devices, from_behind(): lax.ppermute(value, axis, [(source, source + steps) for source in range(i...  16.3 us
    all_gather x1, blocking collectives, per_device(): lax.all_gather(stashed[0], 'fsdp', axis=1, tiled=True)  13.7 us
    all_gather x1, blocking collectives, per_device(): lax.all_gather(incoming, 'fsdp', axis=1, tiled=True)  13.6 us
    all_gather x1, blocking collectives, per_device(): lax.all_gather(upstream, 'fsdp', axis=1, tiled=True)  13.4 us
    unnamed x48, local copies, waits for them, and re-layouts  9.12 us
  transfers between devices with their start and end apart: 12, of which 5 were waited for; matrix products, arithmetic and copies ran while one was open for 13% of the time, Pallas kernels for 0%

commit v1 on v0

v1 whole, which is shorter than its diff:
```python
import jax
import jax.numpy as jnp
from jax import lax
from jax.experimental import pallas as pl
from jax.experimental.pallas import tpu as pltpu
from jax.sharding import PartitionSpec as P

HEAD = 128
WINDOW = 512
SCALE = HEAD ** (-0.5)
BF = jnp.bfloat16
F32 = jnp.float32


def dot_nn(left, right):
    return lax.dot_general(left, right, (((1,), (0,)), ((), ())), preferred_element_type=F32)


def dot_nt(left, right):
    return lax.dot_general(left, right, (((1,), (1,)), ((), ())), preferred_element_type=F32)


def dot_tn(left, right):
    return lax.dot_general(left, right, (((0,), (0,)), ((), ())), preferred_element_type=F32)


def vmem(count):
    return [pl.BlockSpec(memory_space=pltpu.VMEM) for _ in range(count)]


def smem():
    return pl.BlockSpec(memory_space=pltpu.SMEM)


def project_rows(rows, gain_ref, wq_ref, wk_ref, wv_ref, q_ref, kv_ref):
    parts = len(rows)
    width = parts * rows[0].shape[1]
    total = sum(jnp.sum(row * row, axis=1, keepdims=True) for row in rows)
    factor = lax.rsqrt(total / width + 1e-06)
    query = key = value = 0.0
    for part in range(parts):
        h = (rows[part] * factor * gain_ref[part]).astype(BF)
        query = query + dot_nn(h, wq_ref[part])
        key = key + dot_nn(h, wk_ref[part])
        value = value + dot_nn(h, wv_ref[part])
    q_ref[...] = query.astype(BF)
    half = kv_ref.shape[1] // 2
    kv_ref[:, :half] = key.astype(BF)
    kv_ref[:, half:] = value.astype(BF)
    return factor


def project_back_body(x_ref, gain_ref, wq_ref, wk_ref, wv_ref, q_ref, kv_ref, r_ref):
    rows = [x_ref[part].astype(F32) for part in range(x_ref.shape[0])]
    factor = project_rows(rows, gain_ref, wq_ref, wk_ref, wv_ref, q_ref, kv_ref)
    r_ref[...] = jnp.broadcast_to(factor, r_ref.shape)


def project_front_body(x_ref, gain_ref, wq_ref, wk_ref, wv_ref, wo_ref, q_ref, kv_ref, da_ref):
    length = q_ref.shape[0]
    parts, _, share = x_ref.shape
    rows = [x_ref[part, :length, :].astype(F32) for part in range(parts)]
    project_rows(rows, gain_ref, wq_ref, wk_ref, wv_ref, q_ref, kv_ref)
    grad = 0.0
    for part in range(parts):
        weight = wo_ref[:, part * share : (part + 1) * share]
        grad = grad + dot_nt(x_ref[part, length:, :], weight)
    da_ref[...] = grad.astype(BF)


def window_mask(info_ref, docs_ref, length):
    core = info_ref[0]
    index = info_ref[1]
    offsets = (0, 2, 4, 3 - 2 * core, 1 + 2 * core)
    q_row = jnp.broadcast_to(docs_ref[pl.ds(index, 1), :], (length, length))
    q_doc = jnp.transpose(q_row)
    across = lax.broadcasted_iota(jnp.int32, (length, length), 1)
    down = lax.broadcasted_iota(jnp.int32, (length, length), 0)
    masks = []
    for offset in offsets:
        block = index - offset
        k_doc = docs_ref[pl.ds(jnp.maximum(block, 0), 1), :]
        ahead = down - across + offset * length
        keep = (ahead >= 0) & (ahead < WINDOW) & (block >= 0)
        masks.append(keep & (jnp.broadcast_to(k_doc, (length, length)) == q_doc))
    return jnp.concatenate([jnp.where(m, 0.0, -1e30) for m in masks], axis=1)


def softmax_rows(q_rows, keys, bias):
    scores = dot_nt(q_rows, keys) * SCALE + bias
    top = jnp.max(scores, axis=1, keepdims=True)
    expo = jnp.exp(scores - top)
    return expo / jnp.sum(expo, axis=1, keepdims=True)


def attend_body(info_ref, docs_ref, q_ref, own, two, four, late, mid, wo_ref, out_ref):
    length = q_ref.shape[0]
    parts, _, share = out_ref.shape
    kv_heads = own.shape[1] // (2 * HEAD)
    groups = q_ref.shape[1] // HEAD // kv_heads
    bias = window_mask(info_ref, docs_ref, length)
    blocks = (own, two, four, mid, late)
    heads = []
    for kv in range(kv_heads):
        keys = jnp.concatenate([b[:, kv * HEAD : (kv + 1) * HEAD] for b in blocks], axis=0)
        at = (kv_heads + kv) * HEAD
        values = jnp.concatenate([b[:, at : at + HEAD] for b in blocks], axis=0)
        for group in range(groups):
            head = kv * groups + group
            rows = q_ref[:, head * HEAD : (head + 1) * HEAD]
            probs = softmax_rows(rows, keys, bias).astype(BF)
            heads.append(dot_nn(probs, values).astype(BF))
    mixed = jnp.concatenate(heads, axis=1)
    for part in range(parts):
        weight = wo_ref[:, part * share : (part + 1) * share]
        out_ref[part] = dot_nn(mixed, weight).astype(BF)


def attend_back_body(
    info_ref, docs_ref, q_ref, da_ref, own, two, four, late, mid,
    dq_ref, town_ref, ttwo_ref, tfour_ref, tswap_ref,
):
    length = q_ref.shape[0]
    kv_heads = own.shape[1] // (2 * HEAD)
    groups = q_ref.shape[1] // HEAD // kv_heads
    bias = window_mask(info_ref, docs_ref, length)
    blocks = (own, two, four, mid, late)
    for kv in range(kv_heads):
        keys = jnp.concatenate([b[:, kv * HEAD : (kv + 1) * HEAD] for b in blocks], axis=0)
        at = (kv_heads + kv) * HEAD
        values = jnp.concatenate([b[:, at : at + HEAD] for b in blocks], axis=0)
        d_key = d_value = 0.0
        for group in range(groups):
            head = kv * groups + group
            span = slice(head * HEAD, (head + 1) * HEAD)
            rows = q_ref[:, span]
            grad = da_ref[:, span]
            probs = softmax_rows(rows, keys, bias)
            d_value = d_value + dot_tn(probs.astype(BF), grad)
            d_probs = dot_nt(grad, values)
            delta = jnp.sum(probs * d_probs, axis=1, keepdims=True)
            d_scores = (probs * (d_probs - delta)).astype(BF)
            dq_ref[:, span] = (dot_nn(d_scores, keys) * SCALE).astype(BF)
            d_key = d_key + dot_tn(d_scores, rows)
        for terms, start in ((d_key, kv * HEAD), (d_value, at)):
            cols = slice(start, start + HEAD)
            town_ref[:, cols] = terms[:length]
            ttwo_ref[:, cols] = terms[length : 2 * length]
            tfour_ref[:, cols] = terms[2 * length : 3 * length]
            tswap_ref[:length, cols] = terms[4 * length :].astype(BF)
            tswap_ref[length:, cols] = terms[3 * length : 4 * length].astype(BF)


def input_terms_body(
    dq_ref, own_ref, two_ref, four_ref, x_ref, gain_ref, wq_ref, wk_ref, wv_ref, out_ref
):
    parts, _, share = x_ref.shape
    half = own_ref.shape[1] // 2
    total = own_ref[...] + two_ref[...].astype(F32) + four_ref[...].astype(F32)
    d_key = (total[:, :half] * SCALE).astype(BF)
    d_value = total[:, half:].astype(BF)
    row = 0.0
    for part in range(parts):
        d_norm = dot_nt(dq_ref[...], wq_ref[part])
        d_norm = d_norm + dot_nt(d_key, wk_ref[part])
        d_norm = d_norm + dot_nt(d_value, wv_ref[part])
        out_ref[part, :, :share] = d_norm.astype(BF)
        product = x_ref[part].astype(F32) * gain_ref[part] * d_norm
        row = row + jnp.sum(product, axis=1, keepdims=True)
    high = row.astype(BF)
    low = (row - high.astype(F32)).astype(BF)
    for part in range(parts):
        out_ref[part, :, share : share + 1] = high
        out_ref[part, :, share + 1 : share + 2] = low


def finish_body(info_ref, sums_ref, x_ref, up_ref, gain_ref, r_ref, out_ref):
    parts = sums_ref.shape[0]
    share = x_ref.shape[1]
    total = sum(sums_ref[part].astype(F32) for part in range(parts))
    row = total[:, share : share + 1] + total[:, share + 1 : share + 2]
    row = row / (parts * share)
    factor = r_ref[:, :1]
    gain = gain_ref[info_ref[2]]
    values = x_ref[...].astype(F32)
    d_input = factor * gain * total[:, :share] - values * (factor * factor * factor * row)
    out_ref[...] = (up_ref[...].astype(F32) + d_input).astype(BF)


def shifted(value, steps):
    count = lax.axis_size("seq")
    pairs = [(s, s + steps) for s in range(count) if 0 <= s + steps < count]
    return lax.ppermute(value, "seq", pairs)


def swapped(value):
    count = lax.axis_size("seq")
    return lax.ppermute(value, "seq", [(s, s ^ 1) for s in range(count)])


def next_section(value, steps):
    count = lax.axis_size("pipe")
    pairs = [(s, s + steps) for s in range(count) if 0 <= s + steps < count]
    return lax.ppermute(value, "pipe", pairs)


def gather_parts(value):
    parts = lax.axis_size("fsdp")
    spread = jnp.broadcast_to(value[None], (parts,) + value.shape)
    return lax.all_to_all(spread, "fsdp", 0, 0)


def window_blocks(kv, core):
    two = shifted(kv, 2)
    four = shifted(kv, 4)
    mid = swapped(jnp.where(core == 0, kv, four))
    late = swapped(two)
    return (kv, two, four, late, mid)


def per_device(
    embedded, sent_forward, stashed, sent_backward, loss_grad, norm_gain,
    w_query, w_key, value_projection, w_out, forward_docs, backward_docs,
):
    length, share = embedded.shape
    parts = lax.axis_size("fsdp")
    section = lax.axis_index("pipe")
    sections = lax.axis_size("pipe")
    index = lax.axis_index("seq")
    core = index % 2
    info = jnp.stack([core, index, lax.axis_index("fsdp")]).astype(jnp.int32)
    gain = norm_gain[0].reshape(parts, 1, share)
    wq = w_query[0].reshape(parts, share, -1)
    wk = w_key[0].reshape(parts, share, -1)
    wv = value_projection[0].reshape(parts, share, -1)
    wo = w_out[0]
    docs_front = forward_docs[0].reshape(-1, length)
    docs_back = backward_docs[0].reshape(-1, length)
    q_cols = wq.shape[2]
    kv_cols = 2 * wk.shape[2]
    rows_q = jax.ShapeDtypeStruct((length, q_cols), BF)
    rows_kv = jax.ShapeDtypeStruct((length, kv_cols), BF)
    terms = jax.ShapeDtypeStruct((length, kv_cols), F32)

    arrived = next_section(sent_forward[0], 1)
    returned = next_section(sent_backward[0], -1)
    stash = gather_parts(stashed[0])
    incoming = jnp.where(section == 0, embedded, arrived)
    upstream = jnp.where(section == sections - 1, loss_grad, returned)
    both = gather_parts(jnp.concatenate([incoming, upstream], 0))

    q_back, kv_back, factor = pl.pallas_call(
        project_back_body,
        out_shape=(rows_q, rows_kv, jax.ShapeDtypeStruct((length, HEAD), F32)),
        in_specs=vmem(5), out_specs=tuple(vmem(3)), name="project_back",
    )(stash, gain, wq, wk, wv)
    blocks_back = window_blocks(kv_back, core)

    q_front, kv_front, d_attn = pl.pallas_call(
        project_front_body,
        out_shape=(rows_q, rows_kv, rows_q),
        in_specs=vmem(6), out_specs=tuple(vmem(3)), name="project_front",
    )(both, gain, wq, wk, wv, wo)
    blocks_front = window_blocks(kv_front, core)

    d_query, t_own, t_two, t_four, t_swap = pl.pallas_call(
        attend_back_body,
        out_shape=(rows_q, terms, terms, terms, jax.ShapeDtypeStruct((2 * length, kv_cols), BF)),
        in_specs=[smem()] + vmem(8), out_specs=tuple(vmem(5)), name="attend_back",
    )(info, docs_back, q_back, d_attn, *blocks_back)
    t_swap = swapped(t_swap)
    t_late = t_swap[:length].astype(F32)
    t_mid = t_swap[length:].astype(F32)
    back_two = shifted((t_two + t_late).astype(BF), -2)
    back_four = shifted(jnp.where(core == 0, t_four, t_four + t_mid).astype(BF), -4)
    t_own = jnp.where(core == 0, t_own + t_mid, t_own)

    partial_out = pl.pallas_call(
        attend_body,
        out_shape=jax.ShapeDtypeStruct((parts, length, share), BF),
        in_specs=[smem()] + vmem(8), out_specs=vmem(1)[0], name="attend",
    )(info, docs_front, q_front, *blocks_front, wo)
    summed = jnp.sum(lax.all_to_all(partial_out, "fsdp", 0, 0).astype(F32), 0)
    forward_out = (incoming.astype(F32) + summed).astype(BF)

    padded = -(-(share + 2) // 128) * 128
    d_parts = pl.pallas_call(
        input_terms_body,
        out_shape=jax.ShapeDtypeStruct((parts, length, padded), BF),
        in_specs=vmem(9), out_specs=vmem(1)[0], name="input_terms",
    )(d_query, t_own, back_two, back_four, stash, gain, wq, wk, wv)
    d_parts = lax.all_to_all(d_parts, "fsdp", 0, 0)
    input_grad = pl.pallas_call(
        finish_body,
        out_shape=jax.ShapeDtypeStruct((length, share), BF),
        in_specs=[smem()] + vmem(5), out_specs=vmem(1)[0], name="finish",
    )(info, d_parts, stashed[0], upstream, gain, factor)
    return (forward_out[None], input_grad[None])


def solution(mesh):
    placed = (
        P("seq", "fsdp"),
        P("pipe", "seq", "fsdp"),
        P("pipe", "seq", "fsdp"),
        P("pipe", "seq", "fsdp"),
        P("seq", "fsdp"),
        P("pipe", None),
        P("pipe", None, "fsdp"),
        P("pipe", None, "fsdp"),
        P("pipe", None, "fsdp"),
        P("pipe", "fsdp", None),
        P("pipe", None),
        P("pipe", None),
    )
    return jax.shard_map(
        per_device,
        mesh=mesh,
        in_specs=placed,
        out_specs=(P("pipe", "seq", "fsdp"), P("pipe", "seq", "fsdp")),
        check_vma=False,
    )
```

time: 254 us -> 164 us (0.65)
  the two profiles are of different devices: /device:TPU:8 before, /device:TPU:88 now
where the time goes in v1:
time: 164 us; the launch traced here: 163 us
  starting transfers between devices  74.3 us (45%)
  waiting for transfers between devices  36.3 us (22%)
  Pallas kernels  29.7 us (18%)
  local copies, waits for them, and re-layouts  17.9 us (11%)
  other arithmetic  3.65 us (2%)
    ppermute x6, starting transfers between devices, shifted(): return lax.ppermute(value, 'seq', pairs)  40.7 us
    ppermute x6, waiting for transfers between devices, shifted(): return lax.ppermute(value, 'seq', pairs)  14.8 us
    all_to_all x2, waiting for transfers between devices, gather_parts(): return lax.all_to_all(spread, 'fsdp', 0, 0)  10.3 us
    ppermute x5, starting transfers between devices, swapped(): return lax.ppermute(value, 'seq', [(s, s ^ 1) for s in range(count)])  10.1 us
    all_to_all x1, waiting for transfers between devices, per_device(): d_parts = lax.all_to_all(d_parts, 'fsdp', 0, 0)  9.87 us
    unnamed x45, local copies, waits for them, and re-layouts  8.72 us
    all_to_all x2, starting transfers between devices, gather_parts(): return lax.all_to_all(spread, 'fsdp', 0, 0)  7.97 us
    pallas_call x1, Pallas kernels, per_device(): pl.pallas_call(project_front_body, out_shape=(rows_q, rows_kv, rows_q), i...  6.73 us
  transfers between devices with their start and end apart: 17, of which 5 were waited for; matrix products, arithmetic and copies ran while one was open for 9% of the time, Pallas kernels for 17%

profile of v1, /device:TPU:88, one launch (start us, length us, event | category | flops | bytes accessed | tf_op | source)
XLA Modules:
  0.0 162.9 jit_solution(17765270808517486577)
XLA Ops:
  1.7 2.1 %collective-permute-start.1 = (bf16[128,672]{1,0:T(8,128)(2,1)S(1)}, bf16[128,672]{1,0:T(8,128)(2,1)S(1)}, u32[]{:S(2)}, u32[]{:S(2)}) collective-permute-start(bf16[128,672]{1,0:T(8,128)(2,1)S(1)} %bitcast.31), channel_id=1, source_target_pairs={{128,0},{256,128},{384,256},{512,384},{640,512},{129,1},{257,129},... | collective-permute-start | bytes 516104 | tf_op jit(solution)/shard_map/ppermute | solution.py:204
  4.8 4.4 %collective-permute-start = (bf16[128,672]{1,0:T(8,128)(2,1)S(1)}, bf16[128,672]{1,0:T(8,128)(2,1)S(1)}, u32[]{:S(2)}, u32[]{:S(2)}) collective-permute-start(bf16[128,672]{1,0:T(8,128)(2,1)S(1)} %bitcast.30), channel_id=1, source_target_pairs={{0,128},{128,256},{256,384},{384,512},{512,640},{1,129},{129,257},... | collective-permute-start | bytes 516104 | tf_op jit(solution)/shard_map/ppermute | solution.py:204
  9.2 1.9 %broadcast_in_dim.22 = bf16[4,128,672]{1,2,0:T(8,128)(2,1)} broadcast(bf16[128,672]{0,1:T(8,128)(2,1)} %bitcast.29), dimensions={1,2} | broadcast | bytes 860160 | tf_op jit(solution)/shard_map/broadcast_in_dim | solution.py:209
  11.1 4.3 %all-to-all-start.2 = ((bf16[4,128,672]{1,2,0:T(8,128)(2,1)}), bf16[4,128,672]{1,2,0:T(8,128)(2,1)S(1)}, u32[]{:S(2)}, u32[]{:S(2)}) async-start(bf16[4,128,672]{1,2,0:T(8,128)(2,1)} %broadcast_in_dim.22), calls=%async_computation.2 | async-start | bytes 1376256 | tf_op jit(solution)/shard_map/all_to_all | solution.py:210
  16.1 10.3 %all-to-all-done.2 = bf16[4,128,672]{1,2,0:T(8,128)(2,1)S(1)} async-done(((bf16[4,128,672]{1,2,0:T(8,128)(2,1)}), bf16[4,128,672]{1,2,0:T(8,128)(2,1)S(1)}, u32[]{:S(2)}, u32[]{:S(2)}) %all-to-all-start.2) | async-done | bytes 688160 | tf_op jit(solution)/shard_map/all_to_all | solution.py:210
  27.6 3.7 %all-to-all-start = ((bf16[4,256,672]{1,2,0:T(8,128)(2,1)}), bf16[4,256,672]{1,2,0:T(8,128)(2,1)S(1)}, u32[]{:S(2)}, u32[]{:S(2)}) async-start(bf16[4,256,672]{1,2,0:T(8,128)(2,1)} %broadcast_in_dim.19), calls=%async_computation | async-start | bytes 2752512 | tf_op jit(solution)/shard_map/all_to_all | solution.py:210
  33.2 4.7 %project_back.1 = (bf16[128,512]{1,0:T(8,128)(2,1)}, bf16[128,512]{1,0:T(8,128)(2,1)}, f32[128,128]{1,0:T(8,128)}) custom-call(bf16[4,128,672]{2,1,0:T(8,128)(2,1)} %copy.44.x_ref, f32[4,1,672]{2,1,0:T(1,128)} %reshape_squeeze.19.gain_ref, bf16[4,672,512]{2,1,0:T(8,128)(2,1)} %bitcast.16, bf16[4,672,256]{2,1,0:T(8,128)(2,1)} %bitcast.19, ...), custom_call_target="tpu_custom_call" | custom-call | tf_op jit(solution)/shard_map/project_back/pallas_call | solution.py:252
  37.9 14.8 %collective-permute-start.6 = (bf16[128,512]{1,0:T(8,128)(2,1)}, bf16[128,512]{1,0:T(8,128)(2,1)S(1)}, u32[]{:S(2)}, u32[]{:S(2)}) collective-permute-start(bf16[128,512]{1,0:T(8,128)(2,1)} %get-tuple-element.17.own), channel_id=1, source_target_pairs={{0,8},{4,12},{8,16},{12,20},{16,24},{20,28},{24,32},{28,36},{32,40... | collective-permute-start | bytes 393224 | tf_op jit(solution)/shard_map/ppermute | solution.py:193
  52.7 4.7 %collective-permute-start.7 = (bf16[128,512]{1,0:T(8,128)(2,1)}, bf16[128,512]{1,0:T(8,128)(2,1)S(1)}, u32[]{:S(2)}, u32[]{:S(2)}) collective-permute-start(bf16[128,512]{1,0:T(8,128)(2,1)} %get-tuple-element.17.own), channel_id=1, source_target_pairs={{0,16},{4,20},{8,24},{12,28},{16,32},{20,36},{24,40},{28,44},{32,4... | collective-permute-start | bytes 393224 | tf_op jit(solution)/shard_map/ppermute | solution.py:193
  57.4 2.7 %collective-permute-done.6.two = bf16[128,512]{1,0:T(8,128)(2,1)S(1)} collective-permute-done((bf16[128,512]{1,0:T(8,128)(2,1)}, bf16[128,512]{1,0:T(8,128)(2,1)S(1)}, u32[]{:S(2)}, u32[]{:S(2)}) %collective-permute-start.6) | collective-permute-done | bytes 131104 | tf_op jit(solution)/shard_map/ppermute | solution.py:193
  60.1 1.9 %collective-permute-start.8 = (bf16[128,512]{1,0:T(8,128)(2,1)S(1)}, bf16[128,512]{1,0:T(8,128)(2,1)S(1)}, u32[]{:S(2)}, u32[]{:S(2)}) collective-permute-start(bf16[128,512]{1,0:T(8,128)(2,1)S(1)} %collective-permute-done.6.two), channel_id=1, source_target_pairs={{0,4},{4,0},{8,12},{12,8},{16,20},{20,16},{24,28},{28,24},{32,36},... | collective-permute-start | bytes 393224 | tf_op jit(solution)/shard_map/ppermute | solution.py:198
  63.0 1.9 %collective-permute-start.9 = (bf16[128,512]{1,0:T(8,128)(2,1)S(1)}, bf16[128,512]{1,0:T(8,128)(2,1)S(1)}, u32[]{:S(2)}, u32[]{:S(2)}) collective-permute-start(bf16[128,512]{1,0:T(8,128)(2,1)S(1)} %broadcast_select_fusion.2), channel_id=1, source_target_pairs={{0,4},{4,0},{8,12},{12,8},{16,20},{20,16},{24,28},{28,24},{32,36},... | collective-permute-start | bytes 393224 | tf_op jit(solution)/shard_map/ppermute | solution.py:198
  65.0 1.6 copy.39.x_ref
  66.6 6.7 %project_front.1 = (bf16[128,512]{1,0:T(8,128)(2,1)}, bf16[128,512]{1,0:T(8,128)(2,1)}, bf16[128,512]{1,0:T(8,128)(2,1)}) custom-call(bf16[4,256,672]{2,1,0:T(8,128)(2,1)} %copy.39.x_ref, f32[4,1,672]{2,1,0:T(1,128)} %reshape_squeeze.19.gain_ref, bf16[4,672,512]{2,1,0:T(8,128)(2,1)} %bitcast.17, bf16[4,672,256]{2,1,0:T(8,128)(2,1)} %bitcast.20, ...), custom_call_target="tpu_custom_call" | custom-call | tf_op jit(solution)/shard_map/project_front/pallas_call | solution.py:259
  73.3 9.8 %collective-permute-start.2 = (bf16[128,512]{1,0:T(8,128)(2,1)}, bf16[128,512]{1,0:T(8,128)(2,1)S(1)}, u32[]{:S(2)}, u32[]{:S(2)}) collective-permute-start(bf16[128,512]{1,0:T(8,128)(2,1)} %get-tuple-element.14.own), channel_id=1, source_target_pairs={{0,8},{4,12},{8,16},{12,20},{16,24},{20,28},{24,32},{28,36},{32,40... | collective-permute-start | bytes 393224 | tf_op jit(solution)/shard_map/ppermute | solution.py:193
  83.1 4.4 %collective-permute-start.3 = (bf16[128,512]{1,0:T(8,128)(2,1)}, bf16[128,512]{1,0:T(8,128)(2,1)S(1)}, u32[]{:S(2)}, u32[]{:S(2)}) collective-permute-start(bf16[128,512]{1,0:T(8,128)(2,1)} %get-tuple-element.14.own), channel_id=1, source_target_pairs={{0,16},{4,20},{8,24},{12,28},{16,32},{20,36},{24,40},{28,44},{32,4... | collective-permute-start | bytes 393224 | tf_op jit(solution)/shard_map/ppermute | solution.py:193
  88.9 4.7 %attend_back.1 = (bf16[128,512]{1,0:T(8,128)(2,1)}, f32[128,512]{1,0:T(8,128)}, f32[128,512]{1,0:T(8,128)}, f32[128,512]{1,0:T(8,128)}, bf16[256,512]{1,0:T(8,128)(2,1)}) custom-call(s32[3]{0:T(128)} %pad_add_fusion.info_ref, s32[32,128]{1,0:T(8,128)} %bitcast.32, bf16[128,512]{1,0:T(8,128)(2,1)} %get-tuple-element.15.q_ref, ...), custom_call_target="tpu_custom_call" | custom-call | tf_op jit(solution)/shard_map/attend_back/pallas_call | solution.py:266
  93.6 1.9 %collective-permute-start.10 = (bf16[256,512]{1,0:T(8,128)(2,1)}, bf16[256,512]{1,0:T(8,128)(2,1)S(1)}, u32[]{:S(2)}, u32[]{:S(2)}) collective-permute-start(bf16[256,512]{1,0:T(8,128)(2,1)} %get-tuple-element.20), channel_id=1, source_target_pairs={{0,4},{4,0},{8,12},{12,8},{16,20},{20,16},{24,28},{28,24},{32,36},... | collective-permute-start | bytes 786440 | tf_op jit(solution)/shard_map/ppermute | solution.py:198
  95.6 2.4 %collective-permute-start.4 = (bf16[128,512]{1,0:T(8,128)(2,1)S(1)}, bf16[128,512]{1,0:T(8,128)(2,1)S(1)}, u32[]{:S(2)}, u32[]{:S(2)}) collective-permute-start(bf16[128,512]{1,0:T(8,128)(2,1)S(1)} %collective-permute-done.2.two), channel_id=1, source_target_pairs={{0,4},{4,0},{8,12},{12,8},{16,20},{20,16},{24,28},{28,24},{32,36},... | collective-permute-start | bytes 393224 | tf_op jit(solution)/shard_map/ppermute | solution.py:198
  99.0 1.9 %collective-permute-start.5 = (bf16[128,512]{1,0:T(8,128)(2,1)S(1)}, bf16[128,512]{1,0:T(8,128)(2,1)S(1)}, u32[]{:S(2)}, u32[]{:S(2)}) collective-permute-start(bf16[128,512]{1,0:T(8,128)(2,1)S(1)} %broadcast_select_fusion.3), channel_id=1, source_target_pairs={{0,4},{4,0},{8,12},{12,8},{16,20},{20,16},{24,28},{28,24},{32,36},... | collective-permute-start | bytes 393224 | tf_op jit(solution)/shard_map/ppermute | solution.py:198
  100.9 1.3 collective-permute-done.5.mid
  102.9 5.4 %attend.1 = bf16[4,128,672]{2,1,0:T(8,128)(2,1)} custom-call(s32[3]{0:T(128)} %pad_add_fusion.info_ref, s32[32,128]{1,0:T(8,128)} %bitcast.33, bf16[128,512]{1,0:T(8,128)(2,1)} %get-tuple-element.13.q_ref, bf16[128,512]{1,0:T(8,128)(2,1)} %get-tuple-element.14.own, bf16[128,512]{1,0:T(8,128)(2,1)} %copy-done.13, bf16[128,512]{1,0:T(8,128)(2,1)} %copy-done.4, ...), custom_call_target="tpu_custom_call" | custom-call | tf_op jit(solution)/shard_map/attend/pallas_call | solution.py:278
  108.2 2.4 %copy.40 = bf16[4,128,672]{1,2,0:T(8,128)(2,1)} copy(bf16[4,128,672]{2,1,0:T(8,128)(2,1)} %attend.1) | data formatting | bytes 1376256 | tf_op jit(solution)/shard_map/attend/pallas_call | solution.py:278
  110.6 4.4 %all-to-all-start.1 = ((bf16[4,128,672]{1,2,0:T(8,128)(2,1)}), bf16[4,128,672]{1,2,0:T(8,128)(2,1)S(1)}, u32[]{:S(2)}, u32[]{:S(2)}) async-start(bf16[4,128,672]{1,2,0:T(8,128)(2,1)} %copy.40), calls=%async_computation.1 | async-start | bytes 1376256 | tf_op jit(solution)/shard_map/all_to_all | solution.py:283
  115.8 4.7 %collective-permute-start.11 = (bf16[128,512]{1,0:T(8,128)(2,1)S(1)}, bf16[128,512]{1,0:T(8,128)(2,1)S(1)}, u32[]{:S(2)}, u32[]{:S(2)}) collective-permute-start(bf16[128,512]{1,0:T(8,128)(2,1)S(1)} %get-tuple-element.31), channel_id=1, source_target_pairs={{8,0},{12,4},{16,8},{20,12},{24,16},{28,20},{32,24},{36,28},{40,32... | collective-permute-start | bytes 393224 | tf_op jit(solution)/shard_map/ppermute | solution.py:193
  120.6 2.3 %collective-permute-start.12 = (bf16[128,512]{1,0:T(8,128)(2,1)S(1)}, bf16[128,512]{1,0:T(8,128)(2,1)S(1)}, u32[]{:S(2)}, u32[]{:S(2)}) collective-permute-start(bf16[128,512]{1,0:T(8,128)(2,1)S(1)} %get-tuple-element.30), channel_id=1, source_target_pairs={{16,0},{20,4},{24,8},{28,12},{32,16},{36,20},{40,24},{44,28},{48,3... | collective-permute-start | bytes 393224 | tf_op jit(solution)/shard_map/ppermute | solution.py:193
  122.9 12.1 %collective-permute-done.11.two_ref = bf16[128,512]{1,0:T(8,128)(2,1)S(1)} collective-permute-done((bf16[128,512]{1,0:T(8,128)(2,1)S(1)}, bf16[128,512]{1,0:T(8,128)(2,1)S(1)}, u32[]{:S(2)}, u32[]{:S(2)}) %collective-permute-start.11) | collective-permute-done | bytes 131104 | tf_op jit(solution)/shard_map/ppermute | solution.py:193
  135.6 5.9 %input_terms.1 = bf16[4,128,768]{2,1,0:T(8,128)(2,1)} custom-call(bf16[128,512]{1,0:T(8,128)(2,1)} %get-tuple-element.18.dq_ref, f32[128,512]{1,0:T(8,128)} %get-tuple-element.32.own_ref, bf16[128,512]{1,0:T(8,128)(2,1)} %copy-done.10, bf16[128,512]{1,0:T(8,128)(2,1)} %copy-done.11, bf16[4,128,672]{2,1,0:T(8,128)(2,1)} %copy.44.x_ref, ...), custom_call_target="tpu_custom_call" | custom-call | tf_op jit(solution)/shard_map/input_terms/pallas_call | solution.py:287
  141.5 4.6 %all-to-all-start.3 = ((bf16[4,128,768]{2,1,0:T(8,128)(2,1)}), bf16[4,128,768]{2,1,0:T(8,128)(2,1)S(1)}, u32[]{:S(2)}, u32[]{:S(2)}) async-start(bf16[4,128,768]{2,1,0:T(8,128)(2,1)} %input_terms.1), calls=%async_computation.3 | async-start | bytes 1572864 | tf_op jit(solution)/shard_map/all_to_all | solution.py:292
  148.1 9.9 %all-to-all-done.3.sums_ref = bf16[4,128,768]{2,1,0:T(8,128)(2,1)S(1)} async-done(((bf16[4,128,768]{2,1,0:T(8,128)(2,1)}), bf16[4,128,768]{2,1,0:T(8,128)(2,1)S(1)}, u32[]{:S(2)}, u32[]{:S(2)}) %all-to-all-start.3) | async-done | bytes 786464 | tf_op jit(solution)/shard_map/all_to_all | solution.py:292
  158.9 2.3 %finish.1 = bf16[128,672]{1,0:T(8,128)(2,1)} custom-call(s32[3]{0:T(128)} %pad_add_fusion.info_ref, bf16[4,128,768]{2,1,0:T(8,128)(2,1)} %copy-done, bf16[128,672]{1,0:T(8,128)(2,1)} %bitcast.27, bf16[128,672]{1,0:T(8,128)(2,1)} %copy-done.1, f32[4,1,672]{2,1,0:T(1,128)} %reshape_squeeze.19.gain_ref, f32[128,128]{1,0:T(8,128)} %get-tuple-element.23.r_ref), custom_call_target="tpu_custom_call" | custom-call | tf_op jit(solution)/shard_map/finish/pallas_call | solution.py:293
  161.2 1.7 %copy.47 = bf16[1,128,672]{1,2,0:T(8,128)(2,1)} copy(bf16[1,128,672]{2,1,0:T(8,128)(2,1)} %bitcast.28) | data formatting | bytes 344064
  (71 shorter events, 14.1 us)
Async XLA Ops:
  1.7 13.7 %copy-start.8 = (bf16[128,672]{0,1:T(8,128)(2,1)S(1)}, bf16[128,672]{0,1:T(8,128)(2,1)}, u32[]{:S(2)}) copy-start(bf16[128,672]{0,1:T(8,128)(2,1)} %param.16) | copy-start | bytes 516100
  1.7 14.0 %collective-permute-start.1 = (bf16[128,672]{1,0:T(8,128)(2,1)S(1)}, bf16[128,672]{1,0:T(8,128)(2,1)S(1)}, u32[]{:S(2)}, u32[]{:S(2)}) collective-permute-start(bf16[128,672]{1,0:T(8,128)(2,1)S(1)} %bitcast.31), channel_id=1, source_target_pairs={{128,0},{256,128},{384,256},{512,384},{640,512},{129,1},{257,129},... | collective-permute-start | bytes 516104 | tf_op jit(solution)/shard_map/ppermute | solution.py:204
  4.8 10.8 %copy-start.9 = (bf16[128,672]{0,1:T(8,128)(2,1)S(1)}, bf16[128,672]{0,1:T(8,128)(2,1)}, u32[]{:S(2)}) copy-start(bf16[128,672]{0,1:T(8,128)(2,1)} %param.12) | copy-start | bytes 516100
  4.8 11.0 %collective-permute-start = (bf16[128,672]{1,0:T(8,128)(2,1)S(1)}, bf16[128,672]{1,0:T(8,128)(2,1)S(1)}, u32[]{:S(2)}, u32[]{:S(2)}) collective-permute-start(bf16[128,672]{1,0:T(8,128)(2,1)S(1)} %bitcast.30), channel_id=1, source_target_pairs={{0,128},{128,256},{256,384},{384,512},{512,640},{1,129},{129,257},... | collective-permute-start | bytes 516104 | tf_op jit(solution)/shard_map/ppermute | solution.py:204
  11.1 15.2 %all-to-all-start.2 = ((bf16[4,128,672]{1,2,0:T(8,128)(2,1)}), bf16[4,128,672]{1,2,0:T(8,128)(2,1)S(1)}, u32[]{:S(2)}, u32[]{:S(2)}) async-start(bf16[4,128,672]{1,2,0:T(8,128)(2,1)} %broadcast_in_dim.22), calls=%async_computation.2 | async-start | bytes 1376256 | tf_op jit(solution)/shard_map/all_to_all | solution.py:210
  15.8 11.8 %copy-start.1 = (bf16[128,672]{1,0:T(8,128)(2,1)}, bf16[128,672]{1,0:T(8,128)(2,1)S(1)}, u32[]{:S(2)}) copy-start(bf16[128,672]{1,0:T(8,128)(2,1)S(1)} %broadcast_select_fusion.up_ref) | copy-start | bytes 516100
  27.6 3.7 %copy-start.18 = (f32[1,2688]{1,0:T(1,128)S(1)}, f32[1,2688]{1,0:T(1,128)}, u32[]{:S(2)}) copy-start(f32[1,2688]{1,0:T(1,128)} %param.17) | copy-start | bytes 32260
  27.6 37.4 %all-to-all-start = ((bf16[4,256,672]{1,2,0:T(8,128)(2,1)}), bf16[4,256,672]{1,2,0:T(8,128)(2,1)S(1)}, u32[]{:S(2)}, u32[]{:S(2)}) async-start(bf16[4,256,672]{1,2,0:T(8,128)(2,1)} %broadcast_in_dim.19), calls=%async_computation | async-start | bytes 2752512 | tf_op jit(solution)/shard_map/all_to_all | solution.py:210
  37.9 22.3 %collective-permute-start.6 = (bf16[128,512]{1,0:T(8,128)(2,1)}, bf16[128,512]{1,0:T(8,128)(2,1)S(1)}, u32[]{:S(2)}, u32[]{:S(2)}) collective-permute-start(bf16[128,512]{1,0:T(8,128)(2,1)} %get-tuple-element.17.own), channel_id=1, source_target_pairs={{0,8},{4,12},{8,16},{12,20},{16,24},{20,28},{24,32},{28,36},{32,40... | collective-permute-start | bytes 393224 | tf_op jit(solution)/shard_map/ppermute | solution.py:193
  52.7 9.4 %collective-permute-start.7 = (bf16[128,512]{1,0:T(8,128)(2,1)}, bf16[128,512]{1,0:T(8,128)(2,1)S(1)}, u32[]{:S(2)}, u32[]{:S(2)}) collective-permute-start(bf16[128,512]{1,0:T(8,128)(2,1)} %get-tuple-element.17.own), channel_id=1, source_target_pairs={{0,16},{4,20},{8,24},{12,28},{16,32},{20,36},{24,40},{28,44},{32,4... | collective-permute-start | bytes 393224 | tf_op jit(solution)/shard_map/ppermute | solution.py:193
  60.1 6.5 %copy-start.12 = (bf16[128,512]{1,0:T(8,128)(2,1)}, bf16[128,512]{1,0:T(8,128)(2,1)S(1)}, u32[]{:S(2)}) copy-start(bf16[128,512]{1,0:T(8,128)(2,1)S(1)} %collective-permute-done.6.two) | copy-start | bytes 393220
  60.1 28.1 %collective-permute-start.8 = (bf16[128,512]{1,0:T(8,128)(2,1)S(1)}, bf16[128,512]{1,0:T(8,128)(2,1)S(1)}, u32[]{:S(2)}, u32[]{:S(2)}) collective-permute-start(bf16[128,512]{1,0:T(8,128)(2,1)S(1)} %collective-permute-done.6.two), channel_id=1, source_target_pairs={{0,4},{4,0},{8,12},{12,8},{16,20},{20,16},{24,28},{28,24},{32,36},... | collective-permute-start | bytes 393224 | tf_op jit(solution)/shard_map/ppermute | solution.py:198
  62.0 4.5 %copy-start.3 = (bf16[128,512]{1,0:T(8,128)(2,1)}, bf16[128,512]{1,0:T(8,128)(2,1)S(1)}, u32[]{:S(2)}) copy-start(bf16[128,512]{1,0:T(8,128)(2,1)S(1)} %collective-permute-done.7.four) | copy-start | bytes 393220
  63.0 25.2 %collective-permute-start.9 = (bf16[128,512]{1,0:T(8,128)(2,1)S(1)}, bf16[128,512]{1,0:T(8,128)(2,1)S(1)}, u32[]{:S(2)}, u32[]{:S(2)}) collective-permute-start(bf16[128,512]{1,0:T(8,128)(2,1)S(1)} %broadcast_select_fusion.2), channel_id=1, source_target_pairs={{0,4},{4,0},{8,12},{12,8},{16,20},{20,16},{24,28},{28,24},{32,36},... | collective-permute-start | bytes 393224 | tf_op jit(solution)/shard_map/ppermute | solution.py:198
  73.3 22.2 %collective-permute-start.2 = (bf16[128,512]{1,0:T(8,128)(2,1)}, bf16[128,512]{1,0:T(8,128)(2,1)S(1)}, u32[]{:S(2)}, u32[]{:S(2)}) collective-permute-start(bf16[128,512]{1,0:T(8,128)(2,1)} %get-tuple-element.14.own), channel_id=1, source_target_pairs={{0,8},{4,12},{8,16},{12,20},{16,24},{20,28},{24,32},{28,36},{32,40... | collective-permute-start | bytes 393224 | tf_op jit(solution)/shard_map/ppermute | solution.py:193
  83.1 14.8 %collective-permute-start.3 = (bf16[128,512]{1,0:T(8,128)(2,1)}, bf16[128,512]{1,0:T(8,128)(2,1)S(1)}, u32[]{:S(2)}, u32[]{:S(2)}) collective-permute-start(bf16[128,512]{1,0:T(8,128)(2,1)} %get-tuple-element.14.own), channel_id=1, source_target_pairs={{0,16},{4,20},{8,24},{12,28},{16,32},{20,36},{24,40},{28,44},{32,4... | collective-permute-start | bytes 393224 | tf_op jit(solution)/shard_map/ppermute | solution.py:193
  88.2 0.7 copy-start.15
  93.6 21.4 %collective-permute-start.10 = (bf16[256,512]{1,0:T(8,128)(2,1)}, bf16[256,512]{1,0:T(8,128)(2,1)S(1)}, u32[]{:S(2)}, u32[]{:S(2)}) collective-permute-start(bf16[256,512]{1,0:T(8,128)(2,1)} %get-tuple-element.20), channel_id=1, source_target_pairs={{0,4},{4,0},{8,12},{12,8},{16,20},{20,16},{24,28},{28,24},{32,36},... | collective-permute-start | bytes 786440 | tf_op jit(solution)/shard_map/ppermute | solution.py:198
  95.6 6.7 %copy-start.13 = (bf16[128,512]{1,0:T(8,128)(2,1)}, bf16[128,512]{1,0:T(8,128)(2,1)S(1)}, u32[]{:S(2)}) copy-start(bf16[128,512]{1,0:T(8,128)(2,1)S(1)} %collective-permute-done.2.two) | copy-start | bytes 393220
  95.6 5.3 %collective-permute-start.4 = (bf16[128,512]{1,0:T(8,128)(2,1)S(1)}, bf16[128,512]{1,0:T(8,128)(2,1)S(1)}, u32[]{:S(2)}, u32[]{:S(2)}) collective-permute-start(bf16[128,512]{1,0:T(8,128)(2,1)S(1)} %collective-permute-done.2.two), channel_id=1, source_target_pairs={{0,4},{4,0},{8,12},{12,8},{16,20},{20,16},{24,28},{28,24},{32,36},... | collective-permute-start | bytes 393224 | tf_op jit(solution)/shard_map/ppermute | solution.py:198
  98.0 4.2 %copy-start.4 = (bf16[128,512]{1,0:T(8,128)(2,1)}, bf16[128,512]{1,0:T(8,128)(2,1)S(1)}, u32[]{:S(2)}) copy-start(bf16[128,512]{1,0:T(8,128)(2,1)S(1)} %collective-permute-done.3.four) | copy-start | bytes 393220
  99.0 3.2 %collective-permute-start.5 = (bf16[128,512]{1,0:T(8,128)(2,1)S(1)}, bf16[128,512]{1,0:T(8,128)(2,1)S(1)}, u32[]{:S(2)}, u32[]{:S(2)}) collective-permute-start(bf16[128,512]{1,0:T(8,128)(2,1)S(1)} %broadcast_select_fusion.3), channel_id=1, source_target_pairs={{0,4},{4,0},{8,12},{12,8},{16,20},{20,16},{24,28},{28,24},{32,36},... | collective-permute-start | bytes 393224 | tf_op jit(solution)/shard_map/ppermute | solution.py:198
  100.9 1.3 copy-start.16
  108.2 6.8 %copy-start.5 = (f32[128,512]{1,0:T(8,128)S(1)}, f32[128,512]{1,0:T(8,128)}, u32[]{:S(2)}) copy-start(f32[128,512]{1,0:T(8,128)} %get-tuple-element.19) | copy-start | bytes 786436
  108.2 6.8 %copy-start.6 = (f32[128,512]{1,0:T(8,128)S(1)}, f32[128,512]{1,0:T(8,128)}, u32[]{:S(2)}) copy-start(f32[128,512]{1,0:T(8,128)} %get-tuple-element.21) | copy-start | bytes 786436
  108.2 6.8 %copy-start.7 = (f32[128,512]{1,0:T(8,128)S(1)}, f32[128,512]{1,0:T(8,128)}, u32[]{:S(2)}) copy-start(f32[128,512]{1,0:T(8,128)} %get-tuple-element.22) | copy-start | bytes 786436
  110.6 30.9 %all-to-all-start.1 = ((bf16[4,128,672]{1,2,0:T(8,128)(2,1)}), bf16[4,128,672]{1,2,0:T(8,128)(2,1)S(1)}, u32[]{:S(2)}, u32[]{:S(2)}) async-start(bf16[4,128,672]{1,2,0:T(8,128)(2,1)} %copy.40), calls=%async_computation.1 | async-start | bytes 1376256 | tf_op jit(solution)/shard_map/all_to_all | solution.py:283
  115.8 19.1 %collective-permute-start.11 = (bf16[128,512]{1,0:T(8,128)(2,1)S(1)}, bf16[128,512]{1,0:T(8,128)(2,1)S(1)}, u32[]{:S(2)}, u32[]{:S(2)}) collective-permute-start(bf16[128,512]{1,0:T(8,128)(2,1)S(1)} %get-tuple-element.31), channel_id=1, source_target_pairs={{8,0},{12,4},{16,8},{20,12},{24,16},{28,20},{32,24},{36,28},{40,32... | collective-permute-start | bytes 393224 | tf_op jit(solution)/shard_map/ppermute | solution.py:193
  120.6 14.4 %collective-permute-start.12 = (bf16[128,512]{1,0:T(8,128)(2,1)S(1)}, bf16[128,512]{1,0:T(8,128)(2,1)S(1)}, u32[]{:S(2)}, u32[]{:S(2)}) collective-permute-start(bf16[128,512]{1,0:T(8,128)(2,1)S(1)} %get-tuple-element.30), channel_id=1, source_target_pairs={{16,0},{20,4},{24,8},{28,12},{32,16},{36,20},{40,24},{44,28},{48,3... | collective-permute-start | bytes 393224 | tf_op jit(solution)/shard_map/ppermute | solution.py:193
  141.5 4.7 %copy-start.2 = (bf16[1,128,672]{1,2,0:T(8,128)(2,1)S(1)}, bf16[1,128,672]{1,2,0:T(8,128)(2,1)}, u32[]{:S(2)}) copy-start(bf16[1,128,672]{1,2,0:T(8,128)(2,1)} %param.14) | copy-start | bytes 516100
  141.5 16.5 %all-to-all-start.3 = ((bf16[4,128,768]{2,1,0:T(8,128)(2,1)}), bf16[4,128,768]{2,1,0:T(8,128)(2,1)S(1)}, u32[]{:S(2)}, u32[]{:S(2)}) async-start(bf16[4,128,768]{2,1,0:T(8,128)(2,1)} %input_terms.1), calls=%async_computation.3 | async-start | bytes 1572864 | tf_op jit(solution)/shard_map/all_to_all | solution.py:292
  158.0 0.9 copy-start
  (4 other events, 2.6 us)

commit v2 on v1

v2 whole, which is shorter than its diff:
```python
import jax
import jax.numpy as jnp
from jax import lax
from jax.experimental import pallas as pl
from jax.experimental.pallas import tpu as pltpu
from jax.sharding import PartitionSpec as P


HEAD = 128
WINDOW = 512
SCALE = HEAD ** (-0.5)
BF = jnp.bfloat16
F32 = jnp.float32
LIMIT = 14
SENDS = (0, 1, 3, 2)


def dot_nn(left, right):
    return lax.dot_general(left, right, (((1,), (0,)), ((), ())), preferred_element_type=F32)


def dot_nt(left, right):
    return lax.dot_general(left, right, (((1,), (1,)), ((), ())), preferred_element_type=F32)


def dot_tn(left, right):
    return lax.dot_general(left, right, (((0,), (0,)), ((), ())), preferred_element_type=F32)


def vmem(count):
    return [pl.BlockSpec(memory_space=pltpu.VMEM) for _ in range(count)]


def smem():
    return pl.BlockSpec(memory_space=pltpu.SMEM)


def limit(mebibytes):
    return pltpu.CompilerParams(vmem_limit_bytes=mebibytes * 2**20)


def cost(microseconds):
    return pl.CostEstimate(
        flops=0, transcendentals=0, bytes_accessed=int(microseconds * 3_300_000)
    )


def kernel(body, mebibytes, out_shape, in_specs, microseconds=4.0, scratch=()):
    single = not isinstance(out_shape, tuple)
    return pl.pallas_call(
        body,
        out_shape=out_shape,
        in_specs=in_specs,
        out_specs=vmem(1)[0] if single else tuple(vmem(len(out_shape))),
        scratch_shapes=scratch,
        compiler_params=limit(mebibytes),
        cost_estimate=cost(microseconds),
    )


def stacked(ref, start, share):
    return jnp.concatenate([ref[part, start : start + share, :] for part in range(ref.shape[0])], 0)


def normal_rows(value, gain_ref):
    value = jnp.transpose(value).astype(F32)
    mean = jnp.mean(value * value, axis=1, keepdims=True)
    factor = lax.rsqrt(mean + 1e-06)
    return (value * factor * gain_ref[...]).astype(BF), factor


def across(column):
    length = column.shape[0]
    return jnp.transpose(jnp.broadcast_to(column, (length, length)))


def project_rows(h, wk_ref, wv_ref, wq_ref, q_ref, kv_ref):
    half = kv_ref.shape[1] // 2
    kv_ref[:, :half] = dot_nn(h, wk_ref[...]).astype(BF)
    kv_ref[:, half:] = dot_nn(h, wv_ref[...]).astype(BF)
    q_ref[...] = dot_nn(h, wq_ref[...]).astype(BF)


def placed_parts(info_ref, own, one, minus, far, hold_ref):
    place = info_ref[2]
    parts = hold_ref.shape[0]
    for offset, piece in ((0, own), (parts - 1, one), (1, minus), (2, far)):
        hold_ref[lax.rem(place + offset, parts)] = piece[...]


def project_back_body(
    info_ref, own, one, minus, far, gain_ref, wk_ref, wv_ref, wq_ref,
    q_ref, kv_ref, r_ref, hold_ref,
):
    placed_parts(info_ref, own, one, minus, far, hold_ref)
    h, factor = normal_rows(stacked(hold_ref, 0, hold_ref.shape[1]), gain_ref)
    r_ref[...] = jnp.broadcast_to(factor, r_ref.shape)
    project_rows(h, wk_ref, wv_ref, wq_ref, q_ref, kv_ref)


def project_front_body(
    info_ref, own, one, minus, far, gain_ref, wk_ref, wv_ref, wq_ref, wo_ref,
    q_ref, kv_ref, da_ref, hold_ref,
):
    placed_parts(info_ref, own, one, minus, far, hold_ref)
    share = hold_ref.shape[1] // 2
    h, _ = normal_rows(stacked(hold_ref, 0, share), gain_ref)
    project_rows(h, wk_ref, wv_ref, wq_ref, q_ref, kv_ref)
    grad = dot_nn(wo_ref[...], stacked(hold_ref, share, share))
    da_ref[...] = jnp.transpose(grad.astype(BF))


def touch_body(info_ref, gain_ref, wk_ref, wv_ref, wq_ref, wo_ref, out_ref, hold_ref):
    share, length = out_ref.shape
    hold_ref[...] = jnp.transpose(jnp.broadcast_to(gain_ref[...], (length, gain_ref.shape[1])))
    out_ref[...] = hold_ref[pl.ds(pl.multiple_of(info_ref[2] * share, 32), share), :]


def choose_body(info_ref, emb_ref, arr_ref, loss_ref, ret_ref, out_ref):
    share = emb_ref.shape[0]
    out_ref[:share] = jnp.where(info_ref[3] == 1, emb_ref[...], arr_ref[...])
    out_ref[share:] = jnp.where(info_ref[4] == 1, loss_ref[...], ret_ref[...])


def select_body(info_ref, kv_ref, four_ref, out_ref):
    out_ref[...] = jnp.where(info_ref[0] == 0, kv_ref[...], four_ref[...])


def combine_body(info_ref, own_ref, two_ref, four_ref, swap_ref, town_ref, ttwo_ref, tfour_ref):
    length = own_ref.shape[0]
    core = info_ref[0]
    late = swap_ref[:length].astype(F32)
    mid = swap_ref[length:].astype(F32)
    town_ref[...] = own_ref[...] + jnp.where(core == 0, mid, 0.0)
    ttwo_ref[...] = (two_ref[...] + late).astype(BF)
    tfour_ref[...] = (four_ref[...] + jnp.where(core == 0, 0.0, mid)).astype(BF)


def window_mask(info_ref, docs_ref, length):
    core = info_ref[0]
    index = info_ref[1]
    offsets = (0, 2, 4, 3 - 2 * core, 1 + 2 * core)
    q_row = jnp.broadcast_to(docs_ref[pl.ds(index, 1), :], (length, length))
    q_doc = jnp.transpose(q_row)
    across = lax.broadcasted_iota(jnp.int32, (length, length), 1)
    down = lax.broadcasted_iota(jnp.int32, (length, length), 0)
    masks = []
    for offset in offsets:
        block = index - offset
        k_doc = docs_ref[pl.ds(jnp.maximum(block, 0), 1), :]
        ahead = down - across + offset * length
        keep = (ahead >= 0) & (ahead < WINDOW) & (block >= 0)
        masks.append(keep & (jnp.broadcast_to(k_doc, (length, length)) == q_doc))
    return jnp.concatenate([jnp.where(m, 0.0, -1e30) for m in masks], axis=1)


def softmax_rows(q_rows, keys, bias):
    scores = dot_nt(q_rows, keys) * SCALE + bias
    top = jnp.max(scores, axis=1, keepdims=True)
    expo = jnp.exp(scores - top)
    return expo / jnp.sum(expo, axis=1, keepdims=True)


def head_rows(blocks, start):
    return jnp.concatenate([block[:, start : start + HEAD] for block in blocks], axis=0)


def attend_body(info_ref, docs_ref, q_ref, own, two, four, mid, late, wo_ref, *outs):
    length = q_ref.shape[0]
    hold_ref = outs[4]
    kv_heads = own.shape[1] // (2 * HEAD)
    groups = q_ref.shape[1] // HEAD // kv_heads
    bias = window_mask(info_ref, docs_ref, length)
    blocks = (own, two, four, mid, late)
    heads = []
    for kv in range(kv_heads):
        keys = head_rows(blocks, kv * HEAD)
        values = head_rows(blocks, (kv_heads + kv) * HEAD)
        for group in range(groups):
            head = kv * groups + group
            rows = q_ref[:, head * HEAD : (head + 1) * HEAD]
            probs = softmax_rows(rows, keys, bias).astype(BF)
            heads.append(dot_nn(probs, values).astype(BF))
    mixed = jnp.concatenate(heads, axis=1)
    whole = jnp.transpose(dot_nn(mixed, wo_ref[...]).astype(BF))
    hold_ref[...] = whole.reshape(hold_ref.shape)
    parts = hold_ref.shape[0]
    for out_ref, offset in zip(outs, SENDS):
        out_ref[...] = hold_ref[lax.rem(info_ref[2] + offset, parts)]


def attend_back_body(
    info_ref, docs_ref, q_ref, da_ref, own, two, four, mid, late,
    dq_ref, town_ref, ttwo_ref, tfour_ref, tswap_ref,
):
    length = da_ref.shape[0]
    kv_heads = own.shape[1] // (2 * HEAD)
    groups = q_ref.shape[1] // HEAD // kv_heads
    bias = window_mask(info_ref, docs_ref, length)
    blocks = (own, two, four, mid, late)
    for kv in range(kv_heads):
        at = (kv_heads + kv) * HEAD
        keys = head_rows(blocks, kv * HEAD)
        values = head_rows(blocks, at)
        d_key = d_value = 0.0
        for group in range(groups):
            head = kv * groups + group
            span = slice(head * HEAD, (head + 1) * HEAD)
            rows = q_ref[:, span]
            grad = da_ref[:, span]
            probs = softmax_rows(rows, keys, bias)
            d_value = d_value + dot_tn(probs.astype(BF), grad)
            d_probs = dot_nt(grad, values)
            delta = jnp.sum(probs * d_probs, axis=1, keepdims=True)
            d_scores = (probs * (d_probs - delta)).astype(BF)
            dq_ref[:, span] = (dot_nn(d_scores, keys) * SCALE).astype(BF)
            d_key = d_key + dot_tn(d_scores, rows)
        for terms, start in ((d_key, kv * HEAD), (d_value, at)):
            cols = slice(start, start + HEAD)
            town_ref[:, cols] = terms[:length]
            ttwo_ref[:, cols] = terms[length : 2 * length]
            tfour_ref[:, cols] = terms[2 * length : 3 * length]
            tswap_ref[:length, cols] = terms[4 * length :].astype(BF)
            tswap_ref[length:, cols] = terms[3 * length : 4 * length].astype(BF)


def input_terms_body(
    info_ref, dq_ref, own_ref, two_ref, four_ref, q_ref, kv_ref, wk_ref, wv_ref, wq_ref, *outs
):
    rows, length = outs[0].shape
    parts = len(outs)
    share = wq_ref.shape[0] // parts
    half = own_ref.shape[1] // 2
    total = own_ref[...] + two_ref[...].astype(F32) + four_ref[...].astype(F32)
    d_key = (total[:, :half] * SCALE).astype(BF)
    d_value = total[:, half:].astype(BF)
    d_query = dq_ref[...]
    row = jnp.sum(q_ref[...].astype(F32) * d_query.astype(F32), axis=1, keepdims=True)
    keys = kv_ref[:, :half].astype(F32) * d_key.astype(F32)
    values = kv_ref[:, half:].astype(F32) * d_value.astype(F32)
    row = across(row + jnp.sum(keys + values, axis=1, keepdims=True))[: rows - share]
    high = row.astype(BF).astype(F32)
    first = lax.broadcasted_iota(jnp.int32, (rows - share, length), 0) == 0
    pair = jnp.where(first, high, row - high).astype(BF)
    for out_ref, offset in zip(outs, SENDS):
        part = lax.rem(info_ref[2] + offset, parts)
        span = pl.ds(pl.multiple_of(part * share, 32), share)
        d_norm = dot_nt(wq_ref[span, :], d_query)
        d_norm = d_norm + dot_nt(wk_ref[span, :], d_key)
        d_norm = d_norm + dot_nt(wv_ref[span, :], d_value)
        out_ref[:share, :] = d_norm.astype(BF)
        out_ref[share:, :] = pair


def total_of(refs):
    return sum(ref[...].astype(F32) for ref in refs)


def finish_front_body(own, one, minus, far, both_ref, out_ref):
    share = out_ref.shape[0]
    total = total_of((own, one, minus, far))
    out_ref[...] = (both_ref[:share].astype(F32) + total).astype(BF)


def finish_body(own, one, minus, far, x_ref, both_ref, gain_ref, r_ref, out_ref):
    share = x_ref.shape[0]
    total = total_of((own, one, minus, far))
    row = (total[share : share + 1] + total[share + 1 : share + 2]) / (len(SENDS) * share)
    factor = jnp.transpose(r_ref[...])[:1]
    d_input = factor * gain_ref[...] * total[:share]
    d_input = d_input - x_ref[...].astype(F32) * (factor * factor * row)
    out_ref[...] = (both_ref[share:].astype(F32) + d_input).astype(BF)


def shifted(value, steps):
    count = lax.axis_size("seq")
    pairs = [(s, s + steps) for s in range(count) if 0 <= s + steps < count]
    return lax.ppermute(value, "seq", pairs)


def swapped(value):
    count = lax.axis_size("seq")
    return lax.ppermute(value, "seq", [(s, s ^ 1) for s in range(count)])


def next_section(value, steps):
    count = lax.axis_size("pipe")
    pairs = [(s, s + steps) for s in range(count) if 0 <= s + steps < count]
    return lax.ppermute(value, "pipe", pairs)


def exchanged(values):
    count = lax.axis_size("fsdp")
    received = []
    for value, offset in zip(values, SENDS[1:]):
        pairs = [(s, (s + offset) % count) for s in range(count)]
        received.append(lax.ppermute(value, "fsdp", pairs))
    return received


def window_blocks(info, kv):
    two = shifted(kv, 2)
    four = shifted(kv, 4)
    mine = kernel(
        select_body, 4, jax.ShapeDtypeStruct(kv.shape, BF),
        [smem()] + vmem(2), 0.5,
    )(info, kv, four)
    mid = swapped(mine)
    late = swapped(two)
    return (kv, two, four, mid, late)


def step(
    embedded, sent_forward, stashed, sent_backward, loss_grad, norm_gain,
    w_query, w_key, value_projection, w_out, forward_docs, backward_docs,
):
    length, share = embedded.shape
    parts = lax.axis_size("fsdp")
    section = lax.axis_index("pipe")
    sections = lax.axis_size("pipe")
    index = lax.axis_index("seq")
    first = (section == 0).astype(jnp.int32)
    last = (section == sections - 1).astype(jnp.int32)
    info = jnp.stack([index % 2, index, lax.axis_index("fsdp"), first, last]).astype(jnp.int32)
    gain = norm_gain
    docs_front = forward_docs[0].reshape(-1, length)
    docs_back = backward_docs[0].reshape(-1, length)
    wq, wk, wv, wo = w_query[0], w_key[0], value_projection[0], w_out[0]
    q_cols = wq.shape[1]
    kv_cols = 2 * wk.shape[1]

    def rows(count, cols, kind=BF):
        return jax.ShapeDtypeStruct((count, cols), kind)

    def pieces(count):
        return pltpu.VMEM((parts, count, length), BF)

    stash = stashed[0].T
    arrived = next_section(sent_forward[0].T, 1)
    returned = next_section(sent_backward[0].T, -1)
    gathered = exchanged((stash,) * 3)
    own_gain = kernel(
        touch_body, LIMIT, rows(share, length, F32), [smem()] + vmem(5),
        scratch=[pltpu.VMEM((parts * share, length), F32)],
    )(info, gain, wk, wv, wq, wo)

    q_back, kv_back, factor = kernel(
        project_back_body, LIMIT,
        (rows(length, q_cols), rows(length, kv_cols), rows(length, length, F32)),
        [smem()] + vmem(8), scratch=[pieces(share)],
    )(info, stash, *gathered, gain, wk, wv, wq)
    blocks_back = window_blocks(info, kv_back)

    sent = kernel(
        choose_body, LIMIT, rows(2 * share, length), [smem()] + vmem(4), 1.0,
    )(info, embedded.T, arrived, loss_grad.T, returned)
    both = exchanged((sent,) * 3)
    q_front, kv_front, d_attn = kernel(
        project_front_body, LIMIT,
        (rows(length, q_cols), rows(length, kv_cols), rows(length, q_cols)),
        [smem()] + vmem(9), scratch=[pieces(2 * share)],
    )(info, sent, *both, gain, wk, wv, wq, wo)
    blocks_front = window_blocks(info, kv_front)

    terms = rows(length, kv_cols, F32)
    d_query, t_own, t_two, t_four, t_swap = kernel(
        attend_back_body, LIMIT,
        (rows(length, q_cols), terms, terms, terms, rows(2 * length, kv_cols)),
        [smem()] + vmem(8),
    )(info, docs_back, q_back, d_attn, *blocks_back)
    t_swap = swapped(t_swap)
    t_own, send_two, send_four = kernel(
        combine_body, LIMIT, (terms, rows(length, kv_cols), rows(length, kv_cols)),
        [smem()] + vmem(4), 1.0,
    )(info, t_own, t_two, t_four, t_swap)
    back_two = shifted(send_two, -2)
    back_four = shifted(send_four, -4)

    partial_out = kernel(
        attend_body, LIMIT, (rows(share, length),) * 4, [smem()] + vmem(8),
        scratch=[pieces(share)],
    )(info, docs_front, q_front, *blocks_front, wo)
    sums = exchanged(partial_out[1:])
    forward_out = kernel(finish_front_body, 8, rows(share, length), vmem(5), 1.0)(
        partial_out[0], *sums, sent
    )

    d_parts = kernel(
        input_terms_body, LIMIT, (rows(share + 16, length),) * 4,
        [smem()] + vmem(9),
    )(info, d_query, t_own, back_two, back_four, q_back, kv_back, wk, wv, wq)
    sums = exchanged(d_parts[1:])
    input_grad = kernel(finish_body, 8, rows(share, length), vmem(8), 1.0)(
        d_parts[0], *sums, stash, sent, own_gain, factor
    )
    return (forward_out.T[None], input_grad.T[None])


def solution(mesh):
    placed = (
        P("seq", "fsdp"),
        P("pipe", "seq", "fsdp"),
        P("pipe", "seq", "fsdp"),
        P("pipe", "seq", "fsdp"),
        P("seq", "fsdp"),
        P("pipe", None),
        P("pipe", None, "fsdp"),
        P("pipe", None, "fsdp"),
        P("pipe", None, "fsdp"),
        P("pipe", "fsdp", None),
        P("pipe", None),
        P("pipe", None),
    )
    return jax.shard_map(
        step,
        mesh=mesh,
        in_specs=placed,
        out_specs=(P("pipe", "seq", "fsdp"), P("pipe", "seq", "fsdp")),
        check_vma=False,
    )
```

time: 164 us -> 150 us (0.915)
  the two profiles are of different devices: /device:TPU:88 before, /device:TPU:80 now
where the time goes in v2:
time: 150 us; the launch traced here: 149 us
  starting transfers between devices  102 us (68%)
  waiting for transfers between devices  17.9 us (12%)
  Pallas kernels  17.8 us (12%)
  local copies, waits for them, and re-layouts  10.7 us (7%)
    ppermute x6, starting transfers between devices, shifted(): return lax.ppermute(value, 'seq', pairs)  46.9 us
    ppermute x12, starting transfers between devices, exchanged(): received.append(lax.ppermute(value, 'fsdp', pairs))  38.7 us
    ppermute x6, waiting for transfers between devices, shifted(): return lax.ppermute(value, 'seq', pairs)  10.7 us
    unnamed x34, local copies, waits for them, and re-layouts  10.6 us
    ppermute x5, starting transfers between devices, swapped(): return lax.ppermute(value, 'seq', [(s, s ^ 1) for s in range(count)])  10.1 us
    ppermute x2, starting transfers between devices, next_section(): return lax.ppermute(value, 'pipe', pairs)  6.2 us
    ppermute x12, waiting for transfers between devices, exchanged(): received.append(lax.ppermute(value, 'fsdp', pairs))  5.9 us
    pallas_call x1, Pallas kernels, step(): kernel(attend_back_body, LIMIT, (rows(length, q_cols), terms, terms, term...  3.1 us
  transfers between devices with their start and end apart: 25, of which 6 were waited for; matrix products, arithmetic and copies ran while one was open for 0% of the time, Pallas kernels for 11%

profile of v2, /device:TPU:80, one launch (start us, length us, event | category | flops | bytes accessed | tf_op | source)
XLA Modules:
  0.0 149.3 jit_solution(327982031537103009)
XLA Ops:
  0.6 4.3 %collective-permute-start = (bf16[672,128]{1,0:T(8,128)(2,1)}, bf16[672,128]{1,0:T(8,128)(2,1)S(1)}, u32[]{:S(2)}, u32[]{:S(2)}) collective-permute-start(bf16[672,128]{1,0:T(8,128)(2,1)} %bitcast.54), channel_id=1, source_target_pairs={{0,128},{128,256},{256,384},{384,512},{512,640},{1,129},{129,257},... | collective-permute-start | bytes 516104 | tf_op jit(solution)/shard_map/ppermute | solution.py:289
  4.9 1.9 %collective-permute-start.1 = (bf16[672,128]{1,0:T(8,128)(2,1)}, bf16[672,128]{1,0:T(8,128)(2,1)S(1)}, u32[]{:S(2)}, u32[]{:S(2)}) collective-permute-start(bf16[672,128]{1,0:T(8,128)(2,1)} %bitcast.55), channel_id=1, source_target_pairs={{128,0},{256,128},{384,256},{512,384},{640,512},{129,1},{257,129},... | collective-permute-start | bytes 516104 | tf_op jit(solution)/shard_map/ppermute | solution.py:289
  6.8 3.4 %collective-permute-start.12 = (bf16[672,128]{1,0:T(8,128)(2,1)}, bf16[672,128]{1,0:T(8,128)(2,1)S(1)}, u32[]{:S(2)}, u32[]{:S(2)}) collective-permute-start(bf16[672,128]{1,0:T(8,128)(2,1)} %bitcast.43), channel_id=1, source_target_pairs={{0,1},{1,2},{2,3},{3,0},{4,5},{5,6},{6,7},{7,4},{8,9},{9,10},{10,1... | collective-permute-start | bytes 516104 | tf_op jit(solution)/shard_map/ppermute | solution.py:297
  10.3 3.7 %collective-permute-start.13 = (bf16[672,128]{1,0:T(8,128)(2,1)}, bf16[672,128]{1,0:T(8,128)(2,1)S(1)}, u32[]{:S(2)}, u32[]{:S(2)}) collective-permute-start(bf16[672,128]{1,0:T(8,128)(2,1)} %bitcast.44), channel_id=1, source_target_pairs={{0,3},{1,0},{2,1},{3,2},{4,7},{5,4},{6,5},{7,6},{8,11},{9,8},{10,9... | collective-permute-start | bytes 516104 | tf_op jit(solution)/shard_map/ppermute | solution.py:297
  13.9 3.7 %collective-permute-start.14 = (bf16[672,128]{1,0:T(8,128)(2,1)}, bf16[672,128]{1,0:T(8,128)(2,1)S(1)}, u32[]{:S(2)}, u32[]{:S(2)}) collective-permute-start(bf16[672,128]{1,0:T(8,128)(2,1)} %bitcast.45), channel_id=1, source_target_pairs={{0,2},{1,3},{2,0},{3,1},{4,6},{5,7},{6,4},{7,5},{8,10},{9,11},{10,... | collective-permute-start | bytes 516104 | tf_op jit(solution)/shard_map/ppermute | solution.py:297
  20.2 2.5 %collective-permute-start.2 = (bf16[1344,128]{1,0:T(8,128)(2,1)S(1)}, bf16[1344,128]{1,0:T(8,128)(2,1)S(1)}, u32[]{:S(2)}, u32[]{:S(2)}) collective-permute-start(bf16[1344,128]{1,0:T(8,128)(2,1)S(1)} %shard_map.131.own.both_ref), channel_id=1, source_target_pairs={{0,1},{1,2},{2,3},{3,0},{4,5},{5,6},{6,7},{7,4},{8,9},{9,10},{10,1... | collective-permute-start | bytes 1032200 | tf_op jit(solution)/shard_map/ppermute | solution.py:297
  22.8 4.6 %collective-permute-start.3 = (bf16[1344,128]{1,0:T(8,128)(2,1)S(1)}, bf16[1344,128]{1,0:T(8,128)(2,1)S(1)}, u32[]{:S(2)}, u32[]{:S(2)}) collective-permute-start(bf16[1344,128]{1,0:T(8,128)(2,1)S(1)} %shard_map.131.own.both_ref), channel_id=1, source_target_pairs={{0,3},{1,0},{2,1},{3,2},{4,7},{5,4},{6,5},{7,6},{8,11},{9,8},{10,9... | collective-permute-start | bytes 1032200 | tf_op jit(solution)/shard_map/ppermute | solution.py:297
  27.3 2.4 %collective-permute-start.4 = (bf16[1344,128]{1,0:T(8,128)(2,1)S(1)}, bf16[1344,128]{1,0:T(8,128)(2,1)S(1)}, u32[]{:S(2)}, u32[]{:S(2)}) collective-permute-start(bf16[1344,128]{1,0:T(8,128)(2,1)S(1)} %shard_map.131.own.both_ref), channel_id=1, source_target_pairs={{0,2},{1,3},{2,0},{3,1},{4,6},{5,7},{6,4},{7,5},{8,10},{9,11},{10,... | collective-permute-start | bytes 1032200 | tf_op jit(solution)/shard_map/ppermute | solution.py:297
  37.7 3.5 %collective-permute-start.16 = (bf16[128,512]{1,0:T(8,128)(2,1)S(1)}, bf16[128,512]{1,0:T(8,128)(2,1)S(1)}, u32[]{:S(2)}, u32[]{:S(2)}) collective-permute-start(bf16[128,512]{1,0:T(8,128)(2,1)S(1)} %get-tuple-element.32.kv_ref.own), channel_id=1, source_target_pairs={{0,16},{4,20},{8,24},{12,28},{16,32},{20,36},{24,40},{28,44},{32,4... | collective-permute-start | bytes 393224 | tf_op jit(solution)/shard_map/ppermute | solution.py:278
  41.2 13.9 %collective-permute-start.15 = (bf16[128,512]{1,0:T(8,128)(2,1)S(1)}, bf16[128,512]{1,0:T(8,128)(2,1)S(1)}, u32[]{:S(2)}, u32[]{:S(2)}) collective-permute-start(bf16[128,512]{1,0:T(8,128)(2,1)S(1)} %get-tuple-element.32.kv_ref.own), channel_id=1, source_target_pairs={{0,8},{4,12},{8,16},{12,20},{16,24},{20,28},{24,32},{28,36},{32,40... | collective-permute-start | bytes 393224 | tf_op jit(solution)/shard_map/ppermute | solution.py:278
  55.7 1.9 %collective-permute-start.17 = (bf16[128,512]{1,0:T(8,128)(2,1)S(1)}, bf16[128,512]{1,0:T(8,128)(2,1)S(1)}, u32[]{:S(2)}, u32[]{:S(2)}) collective-permute-start(bf16[128,512]{1,0:T(8,128)(2,1)S(1)} %shard_map.137), channel_id=1, source_target_pairs={{0,4},{4,0},{8,12},{12,8},{16,20},{20,16},{24,28},{28,24},{32,36},... | collective-permute-start | bytes 393224 | tf_op jit(solution)/shard_map/ppermute | solution.py:283
  58.3 1.9 %collective-permute-start.18 = (bf16[128,512]{1,0:T(8,128)(2,1)S(1)}, bf16[128,512]{1,0:T(8,128)(2,1)S(1)}, u32[]{:S(2)}, u32[]{:S(2)}) collective-permute-start(bf16[128,512]{1,0:T(8,128)(2,1)S(1)} %collective-permute-done.15.two), channel_id=1, source_target_pairs={{0,4},{4,0},{8,12},{12,8},{16,20},{20,16},{24,28},{28,24},{32,36},... | collective-permute-start | bytes 393224 | tf_op jit(solution)/shard_map/ppermute | solution.py:283
  62.9 2.7 %shard_map.132 = (bf16[128,512]{1,0:T(8,128)(2,1)S(1)}, bf16[128,512]{1,0:T(8,128)(2,1)S(1)}, bf16[128,512]{1,0:T(8,128)(2,1)S(1)}) custom-call(s32[5]{0:T(128)S(1)} %stack.31.info_ref, bf16[1344,128]{1,0:T(8,128)(2,1)S(1)} %shard_map.131.own.both_ref, bf16[1344,128]{1,0:T(8,128)(2,1)S(1)} %collective-permute-done.2.one, ...), custom_call_target="tpu_custom_call" | custom-call | bytes 13200000 | tf_op jit(solution)/shard_map/pallas_call | solution.py:358
  65.6 8.3 %collective-permute-start.6 = (bf16[128,512]{1,0:T(8,128)(2,1)S(1)}, bf16[128,512]{1,0:T(8,128)(2,1)S(1)}, u32[]{:S(2)}, u32[]{:S(2)}) collective-permute-start(bf16[128,512]{1,0:T(8,128)(2,1)S(1)} %get-tuple-element.25.kv_ref.own), channel_id=1, source_target_pairs={{0,16},{4,20},{8,24},{12,28},{16,32},{20,36},{24,40},{28,44},{32,4... | collective-permute-start | bytes 393224 | tf_op jit(solution)/shard_map/ppermute | solution.py:278
  73.9 10.7 %collective-permute-start.5 = (bf16[128,512]{1,0:T(8,128)(2,1)S(1)}, bf16[128,512]{1,0:T(8,128)(2,1)S(1)}, u32[]{:S(2)}, u32[]{:S(2)}) collective-permute-start(bf16[128,512]{1,0:T(8,128)(2,1)S(1)} %get-tuple-element.25.kv_ref.own), channel_id=1, source_target_pairs={{0,8},{4,12},{8,16},{12,20},{16,24},{20,28},{24,32},{28,36},{32,40... | collective-permute-start | bytes 393224 | tf_op jit(solution)/shard_map/ppermute | solution.py:278
  84.7 3.1 %shard_map.138 = (bf16[128,512]{1,0:T(8,128)(2,1)S(1)}, f32[128,512]{1,0:T(8,128)S(1)}, f32[128,512]{1,0:T(8,128)S(1)}, f32[128,512]{1,0:T(8,128)S(1)}, bf16[256,512]{1,0:T(8,128)(2,1)S(1)}) custom-call(s32[5]{0:T(128)S(1)} %stack.31.info_ref, s32[32,128]{1,0:T(8,128)S(1)} %bitcast.50, bf16[128,512]{1,0:T(8,128)(2,1)S(1)} %get-tuple-element.30.q_ref, ...), custom_call_target="tpu_custom_call" | custom-call | bytes 13200000 | tf_op jit(solution)/shard_map/pallas_call | solution.py:366
  87.8 1.9 %collective-permute-start.19 = (bf16[256,512]{1,0:T(8,128)(2,1)S(1)}, bf16[256,512]{1,0:T(8,128)(2,1)S(1)}, u32[]{:S(2)}, u32[]{:S(2)}) collective-permute-start(bf16[256,512]{1,0:T(8,128)(2,1)S(1)} %get-tuple-element.37), channel_id=1, source_target_pairs={{0,4},{4,0},{8,12},{12,8},{16,20},{20,16},{24,28},{28,24},{32,36},... | collective-permute-start | bytes 786440 | tf_op jit(solution)/shard_map/ppermute | solution.py:283
  90.3 2.4 %collective-permute-start.7 = (bf16[128,512]{1,0:T(8,128)(2,1)S(1)}, bf16[128,512]{1,0:T(8,128)(2,1)S(1)}, u32[]{:S(2)}, u32[]{:S(2)}) collective-permute-start(bf16[128,512]{1,0:T(8,128)(2,1)S(1)} %shard_map.133), channel_id=1, source_target_pairs={{0,4},{4,0},{8,12},{12,8},{16,20},{20,16},{24,28},{28,24},{32,36},... | collective-permute-start | bytes 393224 | tf_op jit(solution)/shard_map/ppermute | solution.py:283
  94.3 1.9 %collective-permute-start.8 = (bf16[128,512]{1,0:T(8,128)(2,1)S(1)}, bf16[128,512]{1,0:T(8,128)(2,1)S(1)}, u32[]{:S(2)}, u32[]{:S(2)}) collective-permute-start(bf16[128,512]{1,0:T(8,128)(2,1)S(1)} %collective-permute-done.5.two), channel_id=1, source_target_pairs={{0,4},{4,0},{8,12},{12,8},{16,20},{20,16},{24,28},{28,24},{32,36},... | collective-permute-start | bytes 393224 | tf_op jit(solution)/shard_map/ppermute | solution.py:283
  97.5 2.9 %shard_map.134 = (bf16[672,128]{1,0:T(8,128)(2,1)S(1)}, bf16[672,128]{1,0:T(8,128)(2,1)S(1)}, bf16[672,128]{1,0:T(8,128)(2,1)S(1)}, bf16[672,128]{1,0:T(8,128)(2,1)S(1)}) custom-call(s32[5]{0:T(128)S(1)} %stack.31.info_ref, s32[32,128]{1,0:T(8,128)S(1)} %bitcast.51, bf16[128,512]{1,0:T(8,128)(2,1)S(1)} %get-tuple-element.24.q_ref, ...), custom_call_target="tpu_custom_call" | custom-call | bytes 13200000 | tf_op jit(solution)/shard_map/pallas_call | solution.py:379
  100.5 1.9 %collective-permute-start.9 = (bf16[672,128]{1,0:T(8,128)(2,1)S(1)}, bf16[672,128]{1,0:T(8,128)(2,1)S(1)}, u32[]{:S(2)}, u32[]{:S(2)}) collective-permute-start(bf16[672,128]{1,0:T(8,128)(2,1)S(1)} %get-tuple-element.27), channel_id=1, source_target_pairs={{0,1},{1,2},{2,3},{3,0},{4,5},{5,6},{6,7},{7,4},{8,9},{9,10},{10,1... | collective-permute-start | bytes 516104 | tf_op jit(solution)/shard_map/ppermute | solution.py:297
  103.0 7.1 %collective-permute-start.20 = (bf16[128,512]{1,0:T(8,128)(2,1)S(1)}, bf16[128,512]{1,0:T(8,128)(2,1)S(1)}, u32[]{:S(2)}, u32[]{:S(2)}) collective-permute-start(bf16[128,512]{1,0:T(8,128)(2,1)S(1)} %get-tuple-element.39), channel_id=1, source_target_pairs={{8,0},{12,4},{16,8},{20,12},{24,16},{28,20},{32,24},{36,28},{40,32... | collective-permute-start | bytes 393224 | tf_op jit(solution)/shard_map/ppermute | solution.py:278
  110.2 3.4 %collective-permute-start.21 = (bf16[128,512]{1,0:T(8,128)(2,1)S(1)}, bf16[128,512]{1,0:T(8,128)(2,1)S(1)}, u32[]{:S(2)}, u32[]{:S(2)}) collective-permute-start(bf16[128,512]{1,0:T(8,128)(2,1)S(1)} %get-tuple-element.40), channel_id=1, source_target_pairs={{16,0},{20,4},{24,8},{28,12},{32,16},{36,20},{40,24},{44,28},{48,3... | collective-permute-start | bytes 393224 | tf_op jit(solution)/shard_map/ppermute | solution.py:278
  113.6 8.4 %collective-permute-done.20.two_ref = bf16[128,512]{1,0:T(8,128)(2,1)S(1)} collective-permute-done((bf16[128,512]{1,0:T(8,128)(2,1)S(1)}, bf16[128,512]{1,0:T(8,128)(2,1)S(1)}, u32[]{:S(2)}, u32[]{:S(2)}) %collective-permute-start.20) | collective-permute-done | bytes 131104 | tf_op jit(solution)/shard_map/ppermute | solution.py:278
  122.0 2.1 %shard_map.140 = (bf16[688,128]{1,0:T(8,128)(2,1)S(1)}, bf16[688,128]{1,0:T(8,128)(2,1)S(1)}, bf16[688,128]{1,0:T(8,128)(2,1)S(1)}, bf16[688,128]{1,0:T(8,128)(2,1)S(1)}) custom-call(s32[5]{0:T(128)S(1)} %stack.31.info_ref, bf16[128,512]{1,0:T(8,128)(2,1)S(1)} %get-tuple-element.33.dq_ref, f32[128,512]{1,0:T(8,128)S(1)} %get-tuple-element.38.own_ref, ...), custom_call_target="tpu_custom_call" | custom-call | bytes 13200000 | tf_op jit(solution)/shard_map/pallas_call | solution.py:388
  124.2 4.0 %collective-permute-start.22 = (bf16[688,128]{1,0:T(8,128)(2,1)S(1)}, bf16[688,128]{1,0:T(8,128)(2,1)S(1)}, u32[]{:S(2)}, u32[]{:S(2)}) collective-permute-start(bf16[688,128]{1,0:T(8,128)(2,1)S(1)} %get-tuple-element.42), channel_id=1, source_target_pairs={{0,1},{1,2},{2,3},{3,0},{4,5},{5,6},{6,7},{7,4},{8,9},{9,10},{10,1... | collective-permute-start | bytes 528392 | tf_op jit(solution)/shard_map/ppermute | solution.py:297
  128.2 3.0 %collective-permute-start.23 = (bf16[688,128]{1,0:T(8,128)(2,1)S(1)}, bf16[688,128]{1,0:T(8,128)(2,1)S(1)}, u32[]{:S(2)}, u32[]{:S(2)}) collective-permute-start(bf16[688,128]{1,0:T(8,128)(2,1)S(1)} %get-tuple-element.43), channel_id=1, source_target_pairs={{0,3},{1,0},{2,1},{3,2},{4,7},{5,4},{6,5},{7,6},{8,11},{9,8},{10,9... | collective-permute-start | bytes 528392 | tf_op jit(solution)/shard_map/ppermute | solution.py:297
  131.2 2.9 %collective-permute-start.24 = (bf16[688,128]{1,0:T(8,128)(2,1)S(1)}, bf16[688,128]{1,0:T(8,128)(2,1)S(1)}, u32[]{:S(2)}, u32[]{:S(2)}) collective-permute-start(bf16[688,128]{1,0:T(8,128)(2,1)S(1)} %get-tuple-element.44), channel_id=1, source_target_pairs={{0,2},{1,3},{2,0},{3,1},{4,6},{5,7},{6,4},{7,5},{8,10},{9,11},{10,... | collective-permute-start | bytes 528392 | tf_op jit(solution)/shard_map/ppermute | solution.py:297
  134.1 4.5 %collective-permute-start.10 = (bf16[672,128]{1,0:T(8,128)(2,1)S(1)}, bf16[672,128]{1,0:T(8,128)(2,1)S(1)}, u32[]{:S(2)}, u32[]{:S(2)}) collective-permute-start(bf16[672,128]{1,0:T(8,128)(2,1)S(1)} %get-tuple-element.28), channel_id=1, source_target_pairs={{0,3},{1,0},{2,1},{3,2},{4,7},{5,4},{6,5},{7,6},{8,11},{9,8},{10,9... | collective-permute-start | bytes 516104 | tf_op jit(solution)/shard_map/ppermute | solution.py:297
  138.7 2.1 %collective-permute-start.11 = (bf16[672,128]{1,0:T(8,128)(2,1)S(1)}, bf16[672,128]{1,0:T(8,128)(2,1)S(1)}, u32[]{:S(2)}, u32[]{:S(2)}) collective-permute-start(bf16[672,128]{1,0:T(8,128)(2,1)S(1)} %get-tuple-element.29), channel_id=1, source_target_pairs={{0,2},{1,3},{2,0},{3,1},{4,6},{5,7},{6,4},{7,5},{8,10},{9,11},{10,... | collective-permute-start | bytes 516104 | tf_op jit(solution)/shard_map/ppermute | solution.py:297
  141.7 3.2 %collective-permute-done.10.minus = bf16[672,128]{1,0:T(8,128)(2,1)S(1)} collective-permute-done((bf16[672,128]{1,0:T(8,128)(2,1)S(1)}, bf16[672,128]{1,0:T(8,128)(2,1)S(1)}, u32[]{:S(2)}, u32[]{:S(2)}) %collective-permute-start.10) | collective-permute-done | bytes 172064 | tf_op jit(solution)/shard_map/ppermute | solution.py:297
  144.9 2.7 %collective-permute-done.11.far = bf16[672,128]{1,0:T(8,128)(2,1)S(1)} collective-permute-done((bf16[672,128]{1,0:T(8,128)(2,1)S(1)}, bf16[672,128]{1,0:T(8,128)(2,1)S(1)}, u32[]{:S(2)}, u32[]{:S(2)}) %collective-permute-start.11) | collective-permute-done | bytes 172064 | tf_op jit(solution)/shard_map/ppermute | solution.py:297
  (65 shorter events, 21.3 us)
Async XLA Ops:
  0.6 17.1 %collective-permute-start = (bf16[672,128]{1,0:T(8,128)(2,1)}, bf16[672,128]{1,0:T(8,128)(2,1)S(1)}, u32[]{:S(2)}, u32[]{:S(2)}) collective-permute-start(bf16[672,128]{1,0:T(8,128)(2,1)} %bitcast.54), channel_id=1, source_target_pairs={{0,128},{128,256},{256,384},{384,512},{512,640},{1,129},{129,257},... | collective-permute-start | bytes 516104 | tf_op jit(solution)/shard_map/ppermute | solution.py:289
  4.9 12.8 %collective-permute-start.1 = (bf16[672,128]{1,0:T(8,128)(2,1)}, bf16[672,128]{1,0:T(8,128)(2,1)S(1)}, u32[]{:S(2)}, u32[]{:S(2)}) collective-permute-start(bf16[672,128]{1,0:T(8,128)(2,1)} %bitcast.55), channel_id=1, source_target_pairs={{128,0},{256,128},{384,256},{512,384},{640,512},{129,1},{257,129},... | collective-permute-start | bytes 516104 | tf_op jit(solution)/shard_map/ppermute | solution.py:289
  6.8 20.5 %collective-permute-start.12 = (bf16[672,128]{1,0:T(8,128)(2,1)}, bf16[672,128]{1,0:T(8,128)(2,1)S(1)}, u32[]{:S(2)}, u32[]{:S(2)}) collective-permute-start(bf16[672,128]{1,0:T(8,128)(2,1)} %bitcast.43), channel_id=1, source_target_pairs={{0,1},{1,2},{2,3},{3,0},{4,5},{5,6},{6,7},{7,4},{8,9},{9,10},{10,1... | collective-permute-start | bytes 516104 | tf_op jit(solution)/shard_map/ppermute | solution.py:297
  10.3 19.5 %collective-permute-start.13 = (bf16[672,128]{1,0:T(8,128)(2,1)}, bf16[672,128]{1,0:T(8,128)(2,1)S(1)}, u32[]{:S(2)}, u32[]{:S(2)}) collective-permute-start(bf16[672,128]{1,0:T(8,128)(2,1)} %bitcast.44), channel_id=1, source_target_pairs={{0,3},{1,0},{2,1},{3,2},{4,7},{5,4},{6,5},{7,6},{8,11},{9,8},{10,9... | collective-permute-start | bytes 516104 | tf_op jit(solution)/shard_map/ppermute | solution.py:297
  13.9 15.8 %collective-permute-start.14 = (bf16[672,128]{1,0:T(8,128)(2,1)}, bf16[672,128]{1,0:T(8,128)(2,1)S(1)}, u32[]{:S(2)}, u32[]{:S(2)}) collective-permute-start(bf16[672,128]{1,0:T(8,128)(2,1)} %bitcast.45), channel_id=1, source_target_pairs={{0,2},{1,3},{2,0},{3,1},{4,6},{5,7},{6,4},{7,5},{8,10},{9,11},{10,... | collective-permute-start | bytes 516104 | tf_op jit(solution)/shard_map/ppermute | solution.py:297
  20.2 40.0 %collective-permute-start.2 = (bf16[1344,128]{1,0:T(8,128)(2,1)S(1)}, bf16[1344,128]{1,0:T(8,128)(2,1)S(1)}, u32[]{:S(2)}, u32[]{:S(2)}) collective-permute-start(bf16[1344,128]{1,0:T(8,128)(2,1)S(1)} %shard_map.131.own.both_ref), channel_id=1, source_target_pairs={{0,1},{1,2},{2,3},{3,0},{4,5},{5,6},{6,7},{7,4},{8,9},{9,10},{10,1... | collective-permute-start | bytes 1032200 | tf_op jit(solution)/shard_map/ppermute | solution.py:297
  22.8 37.5 %collective-permute-start.3 = (bf16[1344,128]{1,0:T(8,128)(2,1)S(1)}, bf16[1344,128]{1,0:T(8,128)(2,1)S(1)}, u32[]{:S(2)}, u32[]{:S(2)}) collective-permute-start(bf16[1344,128]{1,0:T(8,128)(2,1)S(1)} %shard_map.131.own.both_ref), channel_id=1, source_target_pairs={{0,3},{1,0},{2,1},{3,2},{4,7},{5,4},{6,5},{7,6},{8,11},{9,8},{10,9... | collective-permute-start | bytes 1032200 | tf_op jit(solution)/shard_map/ppermute | solution.py:297
  27.3 32.9 %collective-permute-start.4 = (bf16[1344,128]{1,0:T(8,128)(2,1)S(1)}, bf16[1344,128]{1,0:T(8,128)(2,1)S(1)}, u32[]{:S(2)}, u32[]{:S(2)}) collective-permute-start(bf16[1344,128]{1,0:T(8,128)(2,1)S(1)} %shard_map.131.own.both_ref), channel_id=1, source_target_pairs={{0,2},{1,3},{2,0},{3,1},{4,6},{5,7},{6,4},{7,5},{8,10},{9,11},{10,... | collective-permute-start | bytes 1032200 | tf_op jit(solution)/shard_map/ppermute | solution.py:297
  35.8 24.4 %copy-start.1 = (bf16[1,2688,512]{2,1,0:T(8,128)(2,1)S(1)}, bf16[1,2688,512]{2,1,0:T(8,128)(2,1)}, u32[]{:S(2)}) copy-start(bf16[1,2688,512]{2,1,0:T(8,128)(2,1)} %param.18) | copy-start | bytes 8257540
  35.9 24.4 %copy-start.2 = (bf16[1,512,2688]{2,1,0:T(8,128)(2,1)S(1)}, bf16[1,512,2688]{2,1,0:T(8,128)(2,1)}, u32[]{:S(2)}) copy-start(bf16[1,512,2688]{2,1,0:T(8,128)(2,1)} %param.21) | copy-start | bytes 8257540
  35.9 24.4 %copy-start.14 = (f32[1,2688]{1,0:T(1,128)S(1)}, f32[1,2688]{1,0:T(1,128)}, u32[]{:S(2)}) copy-start(f32[1,2688]{1,0:T(1,128)} %gain_ref.5) | copy-start | bytes 32260
  37.7 17.4 %collective-permute-start.16 = (bf16[128,512]{1,0:T(8,128)(2,1)S(1)}, bf16[128,512]{1,0:T(8,128)(2,1)S(1)}, u32[]{:S(2)}, u32[]{:S(2)}) collective-permute-start(bf16[128,512]{1,0:T(8,128)(2,1)S(1)} %get-tuple-element.32.kv_ref.own), channel_id=1, source_target_pairs={{0,16},{4,20},{8,24},{12,28},{16,32},{20,36},{24,40},{28,44},{32,4... | collective-permute-start | bytes 393224 | tf_op jit(solution)/shard_map/ppermute | solution.py:278
  41.2 17.0 %collective-permute-start.15 = (bf16[128,512]{1,0:T(8,128)(2,1)S(1)}, bf16[128,512]{1,0:T(8,128)(2,1)S(1)}, u32[]{:S(2)}, u32[]{:S(2)}) collective-permute-start(bf16[128,512]{1,0:T(8,128)(2,1)S(1)} %get-tuple-element.32.kv_ref.own), channel_id=1, source_target_pairs={{0,8},{4,12},{8,16},{12,20},{16,24},{20,28},{24,32},{28,36},{32,40... | collective-permute-start | bytes 393224 | tf_op jit(solution)/shard_map/ppermute | solution.py:278
  55.7 28.9 %collective-permute-start.17 = (bf16[128,512]{1,0:T(8,128)(2,1)S(1)}, bf16[128,512]{1,0:T(8,128)(2,1)S(1)}, u32[]{:S(2)}, u32[]{:S(2)}) collective-permute-start(bf16[128,512]{1,0:T(8,128)(2,1)S(1)} %shard_map.137), channel_id=1, source_target_pairs={{0,4},{4,0},{8,12},{12,8},{16,20},{20,16},{24,28},{28,24},{32,36},... | collective-permute-start | bytes 393224 | tf_op jit(solution)/shard_map/ppermute | solution.py:283
  58.3 26.3 %collective-permute-start.18 = (bf16[128,512]{1,0:T(8,128)(2,1)S(1)}, bf16[128,512]{1,0:T(8,128)(2,1)S(1)}, u32[]{:S(2)}, u32[]{:S(2)}) collective-permute-start(bf16[128,512]{1,0:T(8,128)(2,1)S(1)} %collective-permute-done.15.two), channel_id=1, source_target_pairs={{0,4},{4,0},{8,12},{12,8},{16,20},{20,16},{24,28},{28,24},{32,36},... | collective-permute-start | bytes 393224 | tf_op jit(solution)/shard_map/ppermute | solution.py:283
  62.9 21.7 %copy-start.15 = (s32[1,4096]{1,0:T(1,128)S(1)}, s32[1,4096]{1,0:T(1,128)}, u32[]{:S(2)}) copy-start(s32[1,4096]{1,0:T(1,128)} %param.23) | copy-start | bytes 49156
  62.9 34.6 %copy-start.16 = (s32[1,4096]{1,0:T(1,128)S(1)}, s32[1,4096]{1,0:T(1,128)}, u32[]{:S(2)}) copy-start(s32[1,4096]{1,0:T(1,128)} %param.22) | copy-start | bytes 49156
  65.6 24.0 %collective-permute-start.6 = (bf16[128,512]{1,0:T(8,128)(2,1)S(1)}, bf16[128,512]{1,0:T(8,128)(2,1)S(1)}, u32[]{:S(2)}, u32[]{:S(2)}) collective-permute-start(bf16[128,512]{1,0:T(8,128)(2,1)S(1)} %get-tuple-element.25.kv_ref.own), channel_id=1, source_target_pairs={{0,16},{4,20},{8,24},{12,28},{16,32},{20,36},{24,40},{28,44},{32,4... | collective-permute-start | bytes 393224 | tf_op jit(solution)/shard_map/ppermute | solution.py:278
  73.9 20.4 %collective-permute-start.5 = (bf16[128,512]{1,0:T(8,128)(2,1)S(1)}, bf16[128,512]{1,0:T(8,128)(2,1)S(1)}, u32[]{:S(2)}, u32[]{:S(2)}) collective-permute-start(bf16[128,512]{1,0:T(8,128)(2,1)S(1)} %get-tuple-element.25.kv_ref.own), channel_id=1, source_target_pairs={{0,8},{4,12},{8,16},{12,20},{16,24},{20,28},{24,32},{28,36},{32,40... | collective-permute-start | bytes 393224 | tf_op jit(solution)/shard_map/ppermute | solution.py:278
  84.6 37.4 %copy-start.5 = (bf16[1,2688,256]{2,1,0:T(8,128)(2,1)S(1)}, bf16[1,2688,256]{2,1,0:T(8,128)(2,1)}, u32[]{:S(2)}) copy-start(bf16[1,2688,256]{2,1,0:T(8,128)(2,1)} %param.19) | copy-start | bytes 4128772
  84.6 37.4 %copy-start.8 = (bf16[1,2688,256]{2,1,0:T(8,128)(2,1)S(1)}, bf16[1,2688,256]{2,1,0:T(8,128)(2,1)}, u32[]{:S(2)}) copy-start(bf16[1,2688,256]{2,1,0:T(8,128)(2,1)} %param.20) | copy-start | bytes 4128772
  87.8 14.7 %collective-permute-start.19 = (bf16[256,512]{1,0:T(8,128)(2,1)S(1)}, bf16[256,512]{1,0:T(8,128)(2,1)S(1)}, u32[]{:S(2)}, u32[]{:S(2)}) collective-permute-start(bf16[256,512]{1,0:T(8,128)(2,1)S(1)} %get-tuple-element.37), channel_id=1, source_target_pairs={{0,4},{4,0},{8,12},{12,8},{16,20},{20,16},{24,28},{28,24},{32,36},... | collective-permute-start | bytes 786440 | tf_op jit(solution)/shard_map/ppermute | solution.py:283
  90.3 6.0 %collective-permute-start.7 = (bf16[128,512]{1,0:T(8,128)(2,1)S(1)}, bf16[128,512]{1,0:T(8,128)(2,1)S(1)}, u32[]{:S(2)}, u32[]{:S(2)}) collective-permute-start(bf16[128,512]{1,0:T(8,128)(2,1)S(1)} %shard_map.133), channel_id=1, source_target_pairs={{0,4},{4,0},{8,12},{12,8},{16,20},{20,16},{24,28},{28,24},{32,36},... | collective-permute-start | bytes 393224 | tf_op jit(solution)/shard_map/ppermute | solution.py:283
  94.3 3.2 %collective-permute-start.8 = (bf16[128,512]{1,0:T(8,128)(2,1)S(1)}, bf16[128,512]{1,0:T(8,128)(2,1)S(1)}, u32[]{:S(2)}, u32[]{:S(2)}) collective-permute-start(bf16[128,512]{1,0:T(8,128)(2,1)S(1)} %collective-permute-done.5.two), channel_id=1, source_target_pairs={{0,4},{4,0},{8,12},{12,8},{16,20},{20,16},{24,28},{28,24},{32,36},... | collective-permute-start | bytes 393224 | tf_op jit(solution)/shard_map/ppermute | solution.py:283
  100.5 38.2 %collective-permute-start.9 = (bf16[672,128]{1,0:T(8,128)(2,1)S(1)}, bf16[672,128]{1,0:T(8,128)(2,1)S(1)}, u32[]{:S(2)}, u32[]{:S(2)}) collective-permute-start(bf16[672,128]{1,0:T(8,128)(2,1)S(1)} %get-tuple-element.27), channel_id=1, source_target_pairs={{0,1},{1,2},{2,3},{3,0},{4,5},{5,6},{6,7},{7,4},{8,9},{9,10},{10,1... | collective-permute-start | bytes 516104 | tf_op jit(solution)/shard_map/ppermute | solution.py:297
  103.0 19.0 %collective-permute-start.20 = (bf16[128,512]{1,0:T(8,128)(2,1)S(1)}, bf16[128,512]{1,0:T(8,128)(2,1)S(1)}, u32[]{:S(2)}, u32[]{:S(2)}) collective-permute-start(bf16[128,512]{1,0:T(8,128)(2,1)S(1)} %get-tuple-element.39), channel_id=1, source_target_pairs={{8,0},{12,4},{16,8},{20,12},{24,16},{28,20},{32,24},{36,28},{40,32... | collective-permute-start | bytes 393224 | tf_op jit(solution)/shard_map/ppermute | solution.py:278
  110.2 11.8 %collective-permute-start.21 = (bf16[128,512]{1,0:T(8,128)(2,1)S(1)}, bf16[128,512]{1,0:T(8,128)(2,1)S(1)}, u32[]{:S(2)}, u32[]{:S(2)}) collective-permute-start(bf16[128,512]{1,0:T(8,128)(2,1)S(1)} %get-tuple-element.40), channel_id=1, source_target_pairs={{16,0},{20,4},{24,8},{28,12},{32,16},{36,20},{40,24},{44,28},{48,3... | collective-permute-start | bytes 393224 | tf_op jit(solution)/shard_map/ppermute | solution.py:278
  124.2 24.2 %collective-permute-start.22 = (bf16[688,128]{1,0:T(8,128)(2,1)S(1)}, bf16[688,128]{1,0:T(8,128)(2,1)S(1)}, u32[]{:S(2)}, u32[]{:S(2)}) collective-permute-start(bf16[688,128]{1,0:T(8,128)(2,1)S(1)} %get-tuple-element.42), channel_id=1, source_target_pairs={{0,1},{1,2},{2,3},{3,0},{4,5},{5,6},{6,7},{7,4},{8,9},{9,10},{10,1... | collective-permute-start | bytes 528392 | tf_op jit(solution)/shard_map/ppermute | solution.py:297
  128.2 20.2 %collective-permute-start.23 = (bf16[688,128]{1,0:T(8,128)(2,1)S(1)}, bf16[688,128]{1,0:T(8,128)(2,1)S(1)}, u32[]{:S(2)}, u32[]{:S(2)}) collective-permute-start(bf16[688,128]{1,0:T(8,128)(2,1)S(1)} %get-tuple-element.43), channel_id=1, source_target_pairs={{0,3},{1,0},{2,1},{3,2},{4,7},{5,4},{6,5},{7,6},{8,11},{9,8},{10,9... | collective-permute-start | bytes 528392 | tf_op jit(solution)/shard_map/ppermute | solution.py:297
  131.2 17.2 %collective-permute-start.24 = (bf16[688,128]{1,0:T(8,128)(2,1)S(1)}, bf16[688,128]{1,0:T(8,128)(2,1)S(1)}, u32[]{:S(2)}, u32[]{:S(2)}) collective-permute-start(bf16[688,128]{1,0:T(8,128)(2,1)S(1)} %get-tuple-element.44), channel_id=1, source_target_pairs={{0,2},{1,3},{2,0},{3,1},{4,6},{5,7},{6,4},{7,5},{8,10},{9,11},{10,... | collective-permute-start | bytes 528392 | tf_op jit(solution)/shard_map/ppermute | solution.py:297
  134.1 10.8 %collective-permute-start.10 = (bf16[672,128]{1,0:T(8,128)(2,1)S(1)}, bf16[672,128]{1,0:T(8,128)(2,1)S(1)}, u32[]{:S(2)}, u32[]{:S(2)}) collective-permute-start(bf16[672,128]{1,0:T(8,128)(2,1)S(1)} %get-tuple-element.28), channel_id=1, source_target_pairs={{0,3},{1,0},{2,1},{3,2},{4,7},{5,4},{6,5},{7,6},{8,11},{9,8},{10,9... | collective-permute-start | bytes 516104 | tf_op jit(solution)/shard_map/ppermute | solution.py:297
  138.7 8.9 %collective-permute-start.11 = (bf16[672,128]{1,0:T(8,128)(2,1)S(1)}, bf16[672,128]{1,0:T(8,128)(2,1)S(1)}, u32[]{:S(2)}, u32[]{:S(2)}) collective-permute-start(bf16[672,128]{1,0:T(8,128)(2,1)S(1)} %get-tuple-element.29), channel_id=1, source_target_pairs={{0,2},{1,3},{2,0},{3,1},{4,6},{5,7},{6,4},{7,5},{8,10},{9,11},{10,... | collective-permute-start | bytes 516104 | tf_op jit(solution)/shard_map/ppermute | solution.py:297
  (10 other events, 20.3 us)

commit v3 on v2

--- a/solution.py
+++ b/solution.py
@@ -88,12 +88,13 @@
         hold_ref[lax.rem(place + offset, parts)] = piece[...]
 
 
-def project_back_body(
-    info_ref, own, one, minus, far, gain_ref, wk_ref, wv_ref, wq_ref,
-    q_ref, kv_ref, r_ref, hold_ref,
-):
-    placed_parts(info_ref, own, one, minus, far, hold_ref)
-    h, factor = normal_rows(stacked(hold_ref, 0, hold_ref.shape[1]), gain_ref)
+def spread_body(x_ref, out_ref):
+    for part in range(out_ref.shape[0]):
+        out_ref[part] = x_ref[...]
+
+
+def project_back_body(x_ref, gain_ref, wk_ref, wv_ref, wq_ref, q_ref, kv_ref, r_ref):
+    h, factor = normal_rows(stacked(x_ref, 0, x_ref.shape[1]), gain_ref)
     r_ref[...] = jnp.broadcast_to(factor, r_ref.shape)
     project_rows(h, wk_ref, wv_ref, wq_ref, q_ref, kv_ref)
 
@@ -110,7 +111,7 @@
     da_ref[...] = jnp.transpose(grad.astype(BF))
 
 
-def touch_body(info_ref, gain_ref, wk_ref, wv_ref, wq_ref, wo_ref, out_ref, hold_ref):
+def touch_body(info_ref, gain_ref, out_ref, hold_ref):
     share, length = out_ref.shape
     hold_ref[...] = jnp.transpose(jnp.broadcast_to(gain_ref[...], (length, gain_ref.shape[1])))
     out_ref[...] = hold_ref[pl.ds(pl.multiple_of(info_ref[2] * share, 32), share), :]
@@ -335,24 +336,29 @@
     def pieces(count):
         return pltpu.VMEM((parts, count, length), BF)
 
-    stash = stashed[0].T
-    arrived = next_section(sent_forward[0].T, 1)
-    returned = next_section(sent_backward[0].T, -1)
-    gathered = exchanged((stash,) * 3)
+    stash, ahead, behind, info = lax.optimization_barrier(
+        (stashed[0].T, sent_forward[0].T, sent_backward[0].T, info)
+    )
+    arrived = next_section(ahead, 1)
+    returned = next_section(behind, -1)
+    spread = kernel(
+        spread_body, 4, jax.ShapeDtypeStruct((parts, share, length), BF), vmem(1), 1.0
+    )(stash)
+    gathered = lax.all_to_all(spread, "fsdp", 0, 0)
     own_gain = kernel(
-        touch_body, LIMIT, rows(share, length, F32), [smem()] + vmem(5),
+        touch_body, LIMIT, rows(share, length, F32), [smem()] + vmem(1),
         scratch=[pltpu.VMEM((parts * share, length), F32)],
-    )(info, gain, wk, wv, wq, wo)
+    )(info, gain)
 
     q_back, kv_back, factor = kernel(
         project_back_body, LIMIT,
         (rows(length, q_cols), rows(length, kv_cols), rows(length, length, F32)),
-        [smem()] + vmem(8), scratch=[pieces(share)],
-    )(info, stash, *gathered, gain, wk, wv, wq)
+        vmem(5),
+    )(gathered, gain, wk, wv, wq)
     blocks_back = window_blocks(info, kv_back)
 
     sent = kernel(
-        choose_body, LIMIT, rows(2 * share, length), [smem()] + vmem(4), 1.0,
+        choose_body, LIMIT, rows(2 * share, length), [smem()] + vmem(4), 20.0,
     )(info, embedded.T, arrived, loss_grad.T, returned)
     both = exchanged((sent,) * 3)
     q_front, kv_front, d_attn = kernel(

time: 150 us -> 147 us (0.980)
  the two profiles are of different devices: /device:TPU:80 before, /device:TPU:16 now
where the time goes in v3:
time: 147 us; the launch traced here: 146 us
  starting transfers between devices  90.8 us (62%)
  waiting for transfers between devices  27.5 us (19%)
  Pallas kernels  20 us (14%)
  local copies, waits for them, and re-layouts  6.4 us (4%)
    ppermute x6, starting transfers between devices, shifted(): return lax.ppermute(value, 'seq', pairs)  39.8 us
    ppermute x9, starting transfers between devices, exchanged(): received.append(lax.ppermute(value, 'fsdp', pairs))  31 us
    ppermute x6, waiting for transfers between devices, shifted(): return lax.ppermute(value, 'seq', pairs)  13.1 us
    ppermute x5, starting transfers between devices, swapped(): return lax.ppermute(value, 'seq', [(s, s ^ 1) for s in range(count)])  10.1 us
    ppermute x2, waiting for transfers between devices, next_section(): return lax.ppermute(value, 'pipe', pairs)  7.18 us
    unnamed x28, local copies, waits for them, and re-layouts  6.32 us
    ppermute x9, waiting for transfers between devices, exchanged(): received.append(lax.ppermute(value, 'fsdp', pairs))  5.89 us
    ppermute x2, starting transfers between devices, next_section(): return lax.ppermute(value, 'pipe', pairs)  5.57 us
  transfers between devices with their start and end apart: 23, of which 8 were waited for; matrix products, arithmetic and copies ran while one was open for 0% of the time, Pallas kernels for 12%

profile of v3, /device:TPU:16, one launch (start us, length us, event | category | flops | bytes accessed | tf_op | source)
XLA Modules:
  0.0 145.7 jit_solution(15602814346139526402)
XLA Ops:
  2.8 4.3 %all-to-all-start = ((bf16[4,672,128]{2,1,0:T(8,128)(2,1)}), bf16[4,672,128]{2,1,0:T(8,128)(2,1)}, u32[]{:S(2)}, u32[]{:S(2)}) async-start(bf16[4,672,128]{2,1,0:T(8,128)(2,1)} %shard_map.136), calls=%async_computation | async-start | bytes 1376256 | tf_op jit(solution)/shard_map/all_to_all | solution.py:347
  7.1 4.3 %collective-permute-start = (bf16[672,128]{1,0:T(8,128)(2,1)}, bf16[672,128]{1,0:T(8,128)(2,1)S(1)}, u32[]{:S(2)}, u32[]{:S(2)}) collective-permute-start(bf16[672,128]{1,0:T(8,128)(2,1)} %bitcast.47), channel_id=1, source_target_pairs={{0,128},{128,256},{256,384},{384,512},{512,640},{1,129},{129,257},... | collective-permute-start | bytes 516104 | tf_op jit(solution)/shard_map/ppermute | solution.py:290
  12.7 2.5 %collective-permute-done.arr_ref = bf16[672,128]{1,0:T(8,128)(2,1)S(1)} collective-permute-done((bf16[672,128]{1,0:T(8,128)(2,1)}, bf16[672,128]{1,0:T(8,128)(2,1)S(1)}, u32[]{:S(2)}, u32[]{:S(2)}) %collective-permute-start) | collective-permute-done | bytes 172064 | tf_op jit(solution)/shard_map/ppermute | solution.py:290
  15.2 4.7 %collective-permute-done.1.ret_ref = bf16[672,128]{1,0:T(8,128)(2,1)S(1)} collective-permute-done((bf16[672,128]{1,0:T(8,128)(2,1)}, bf16[672,128]{1,0:T(8,128)(2,1)S(1)}, u32[]{:S(2)}, u32[]{:S(2)}) %collective-permute-start.1) | collective-permute-done | bytes 172064 | tf_op jit(solution)/shard_map/ppermute | solution.py:290
  22.3 3.6 %collective-permute-start.2 = (bf16[1344,128]{1,0:T(8,128)(2,1)S(1)}, bf16[1344,128]{1,0:T(8,128)(2,1)S(1)}, u32[]{:S(2)}, u32[]{:S(2)}) collective-permute-start(bf16[1344,128]{1,0:T(8,128)(2,1)S(1)} %shard_map.131.own.both_ref), channel_id=1, source_target_pairs={{0,1},{1,2},{2,3},{3,0},{4,5},{5,6},{6,7},{7,4},{8,9},{9,10},{10,1... | collective-permute-start | bytes 1032200 | tf_op jit(solution)/shard_map/ppermute | solution.py:298
  25.9 3.5 %collective-permute-start.3 = (bf16[1344,128]{1,0:T(8,128)(2,1)S(1)}, bf16[1344,128]{1,0:T(8,128)(2,1)}, u32[]{:S(2)}, u32[]{:S(2)}) collective-permute-start(bf16[1344,128]{1,0:T(8,128)(2,1)S(1)} %shard_map.131.own.both_ref), channel_id=1, source_target_pairs={{0,3},{1,0},{2,1},{3,2},{4,7},{5,4},{6,5},{7,6},{8,11},{9,8},{10,9... | collective-permute-start | bytes 1032200 | tf_op jit(solution)/shard_map/ppermute | solution.py:298
  29.4 3.9 %collective-permute-start.4 = (bf16[1344,128]{1,0:T(8,128)(2,1)S(1)}, bf16[1344,128]{1,0:T(8,128)(2,1)}, u32[]{:S(2)}, u32[]{:S(2)}) collective-permute-start(bf16[1344,128]{1,0:T(8,128)(2,1)S(1)} %shard_map.131.own.both_ref), channel_id=1, source_target_pairs={{0,2},{1,3},{2,0},{3,1},{4,6},{5,7},{6,4},{7,5},{8,10},{9,11},{10,... | collective-permute-start | bytes 1032200 | tf_op jit(solution)/shard_map/ppermute | solution.py:298
  36.7 2.5 %shard_map.137 = (bf16[128,512]{1,0:T(8,128)(2,1)S(1)}, bf16[128,512]{1,0:T(8,128)(2,1)S(1)}, f32[128,128]{1,0:T(8,128)S(1)}) custom-call(bf16[4,672,128]{2,1,0:T(8,128)(2,1)} %all-to-all-done.x_ref, f32[1,2688]{1,0:T(1,128)S(1)} %copy-done.10, bf16[2688,256]{1,0:T(8,128)(2,1)S(1)} %bitcast.31, bf16[2688,256]{1,0:T(8,128)(2,1)S(1)} %bitcast.34, ...), custom_call_target="tpu_custom_call" | custom-call | bytes 13200000 | tf_op jit(solution)/shard_map/pallas_call | solution.py:353
  39.2 3.5 %collective-permute-start.13 = (bf16[128,512]{1,0:T(8,128)(2,1)S(1)}, bf16[128,512]{1,0:T(8,128)(2,1)S(1)}, u32[]{:S(2)}, u32[]{:S(2)}) collective-permute-start(bf16[128,512]{1,0:T(8,128)(2,1)S(1)} %get-tuple-element.40.kv_ref.own), channel_id=1, source_target_pairs={{0,16},{4,20},{8,24},{12,28},{16,32},{20,36},{24,40},{28,44},{32,4... | collective-permute-start | bytes 393224 | tf_op jit(solution)/shard_map/ppermute | solution.py:279
  42.7 14.2 %collective-permute-start.12 = (bf16[128,512]{1,0:T(8,128)(2,1)S(1)}, bf16[128,512]{1,0:T(8,128)(2,1)S(1)}, u32[]{:S(2)}, u32[]{:S(2)}) collective-permute-start(bf16[128,512]{1,0:T(8,128)(2,1)S(1)} %get-tuple-element.40.kv_ref.own), channel_id=1, source_target_pairs={{0,8},{4,12},{8,16},{12,20},{16,24},{20,28},{24,32},{28,36},{32,40... | collective-permute-start | bytes 393224 | tf_op jit(solution)/shard_map/ppermute | solution.py:279
  57.5 1.9 %collective-permute-start.14 = (bf16[128,512]{1,0:T(8,128)(2,1)S(1)}, bf16[128,512]{1,0:T(8,128)(2,1)S(1)}, u32[]{:S(2)}, u32[]{:S(2)}) collective-permute-start(bf16[128,512]{1,0:T(8,128)(2,1)S(1)} %shard_map.138), channel_id=1, source_target_pairs={{0,4},{4,0},{8,12},{12,8},{16,20},{20,16},{24,28},{28,24},{32,36},... | collective-permute-start | bytes 393224 | tf_op jit(solution)/shard_map/ppermute | solution.py:284
  59.5 3.1 %collective-permute-done.12.two = bf16[128,512]{1,0:T(8,128)(2,1)S(1)} collective-permute-done((bf16[128,512]{1,0:T(8,128)(2,1)S(1)}, bf16[128,512]{1,0:T(8,128)(2,1)S(1)}, u32[]{:S(2)}, u32[]{:S(2)}) %collective-permute-start.12) | collective-permute-done | bytes 131104 | tf_op jit(solution)/shard_map/ppermute | solution.py:279
  64.5 3.2 %shard_map.132 = (bf16[128,512]{1,0:T(8,128)(2,1)S(1)}, bf16[128,512]{1,0:T(8,128)(2,1)S(1)}, bf16[128,512]{1,0:T(8,128)(2,1)S(1)}) custom-call(s32[5]{0:T(128)S(1)} %stack.31.info_ref, bf16[1344,128]{1,0:T(8,128)(2,1)S(1)} %shard_map.131.own.both_ref, bf16[1344,128]{1,0:T(8,128)(2,1)S(1)} %collective-permute-done.2.one, ...), custom_call_target="tpu_custom_call" | custom-call | bytes 13200000 | tf_op jit(solution)/shard_map/pallas_call | solution.py:364
  67.8 3.5 %collective-permute-start.6 = (bf16[128,512]{1,0:T(8,128)(2,1)S(1)}, bf16[128,512]{1,0:T(8,128)(2,1)S(1)}, u32[]{:S(2)}, u32[]{:S(2)}) collective-permute-start(bf16[128,512]{1,0:T(8,128)(2,1)S(1)} %get-tuple-element.32.kv_ref.own), channel_id=1, source_target_pairs={{0,16},{4,20},{8,24},{12,28},{16,32},{20,36},{24,40},{28,44},{32,4... | collective-permute-start | bytes 393224 | tf_op jit(solution)/shard_map/ppermute | solution.py:279
  71.2 10.7 %collective-permute-start.5 = (bf16[128,512]{1,0:T(8,128)(2,1)S(1)}, bf16[128,512]{1,0:T(8,128)(2,1)S(1)}, u32[]{:S(2)}, u32[]{:S(2)}) collective-permute-start(bf16[128,512]{1,0:T(8,128)(2,1)S(1)} %get-tuple-element.32.kv_ref.own), channel_id=1, source_target_pairs={{0,8},{4,12},{8,16},{12,20},{16,24},{20,28},{24,32},{28,36},{32,40... | collective-permute-start | bytes 393224 | tf_op jit(solution)/shard_map/ppermute | solution.py:279
  82.0 3.1 %shard_map.139 = (bf16[128,512]{1,0:T(8,128)(2,1)S(1)}, f32[128,512]{1,0:T(8,128)S(1)}, f32[128,512]{1,0:T(8,128)S(1)}, f32[128,512]{1,0:T(8,128)S(1)}, bf16[256,512]{1,0:T(8,128)(2,1)S(1)}) custom-call(s32[5]{0:T(128)S(1)} %stack.31.info_ref, s32[32,128]{1,0:T(8,128)S(1)} %bitcast.43, bf16[128,512]{1,0:T(8,128)(2,1)S(1)} %get-tuple-element.38.q_ref, ...), custom_call_target="tpu_custom_call" | custom-call | bytes 13200000 | tf_op jit(solution)/shard_map/pallas_call | solution.py:372
  87.6 2.4 %collective-permute-start.7 = (bf16[128,512]{1,0:T(8,128)(2,1)S(1)}, bf16[128,512]{1,0:T(8,128)(2,1)S(1)}, u32[]{:S(2)}, u32[]{:S(2)}) collective-permute-start(bf16[128,512]{1,0:T(8,128)(2,1)S(1)} %shard_map.133), channel_id=1, source_target_pairs={{0,4},{4,0},{8,12},{12,8},{16,20},{20,16},{24,28},{28,24},{32,36},... | collective-permute-start | bytes 393224 | tf_op jit(solution)/shard_map/ppermute | solution.py:284
  90.0 1.9 %collective-permute-start.8 = (bf16[128,512]{1,0:T(8,128)(2,1)S(1)}, bf16[128,512]{1,0:T(8,128)(2,1)S(1)}, u32[]{:S(2)}, u32[]{:S(2)}) collective-permute-start(bf16[128,512]{1,0:T(8,128)(2,1)S(1)} %collective-permute-done.5.two), channel_id=1, source_target_pairs={{0,4},{4,0},{8,12},{12,8},{16,20},{20,16},{24,28},{28,24},{32,36},... | collective-permute-start | bytes 393224 | tf_op jit(solution)/shard_map/ppermute | solution.py:284
  93.2 2.9 %shard_map.134 = (bf16[672,128]{1,0:T(8,128)(2,1)S(1)}, bf16[672,128]{1,0:T(8,128)(2,1)S(1)}, bf16[672,128]{1,0:T(8,128)(2,1)S(1)}, bf16[672,128]{1,0:T(8,128)(2,1)S(1)}) custom-call(s32[5]{0:T(128)S(1)} %stack.31.info_ref, s32[32,128]{1,0:T(8,128)S(1)} %bitcast.44, bf16[128,512]{1,0:T(8,128)(2,1)S(1)} %get-tuple-element.31.q_ref, ...), custom_call_target="tpu_custom_call" | custom-call | bytes 13200000 | tf_op jit(solution)/shard_map/pallas_call | solution.py:385
  96.2 2.9 %collective-permute-start.9 = (bf16[672,128]{1,0:T(8,128)(2,1)S(1)}, bf16[672,128]{1,0:T(8,128)(2,1)S(1)}, u32[]{:S(2)}, u32[]{:S(2)}) collective-permute-start(bf16[672,128]{1,0:T(8,128)(2,1)S(1)} %get-tuple-element.34), channel_id=1, source_target_pairs={{0,1},{1,2},{2,3},{3,0},{4,5},{5,6},{6,7},{7,4},{8,9},{9,10},{10,1... | collective-permute-start | bytes 516104 | tf_op jit(solution)/shard_map/ppermute | solution.py:298
  99.7 5.9 %collective-permute-start.17 = (bf16[128,512]{1,0:T(8,128)(2,1)S(1)}, bf16[128,512]{1,0:T(8,128)(2,1)S(1)}, u32[]{:S(2)}, u32[]{:S(2)}) collective-permute-start(bf16[128,512]{1,0:T(8,128)(2,1)S(1)} %get-tuple-element.47), channel_id=1, source_target_pairs={{8,0},{12,4},{16,8},{20,12},{24,16},{28,20},{32,24},{36,28},{40,32... | collective-permute-start | bytes 393224 | tf_op jit(solution)/shard_map/ppermute | solution.py:279
  105.6 2.1 %collective-permute-start.18 = (bf16[128,512]{1,0:T(8,128)(2,1)S(1)}, bf16[128,512]{1,0:T(8,128)(2,1)S(1)}, u32[]{:S(2)}, u32[]{:S(2)}) collective-permute-start(bf16[128,512]{1,0:T(8,128)(2,1)S(1)} %get-tuple-element.48), channel_id=1, source_target_pairs={{16,0},{20,4},{24,8},{28,12},{32,16},{36,20},{40,24},{44,28},{48,3... | collective-permute-start | bytes 393224 | tf_op jit(solution)/shard_map/ppermute | solution.py:279
  107.7 7.1 %collective-permute-done.17.two_ref = bf16[128,512]{1,0:T(8,128)(2,1)S(1)} collective-permute-done((bf16[128,512]{1,0:T(8,128)(2,1)S(1)}, bf16[128,512]{1,0:T(8,128)(2,1)S(1)}, u32[]{:S(2)}, u32[]{:S(2)}) %collective-permute-start.17) | collective-permute-done | bytes 131104 | tf_op jit(solution)/shard_map/ppermute | solution.py:279
  114.7 3.0 %collective-permute-done.18.four_ref = bf16[128,512]{1,0:T(8,128)(2,1)S(1)} collective-permute-done((bf16[128,512]{1,0:T(8,128)(2,1)S(1)}, bf16[128,512]{1,0:T(8,128)(2,1)S(1)}, u32[]{:S(2)}, u32[]{:S(2)}) %collective-permute-start.18) | collective-permute-done | bytes 131104 | tf_op jit(solution)/shard_map/ppermute | solution.py:279
  117.7 2.1 %shard_map.141 = (bf16[688,128]{1,0:T(8,128)(2,1)S(1)}, bf16[688,128]{1,0:T(8,128)(2,1)S(1)}, bf16[688,128]{1,0:T(8,128)(2,1)S(1)}, bf16[688,128]{1,0:T(8,128)(2,1)S(1)}) custom-call(s32[5]{0:T(128)S(1)} %stack.31.info_ref, bf16[128,512]{1,0:T(8,128)(2,1)S(1)} %get-tuple-element.41.dq_ref, f32[128,512]{1,0:T(8,128)S(1)} %get-tuple-element.46.own_ref, ...), custom_call_target="tpu_custom_call" | custom-call | bytes 13200000 | tf_op jit(solution)/shard_map/pallas_call | solution.py:394
  119.8 4.9 %collective-permute-start.19 = (bf16[688,128]{1,0:T(8,128)(2,1)S(1)}, bf16[688,128]{1,0:T(8,128)(2,1)S(1)}, u32[]{:S(2)}, u32[]{:S(2)}) collective-permute-start(bf16[688,128]{1,0:T(8,128)(2,1)S(1)} %get-tuple-element.50), channel_id=1, source_target_pairs={{0,1},{1,2},{2,3},{3,0},{4,5},{5,6},{6,7},{7,4},{8,9},{9,10},{10,1... | collective-permute-start | bytes 528392 | tf_op jit(solution)/shard_map/ppermute | solution.py:298
  124.7 2.2 %collective-permute-start.20 = (bf16[688,128]{1,0:T(8,128)(2,1)S(1)}, bf16[688,128]{1,0:T(8,128)(2,1)S(1)}, u32[]{:S(2)}, u32[]{:S(2)}) collective-permute-start(bf16[688,128]{1,0:T(8,128)(2,1)S(1)} %get-tuple-element.51), channel_id=1, source_target_pairs={{0,3},{1,0},{2,1},{3,2},{4,7},{5,4},{6,5},{7,6},{8,11},{9,8},{10,9... | collective-permute-start | bytes 528392 | tf_op jit(solution)/shard_map/ppermute | solution.py:298
  126.9 4.5 %collective-permute-start.21 = (bf16[688,128]{1,0:T(8,128)(2,1)S(1)}, bf16[688,128]{1,0:T(8,128)(2,1)S(1)}, u32[]{:S(2)}, u32[]{:S(2)}) collective-permute-start(bf16[688,128]{1,0:T(8,128)(2,1)S(1)} %get-tuple-element.52), channel_id=1, source_target_pairs={{0,2},{1,3},{2,0},{3,1},{4,6},{5,7},{6,4},{7,5},{8,10},{9,11},{10,... | collective-permute-start | bytes 528392 | tf_op jit(solution)/shard_map/ppermute | solution.py:298
  131.3 3.8 %collective-permute-start.10 = (bf16[672,128]{1,0:T(8,128)(2,1)S(1)}, bf16[672,128]{1,0:T(8,128)(2,1)S(1)}, u32[]{:S(2)}, u32[]{:S(2)}) collective-permute-start(bf16[672,128]{1,0:T(8,128)(2,1)S(1)} %get-tuple-element.35), channel_id=1, source_target_pairs={{0,3},{1,0},{2,1},{3,2},{4,7},{5,4},{6,5},{7,6},{8,11},{9,8},{10,9... | collective-permute-start | bytes 516104 | tf_op jit(solution)/shard_map/ppermute | solution.py:298
  135.2 1.9 %collective-permute-start.11 = (bf16[672,128]{1,0:T(8,128)(2,1)S(1)}, bf16[672,128]{1,0:T(8,128)(2,1)S(1)}, u32[]{:S(2)}, u32[]{:S(2)}) collective-permute-start(bf16[672,128]{1,0:T(8,128)(2,1)S(1)} %get-tuple-element.36), channel_id=1, source_target_pairs={{0,2},{1,3},{2,0},{3,1},{4,6},{5,7},{6,4},{7,5},{8,10},{9,11},{10,... | collective-permute-start | bytes 516104 | tf_op jit(solution)/shard_map/ppermute | solution.py:298
  138.1 2.0 %collective-permute-done.10.minus = bf16[672,128]{1,0:T(8,128)(2,1)S(1)} collective-permute-done((bf16[672,128]{1,0:T(8,128)(2,1)S(1)}, bf16[672,128]{1,0:T(8,128)(2,1)S(1)}, u32[]{:S(2)}, u32[]{:S(2)}) %collective-permute-start.10) | collective-permute-done | bytes 172064 | tf_op jit(solution)/shard_map/ppermute | solution.py:298
  140.1 3.8 %collective-permute-done.11.far = bf16[672,128]{1,0:T(8,128)(2,1)S(1)} collective-permute-done((bf16[672,128]{1,0:T(8,128)(2,1)S(1)}, bf16[672,128]{1,0:T(8,128)(2,1)S(1)}, u32[]{:S(2)}, u32[]{:S(2)}) %collective-permute-start.11) | collective-permute-done | bytes 172064 | tf_op jit(solution)/shard_map/ppermute | solution.py:298
  (56 shorter events, 18.9 us)
Async XLA Ops:
  0.6 32.7 %copy-start = (bf16[1,2688,512]{2,1,0:T(8,128)(2,1)S(1)}, bf16[1,2688,512]{2,1,0:T(8,128)(2,1)}, u32[]{:S(2)}) copy-start(bf16[1,2688,512]{2,1,0:T(8,128)(2,1)} %param.18) | copy-start | bytes 8257540
  2.8 30.5 %all-to-all-start = ((bf16[4,672,128]{2,1,0:T(8,128)(2,1)}), bf16[4,672,128]{2,1,0:T(8,128)(2,1)}, u32[]{:S(2)}, u32[]{:S(2)}) async-start(bf16[4,672,128]{2,1,0:T(8,128)(2,1)} %shard_map.136), calls=%async_computation | async-start | bytes 1376256 | tf_op jit(solution)/shard_map/all_to_all | solution.py:347
  7.1 8.1 %collective-permute-start = (bf16[672,128]{1,0:T(8,128)(2,1)}, bf16[672,128]{1,0:T(8,128)(2,1)S(1)}, u32[]{:S(2)}, u32[]{:S(2)}) collective-permute-start(bf16[672,128]{1,0:T(8,128)(2,1)} %bitcast.47), channel_id=1, source_target_pairs={{0,128},{128,256},{256,384},{384,512},{512,640},{1,129},{129,257},... | collective-permute-start | bytes 516104 | tf_op jit(solution)/shard_map/ppermute | solution.py:290
  11.4 8.5 %collective-permute-start.1 = (bf16[672,128]{1,0:T(8,128)(2,1)}, bf16[672,128]{1,0:T(8,128)(2,1)S(1)}, u32[]{:S(2)}, u32[]{:S(2)}) collective-permute-start(bf16[672,128]{1,0:T(8,128)(2,1)} %bitcast.48), channel_id=1, source_target_pairs={{128,0},{256,128},{384,256},{512,384},{640,512},{129,1},{257,129},... | collective-permute-start | bytes 516104 | tf_op jit(solution)/shard_map/ppermute | solution.py:290
  22.3 42.1 %collective-permute-start.2 = (bf16[1344,128]{1,0:T(8,128)(2,1)S(1)}, bf16[1344,128]{1,0:T(8,128)(2,1)S(1)}, u32[]{:S(2)}, u32[]{:S(2)}) collective-permute-start(bf16[1344,128]{1,0:T(8,128)(2,1)S(1)} %shard_map.131.own.both_ref), channel_id=1, source_target_pairs={{0,1},{1,2},{2,3},{3,0},{4,5},{5,6},{6,7},{7,4},{8,9},{9,10},{10,1... | collective-permute-start | bytes 1032200 | tf_op jit(solution)/shard_map/ppermute | solution.py:298
  25.9 38.5 %collective-permute-start.3 = (bf16[1344,128]{1,0:T(8,128)(2,1)S(1)}, bf16[1344,128]{1,0:T(8,128)(2,1)}, u32[]{:S(2)}, u32[]{:S(2)}) collective-permute-start(bf16[1344,128]{1,0:T(8,128)(2,1)S(1)} %shard_map.131.own.both_ref), channel_id=1, source_target_pairs={{0,3},{1,0},{2,1},{3,2},{4,7},{5,4},{6,5},{7,6},{8,11},{9,8},{10,9... | collective-permute-start | bytes 1032200 | tf_op jit(solution)/shard_map/ppermute | solution.py:298
  29.4 35.1 %collective-permute-start.4 = (bf16[1344,128]{1,0:T(8,128)(2,1)S(1)}, bf16[1344,128]{1,0:T(8,128)(2,1)}, u32[]{:S(2)}, u32[]{:S(2)}) collective-permute-start(bf16[1344,128]{1,0:T(8,128)(2,1)S(1)} %shard_map.131.own.both_ref), channel_id=1, source_target_pairs={{0,2},{1,3},{2,0},{3,1},{4,6},{5,7},{6,4},{7,5},{8,10},{9,11},{10,... | collective-permute-start | bytes 1032200 | tf_op jit(solution)/shard_map/ppermute | solution.py:298
  33.3 1.3 copy-start.1
  36.7 27.8 %copy-start.2 = (bf16[1,2688,256]{2,1,0:T(8,128)(2,1)S(1)}, bf16[1,2688,256]{2,1,0:T(8,128)(2,1)}, u32[]{:S(2)}) copy-start(bf16[1,2688,256]{2,1,0:T(8,128)(2,1)} %param.19) | copy-start | bytes 4128772
  36.7 27.8 %copy-start.4 = (bf16[1,2688,256]{2,1,0:T(8,128)(2,1)S(1)}, bf16[1,2688,256]{2,1,0:T(8,128)(2,1)}, u32[]{:S(2)}) copy-start(bf16[1,2688,256]{2,1,0:T(8,128)(2,1)} %param.20) | copy-start | bytes 4128772
  36.7 27.8 %copy-start.5 = (bf16[1,512,2688]{2,1,0:T(8,128)(2,1)S(1)}, bf16[1,512,2688]{2,1,0:T(8,128)(2,1)}, u32[]{:S(2)}) copy-start(bf16[1,512,2688]{2,1,0:T(8,128)(2,1)} %param.21) | copy-start | bytes 8257540
  36.7 27.8 %copy-start.11 = (f32[1,2688]{1,0:T(1,128)S(1)}, f32[1,2688]{1,0:T(1,128)}, u32[]{:S(2)}) copy-start(f32[1,2688]{1,0:T(1,128)} %gain_ref.5) | copy-start | bytes 32260
  39.2 17.7 %collective-permute-start.13 = (bf16[128,512]{1,0:T(8,128)(2,1)S(1)}, bf16[128,512]{1,0:T(8,128)(2,1)S(1)}, u32[]{:S(2)}, u32[]{:S(2)}) collective-permute-start(bf16[128,512]{1,0:T(8,128)(2,1)S(1)} %get-tuple-element.40.kv_ref.own), channel_id=1, source_target_pairs={{0,16},{4,20},{8,24},{12,28},{16,32},{20,36},{24,40},{28,44},{32,4... | collective-permute-start | bytes 393224 | tf_op jit(solution)/shard_map/ppermute | solution.py:279
  42.7 19.8 %collective-permute-start.12 = (bf16[128,512]{1,0:T(8,128)(2,1)S(1)}, bf16[128,512]{1,0:T(8,128)(2,1)S(1)}, u32[]{:S(2)}, u32[]{:S(2)}) collective-permute-start(bf16[128,512]{1,0:T(8,128)(2,1)S(1)} %get-tuple-element.40.kv_ref.own), channel_id=1, source_target_pairs={{0,8},{4,12},{8,16},{12,20},{16,24},{20,28},{24,32},{28,36},{32,40... | collective-permute-start | bytes 393224 | tf_op jit(solution)/shard_map/ppermute | solution.py:279
  57.5 24.4 %collective-permute-start.14 = (bf16[128,512]{1,0:T(8,128)(2,1)S(1)}, bf16[128,512]{1,0:T(8,128)(2,1)S(1)}, u32[]{:S(2)}, u32[]{:S(2)}) collective-permute-start(bf16[128,512]{1,0:T(8,128)(2,1)S(1)} %shard_map.138), channel_id=1, source_target_pairs={{0,4},{4,0},{8,12},{12,8},{16,20},{20,16},{24,28},{28,24},{32,36},... | collective-permute-start | bytes 393224 | tf_op jit(solution)/shard_map/ppermute | solution.py:284
  62.5 19.4 %collective-permute-start.15 = (bf16[128,512]{1,0:T(8,128)(2,1)S(1)}, bf16[128,512]{1,0:T(8,128)(2,1)S(1)}, u32[]{:S(2)}, u32[]{:S(2)}) collective-permute-start(bf16[128,512]{1,0:T(8,128)(2,1)S(1)} %collective-permute-done.12.two), channel_id=1, source_target_pairs={{0,4},{4,0},{8,12},{12,8},{16,20},{20,16},{24,28},{28,24},{32,36},... | collective-permute-start | bytes 393224 | tf_op jit(solution)/shard_map/ppermute | solution.py:284
  64.5 17.5 %copy-start.12 = (s32[1,4096]{1,0:T(1,128)S(1)}, s32[1,4096]{1,0:T(1,128)}, u32[]{:S(2)}) copy-start(s32[1,4096]{1,0:T(1,128)} %param.23) | copy-start | bytes 49156
  64.5 28.7 %copy-start.13 = (s32[1,4096]{1,0:T(1,128)S(1)}, s32[1,4096]{1,0:T(1,128)}, u32[]{:S(2)}) copy-start(s32[1,4096]{1,0:T(1,128)} %param.22) | copy-start | bytes 49156
  67.8 19.2 %collective-permute-start.6 = (bf16[128,512]{1,0:T(8,128)(2,1)S(1)}, bf16[128,512]{1,0:T(8,128)(2,1)S(1)}, u32[]{:S(2)}, u32[]{:S(2)}) collective-permute-start(bf16[128,512]{1,0:T(8,128)(2,1)S(1)} %get-tuple-element.32.kv_ref.own), channel_id=1, source_target_pairs={{0,16},{4,20},{8,24},{12,28},{16,32},{20,36},{24,40},{28,44},{32,4... | collective-permute-start | bytes 393224 | tf_op jit(solution)/shard_map/ppermute | solution.py:279
  71.2 18.8 %collective-permute-start.5 = (bf16[128,512]{1,0:T(8,128)(2,1)S(1)}, bf16[128,512]{1,0:T(8,128)(2,1)S(1)}, u32[]{:S(2)}, u32[]{:S(2)}) collective-permute-start(bf16[128,512]{1,0:T(8,128)(2,1)S(1)} %get-tuple-element.32.kv_ref.own), channel_id=1, source_target_pairs={{0,8},{4,12},{8,16},{12,20},{16,24},{20,28},{24,32},{28,36},{32,40... | collective-permute-start | bytes 393224 | tf_op jit(solution)/shard_map/ppermute | solution.py:279
  85.1 14.0 %collective-permute-start.16 = (bf16[256,512]{1,0:T(8,128)(2,1)S(1)}, bf16[256,512]{1,0:T(8,128)(2,1)S(1)}, u32[]{:S(2)}, u32[]{:S(2)}) collective-permute-start(bf16[256,512]{1,0:T(8,128)(2,1)S(1)} %get-tuple-element.45), channel_id=1, source_target_pairs={{0,4},{4,0},{8,12},{12,8},{16,20},{20,16},{24,28},{28,24},{32,36},... | collective-permute-start | bytes 786440 | tf_op jit(solution)/shard_map/ppermute | solution.py:284
  87.6 4.4 %collective-permute-start.7 = (bf16[128,512]{1,0:T(8,128)(2,1)S(1)}, bf16[128,512]{1,0:T(8,128)(2,1)S(1)}, u32[]{:S(2)}, u32[]{:S(2)}) collective-permute-start(bf16[128,512]{1,0:T(8,128)(2,1)S(1)} %shard_map.133), channel_id=1, source_target_pairs={{0,4},{4,0},{8,12},{12,8},{16,20},{20,16},{24,28},{28,24},{32,36},... | collective-permute-start | bytes 393224 | tf_op jit(solution)/shard_map/ppermute | solution.py:284
  90.0 3.2 %collective-permute-start.8 = (bf16[128,512]{1,0:T(8,128)(2,1)S(1)}, bf16[128,512]{1,0:T(8,128)(2,1)S(1)}, u32[]{:S(2)}, u32[]{:S(2)}) collective-permute-start(bf16[128,512]{1,0:T(8,128)(2,1)S(1)} %collective-permute-done.5.two), channel_id=1, source_target_pairs={{0,4},{4,0},{8,12},{12,8},{16,20},{20,16},{24,28},{28,24},{32,36},... | collective-permute-start | bytes 393224 | tf_op jit(solution)/shard_map/ppermute | solution.py:284
  96.2 39.0 %collective-permute-start.9 = (bf16[672,128]{1,0:T(8,128)(2,1)S(1)}, bf16[672,128]{1,0:T(8,128)(2,1)S(1)}, u32[]{:S(2)}, u32[]{:S(2)}) collective-permute-start(bf16[672,128]{1,0:T(8,128)(2,1)S(1)} %get-tuple-element.34), channel_id=1, source_target_pairs={{0,1},{1,2},{2,3},{3,0},{4,5},{5,6},{6,7},{7,4},{8,9},{9,10},{10,1... | collective-permute-start | bytes 516104 | tf_op jit(solution)/shard_map/ppermute | solution.py:298
  99.7 15.0 %collective-permute-start.17 = (bf16[128,512]{1,0:T(8,128)(2,1)S(1)}, bf16[128,512]{1,0:T(8,128)(2,1)S(1)}, u32[]{:S(2)}, u32[]{:S(2)}) collective-permute-start(bf16[128,512]{1,0:T(8,128)(2,1)S(1)} %get-tuple-element.47), channel_id=1, source_target_pairs={{8,0},{12,4},{16,8},{20,12},{24,16},{28,20},{32,24},{36,28},{40,32... | collective-permute-start | bytes 393224 | tf_op jit(solution)/shard_map/ppermute | solution.py:279
  105.6 12.1 %collective-permute-start.18 = (bf16[128,512]{1,0:T(8,128)(2,1)S(1)}, bf16[128,512]{1,0:T(8,128)(2,1)S(1)}, u32[]{:S(2)}, u32[]{:S(2)}) collective-permute-start(bf16[128,512]{1,0:T(8,128)(2,1)S(1)} %get-tuple-element.48), channel_id=1, source_target_pairs={{16,0},{20,4},{24,8},{28,12},{32,16},{36,20},{40,24},{44,28},{48,3... | collective-permute-start | bytes 393224 | tf_op jit(solution)/shard_map/ppermute | solution.py:279
  117.7 27.1 %copy-start.7 = (bf16[1,128,672]{1,2,0:T(8,128)(2,1)S(1)}, bf16[1,128,672]{1,2,0:T(8,128)(2,1)}, u32[]{:S(2)}) copy-start(bf16[1,128,672]{1,2,0:T(8,128)(2,1)} %param.14) | copy-start | bytes 516100
  119.8 24.9 %collective-permute-start.19 = (bf16[688,128]{1,0:T(8,128)(2,1)S(1)}, bf16[688,128]{1,0:T(8,128)(2,1)S(1)}, u32[]{:S(2)}, u32[]{:S(2)}) collective-permute-start(bf16[688,128]{1,0:T(8,128)(2,1)S(1)} %get-tuple-element.50), channel_id=1, source_target_pairs={{0,1},{1,2},{2,3},{3,0},{4,5},{5,6},{6,7},{7,4},{8,9},{9,10},{10,1... | collective-permute-start | bytes 528392 | tf_op jit(solution)/shard_map/ppermute | solution.py:298
  124.7 20.0 %collective-permute-start.20 = (bf16[688,128]{1,0:T(8,128)(2,1)S(1)}, bf16[688,128]{1,0:T(8,128)(2,1)S(1)}, u32[]{:S(2)}, u32[]{:S(2)}) collective-permute-start(bf16[688,128]{1,0:T(8,128)(2,1)S(1)} %get-tuple-element.51), channel_id=1, source_target_pairs={{0,3},{1,0},{2,1},{3,2},{4,7},{5,4},{6,5},{7,6},{8,11},{9,8},{10,9... | collective-permute-start | bytes 528392 | tf_op jit(solution)/shard_map/ppermute | solution.py:298
  126.9 17.9 %collective-permute-start.21 = (bf16[688,128]{1,0:T(8,128)(2,1)S(1)}, bf16[688,128]{1,0:T(8,128)(2,1)S(1)}, u32[]{:S(2)}, u32[]{:S(2)}) collective-permute-start(bf16[688,128]{1,0:T(8,128)(2,1)S(1)} %get-tuple-element.52), channel_id=1, source_target_pairs={{0,2},{1,3},{2,0},{3,1},{4,6},{5,7},{6,4},{7,5},{8,10},{9,11},{10,... | collective-permute-start | bytes 528392 | tf_op jit(solution)/shard_map/ppermute | solution.py:298
  131.3 8.8 %collective-permute-start.10 = (bf16[672,128]{1,0:T(8,128)(2,1)S(1)}, bf16[672,128]{1,0:T(8,128)(2,1)S(1)}, u32[]{:S(2)}, u32[]{:S(2)}) collective-permute-start(bf16[672,128]{1,0:T(8,128)(2,1)S(1)} %get-tuple-element.35), channel_id=1, source_target_pairs={{0,3},{1,0},{2,1},{3,2},{4,7},{5,4},{6,5},{7,6},{8,11},{9,8},{10,9... | collective-permute-start | bytes 516104 | tf_op jit(solution)/shard_map/ppermute | solution.py:298
  135.2 8.8 %collective-permute-start.11 = (bf16[672,128]{1,0:T(8,128)(2,1)S(1)}, bf16[672,128]{1,0:T(8,128)(2,1)S(1)}, u32[]{:S(2)}, u32[]{:S(2)}) collective-permute-start(bf16[672,128]{1,0:T(8,128)(2,1)S(1)} %get-tuple-element.36), channel_id=1, source_target_pairs={{0,2},{1,3},{2,0},{3,1},{4,6},{5,7},{6,4},{7,5},{8,10},{9,11},{10,... | collective-permute-start | bytes 516104 | tf_op jit(solution)/shard_map/ppermute | solution.py:298
  (5 other events, 4.9 us)

commit v4 on v3

--- a/solution.py
+++ b/solution.py
@@ -29,6 +29,10 @@
 
 def vmem(count):
     return [pl.BlockSpec(memory_space=pltpu.VMEM) for _ in range(count)]
+
+
+def any_space():
+    return pl.BlockSpec(memory_space=pl.ANY)
 
 
 def smem():
@@ -88,9 +92,15 @@
         hold_ref[lax.rem(place + offset, parts)] = piece[...]
 
 
-def spread_body(x_ref, out_ref):
-    for part in range(out_ref.shape[0]):
-        out_ref[part] = x_ref[...]
+def spread_body(x_ref, out_ref, sems):
+    copies = [
+        pltpu.make_async_copy(x_ref, out_ref.at[part], sems.at[part])
+        for part in range(out_ref.shape[0])
+    ]
+    for copy in copies:
+        copy.start()
+    for copy in copies:
+        copy.wait()
 
 
 def project_back_body(x_ref, gain_ref, wk_ref, wv_ref, wq_ref, q_ref, kv_ref, r_ref):
@@ -226,10 +236,9 @@
 
 
 def input_terms_body(
-    info_ref, dq_ref, own_ref, two_ref, four_ref, q_ref, kv_ref, wk_ref, wv_ref, wq_ref, *outs
+    dq_ref, own_ref, two_ref, four_ref, q_ref, kv_ref, wk_ref, wv_ref, wq_ref, out_ref
 ):
-    rows, length = outs[0].shape
-    parts = len(outs)
+    parts, rows, length = out_ref.shape
     share = wq_ref.shape[0] // parts
     half = own_ref.shape[1] // 2
     total = own_ref[...] + two_ref[...].astype(F32) + four_ref[...].astype(F32)
@@ -243,14 +252,13 @@
     high = row.astype(BF).astype(F32)
     first = lax.broadcasted_iota(jnp.int32, (rows - share, length), 0) == 0
     pair = jnp.where(first, high, row - high).astype(BF)
-    for out_ref, offset in zip(outs, SENDS):
-        part = lax.rem(info_ref[2] + offset, parts)
-        span = pl.ds(pl.multiple_of(part * share, 32), share)
-        d_norm = dot_nt(wq_ref[span, :], d_query)
-        d_norm = d_norm + dot_nt(wk_ref[span, :], d_key)
-        d_norm = d_norm + dot_nt(wv_ref[span, :], d_value)
-        out_ref[:share, :] = d_norm.astype(BF)
-        out_ref[share:, :] = pair
+    for part in range(parts):
+        span = slice(part * share, (part + 1) * share)
+        d_norm = dot_nt(wq_ref[span], d_query)
+        d_norm = d_norm + dot_nt(wk_ref[span], d_key)
+        d_norm = d_norm + dot_nt(wv_ref[span], d_value)
+        out_ref[part, :share] = d_norm.astype(BF)
+        out_ref[part, share:] = pair
 
 
 def total_of(refs):
@@ -263,10 +271,11 @@
     out_ref[...] = (both_ref[:share].astype(F32) + total).astype(BF)
 
 
-def finish_body(own, one, minus, far, x_ref, both_ref, gain_ref, r_ref, out_ref):
+def finish_body(sums_ref, x_ref, both_ref, gain_ref, r_ref, out_ref):
     share = x_ref.shape[0]
-    total = total_of((own, one, minus, far))
-    row = (total[share : share + 1] + total[share + 1 : share + 2]) / (len(SENDS) * share)
+    parts = sums_ref.shape[0]
+    total = sum(sums_ref[part].astype(F32) for part in range(parts))
+    row = (total[share : share + 1] + total[share + 1 : share + 2]) / (parts * share)
     factor = jnp.transpose(r_ref[...])[:1]
     d_input = factor * gain_ref[...] * total[:share]
     d_input = d_input - x_ref[...].astype(F32) * (factor * factor * row)
@@ -341,8 +350,12 @@
     )
     arrived = next_section(ahead, 1)
     returned = next_section(behind, -1)
-    spread = kernel(
-        spread_body, 4, jax.ShapeDtypeStruct((parts, share, length), BF), vmem(1), 1.0
+    spread = pl.pallas_call(
+        spread_body,
+        out_shape=jax.ShapeDtypeStruct((parts, share, length), BF),
+        in_specs=[any_space()], out_specs=any_space(),
+        scratch_shapes=[pltpu.SemaphoreType.DMA((parts,))],
+        name="spread", compiler_params=limit(4), cost_estimate=cost(1.0),
     )(stash)
     gathered = lax.all_to_all(spread, "fsdp", 0, 0)
     own_gain = kernel(
@@ -358,7 +371,7 @@
     blocks_back = window_blocks(info, kv_back)
 
     sent = kernel(
-        choose_body, LIMIT, rows(2 * share, length), [smem()] + vmem(4), 20.0,
+        choose_body, LIMIT, rows(2 * share, length), [smem()] + vmem(4), 4.0,
     )(info, embedded.T, arrived, loss_grad.T, returned)
     both = exchanged((sent,) * 3)
     q_front, kv_front, d_attn = kernel(
@@ -392,12 +405,12 @@
     )
 
     d_parts = kernel(
-        input_terms_body, LIMIT, (rows(share + 16, length),) * 4,
-        [smem()] + vmem(9),
-    )(info, d_query, t_own, back_two, back_four, q_back, kv_back, wk, wv, wq)
-    sums = exchanged(d_parts[1:])
-    input_grad = kernel(finish_body, 8, rows(share, length), vmem(8), 1.0)(
-        d_parts[0], *sums, stash, sent, own_gain, factor
+        input_terms_body, LIMIT,
+        jax.ShapeDtypeStruct((parts, share + 16, length), BF), vmem(9),
+    )(d_query, t_own, back_two, back_four, q_back, kv_back, wk, wv, wq)
+    d_parts = lax.all_to_all(d_parts, "fsdp", 0, 0)
+    input_grad = kernel(finish_body, 8, rows(share, length), vmem(5), 1.0)(
+        d_parts, stash, sent, own_gain, factor
     )
     return (forward_out.T[None], input_grad.T[None])
 

time: 147 us -> 154 us (1.048)
  the two profiles are of different devices: /device:TPU:16 before, /device:TPU:24 now
where the time goes in v4:
time: 154 us; the launch traced here: 153 us
  starting transfers between devices  92.2 us (60%)
  waiting for transfers between devices  29.8 us (19%)
  Pallas kernels  19.3 us (13%)
  local copies, waits for them, and re-layouts  10.7 us (7%)
    ppermute x6, starting transfers between devices, shifted(): return lax.ppermute(value, 'seq', pairs)  46.6 us
    ppermute x6, starting transfers between devices, exchanged(): received.append(lax.ppermute(value, 'fsdp', pairs))  21.9 us
    ppermute x6, waiting for transfers between devices, shifted(): return lax.ppermute(value, 'seq', pairs)  15.8 us
    unnamed x36, local copies, waits for them, and re-layouts  10.6 us
    ppermute x5, starting transfers between devices, swapped(): return lax.ppermute(value, 'seq', [(s, s ^ 1) for s in range(count)])  10.1 us
    ppermute x2, waiting for transfers between devices, next_section(): return lax.ppermute(value, 'pipe', pairs)  7.17 us
    ppermute x2, starting transfers between devices, next_section(): return lax.ppermute(value, 'pipe', pairs)  5.57 us
    ppermute x6, waiting for transfers between devices, exchanged(): received.append(lax.ppermute(value, 'fsdp', pairs))  4.34 us
  transfers between devices with their start and end apart: 21, of which 9 were waited for; matrix products, arithmetic and copies ran while one was open for 0% of the time, Pallas kernels for 8%

profile of v4, /device:TPU:24, one launch (start us, length us, event | category | flops | bytes accessed | tf_op | source)
XLA Modules:
  0.0 153.0 jit_solution(4332499133425056901)
XLA Ops:
  2.7 4.3 %all-to-all-start = ((bf16[4,672,128]{2,1,0:T(8,128)(2,1)}), bf16[4,672,128]{2,1,0:T(8,128)(2,1)}, u32[]{:S(2)}, u32[]{:S(2)}) async-start(bf16[4,672,128]{2,1,0:T(8,128)(2,1)} %spread.1), calls=%async_computation | async-start | bytes 1376256 | tf_op jit(solution)/shard_map/all_to_all | solution.py:360
  7.0 4.3 %collective-permute-start = (bf16[672,128]{1,0:T(8,128)(2,1)}, bf16[672,128]{1,0:T(8,128)(2,1)S(1)}, u32[]{:S(2)}, u32[]{:S(2)}) collective-permute-start(bf16[672,128]{1,0:T(8,128)(2,1)} %bitcast.47), channel_id=1, source_target_pairs={{0,128},{128,256},{256,384},{384,512},{512,640},{1,129},{129,257},... | collective-permute-start | bytes 516104 | tf_op jit(solution)/shard_map/ppermute | solution.py:299
  12.6 2.5 %collective-permute-done.arr_ref = bf16[672,128]{1,0:T(8,128)(2,1)S(1)} collective-permute-done((bf16[672,128]{1,0:T(8,128)(2,1)}, bf16[672,128]{1,0:T(8,128)(2,1)S(1)}, u32[]{:S(2)}, u32[]{:S(2)}) %collective-permute-start) | collective-permute-done | bytes 172064 | tf_op jit(solution)/shard_map/ppermute | solution.py:299
  15.1 4.7 %collective-permute-done.1.ret_ref = bf16[672,128]{1,0:T(8,128)(2,1)S(1)} collective-permute-done((bf16[672,128]{1,0:T(8,128)(2,1)}, bf16[672,128]{1,0:T(8,128)(2,1)S(1)}, u32[]{:S(2)}, u32[]{:S(2)}) %collective-permute-start.1) | collective-permute-done | bytes 172064 | tf_op jit(solution)/shard_map/ppermute | solution.py:299
  22.3 3.6 %collective-permute-start.2 = (bf16[1344,128]{1,0:T(8,128)(2,1)S(1)}, bf16[1344,128]{1,0:T(8,128)(2,1)S(1)}, u32[]{:S(2)}, u32[]{:S(2)}) collective-permute-start(bf16[1344,128]{1,0:T(8,128)(2,1)S(1)} %shard_map.131.own.both_ref), channel_id=1, source_target_pairs={{0,1},{1,2},{2,3},{3,0},{4,5},{5,6},{6,7},{7,4},{8,9},{9,10},{10,1... | collective-permute-start | bytes 1032200 | tf_op jit(solution)/shard_map/ppermute | solution.py:307
  25.9 3.5 %collective-permute-start.3 = (bf16[1344,128]{1,0:T(8,128)(2,1)S(1)}, bf16[1344,128]{1,0:T(8,128)(2,1)}, u32[]{:S(2)}, u32[]{:S(2)}) collective-permute-start(bf16[1344,128]{1,0:T(8,128)(2,1)S(1)} %shard_map.131.own.both_ref), channel_id=1, source_target_pairs={{0,3},{1,0},{2,1},{3,2},{4,7},{5,4},{6,5},{7,6},{8,11},{9,8},{10,9... | collective-permute-start | bytes 1032200 | tf_op jit(solution)/shard_map/ppermute | solution.py:307
  29.3 3.9 %collective-permute-start.4 = (bf16[1344,128]{1,0:T(8,128)(2,1)S(1)}, bf16[1344,128]{1,0:T(8,128)(2,1)}, u32[]{:S(2)}, u32[]{:S(2)}) collective-permute-start(bf16[1344,128]{1,0:T(8,128)(2,1)S(1)} %shard_map.131.own.both_ref), channel_id=1, source_target_pairs={{0,2},{1,3},{2,0},{3,1},{4,6},{5,7},{6,4},{7,5},{8,10},{9,11},{10,... | collective-permute-start | bytes 1032200 | tf_op jit(solution)/shard_map/ppermute | solution.py:307
  36.6 2.5 %shard_map.136 = (bf16[128,512]{1,0:T(8,128)(2,1)S(1)}, bf16[128,512]{1,0:T(8,128)(2,1)S(1)}, f32[128,128]{1,0:T(8,128)S(1)}) custom-call(bf16[4,672,128]{2,1,0:T(8,128)(2,1)} %all-to-all-done.x_ref, f32[1,2688]{1,0:T(1,128)S(1)} %copy-done.14, bf16[2688,256]{1,0:T(8,128)(2,1)S(1)} %bitcast.31, bf16[2688,256]{1,0:T(8,128)(2,1)S(1)} %bitcast.34, ...), custom_call_target="tpu_custom_call" | custom-call | bytes 13200000 | tf_op jit(solution)/shard_map/pallas_call | solution.py:366
  39.1 4.7 %collective-permute-start.13 = (bf16[128,512]{1,0:T(8,128)(2,1)S(1)}, bf16[128,512]{1,0:T(8,128)(2,1)S(1)}, u32[]{:S(2)}, u32[]{:S(2)}) collective-permute-start(bf16[128,512]{1,0:T(8,128)(2,1)S(1)} %get-tuple-element.36.kv_ref.own), channel_id=1, source_target_pairs={{0,16},{4,20},{8,24},{12,28},{16,32},{20,36},{24,40},{28,44},{32,4... | collective-permute-start | bytes 393224 | tf_op jit(solution)/shard_map/ppermute | solution.py:288
  43.8 14.2 %collective-permute-start.12 = (bf16[128,512]{1,0:T(8,128)(2,1)S(1)}, bf16[128,512]{1,0:T(8,128)(2,1)S(1)}, u32[]{:S(2)}, u32[]{:S(2)}) collective-permute-start(bf16[128,512]{1,0:T(8,128)(2,1)S(1)} %get-tuple-element.36.kv_ref.own), channel_id=1, source_target_pairs={{0,8},{4,12},{8,16},{12,20},{16,24},{20,28},{24,32},{28,36},{32,40... | collective-permute-start | bytes 393224 | tf_op jit(solution)/shard_map/ppermute | solution.py:288
  58.6 1.9 %collective-permute-start.14 = (bf16[128,512]{1,0:T(8,128)(2,1)S(1)}, bf16[128,512]{1,0:T(8,128)(2,1)S(1)}, u32[]{:S(2)}, u32[]{:S(2)}) collective-permute-start(bf16[128,512]{1,0:T(8,128)(2,1)S(1)} %shard_map.137), channel_id=1, source_target_pairs={{0,4},{4,0},{8,12},{12,8},{16,20},{20,16},{24,28},{28,24},{32,36},... | collective-permute-start | bytes 393224 | tf_op jit(solution)/shard_map/ppermute | solution.py:293
  60.6 1.8 %collective-permute-done.12.two = bf16[128,512]{1,0:T(8,128)(2,1)S(1)} collective-permute-done((bf16[128,512]{1,0:T(8,128)(2,1)S(1)}, bf16[128,512]{1,0:T(8,128)(2,1)S(1)}, u32[]{:S(2)}, u32[]{:S(2)}) %collective-permute-start.12) | collective-permute-done | bytes 131104 | tf_op jit(solution)/shard_map/ppermute | solution.py:288
  62.4 1.9 %collective-permute-start.15 = (bf16[128,512]{1,0:T(8,128)(2,1)S(1)}, bf16[128,512]{1,0:T(8,128)(2,1)S(1)}, u32[]{:S(2)}, u32[]{:S(2)}) collective-permute-start(bf16[128,512]{1,0:T(8,128)(2,1)S(1)} %collective-permute-done.12.two), channel_id=1, source_target_pairs={{0,4},{4,0},{8,12},{12,8},{16,20},{20,16},{24,28},{28,24},{32,36},... | collective-permute-start | bytes 393224 | tf_op jit(solution)/shard_map/ppermute | solution.py:293
  66.1 3.2 %shard_map.132 = (bf16[128,512]{1,0:T(8,128)(2,1)S(1)}, bf16[128,512]{1,0:T(8,128)(2,1)S(1)}, bf16[128,512]{1,0:T(8,128)(2,1)S(1)}) custom-call(s32[5]{0:T(128)S(1)} %stack.31.info_ref, bf16[1344,128]{1,0:T(8,128)(2,1)S(1)} %shard_map.131.own.both_ref, bf16[1344,128]{1,0:T(8,128)(2,1)S(1)} %copy-done.11, bf16[1344,128]{1,0:T(8,128)(2,1)} %collective-permute-done.3.minus, ...), custom_call_target="tpu_custom_call" | custom-call | bytes 13200000 | tf_op jit(solution)/shard_map/pallas_call | solution.py:377
  69.3 3.1 %shard_map.138 = (bf16[128,512]{1,0:T(8,128)(2,1)S(1)}, f32[128,512]{1,0:T(8,128)S(1)}, f32[128,512]{1,0:T(8,128)S(1)}, f32[128,512]{1,0:T(8,128)S(1)}, bf16[256,512]{1,0:T(8,128)(2,1)S(1)}) custom-call(s32[5]{0:T(128)S(1)} %stack.31.info_ref, s32[32,128]{1,0:T(8,128)S(1)} %bitcast.43, bf16[128,512]{1,0:T(8,128)(2,1)S(1)} %get-tuple-element.34.q_ref, ...), custom_call_target="tpu_custom_call" | custom-call | bytes 13200000 | tf_op jit(solution)/shard_map/pallas_call | solution.py:385
  72.4 2.4 %collective-permute-start.16 = (bf16[256,512]{1,0:T(8,128)(2,1)S(1)}, bf16[256,512]{1,0:T(8,128)(2,1)S(1)}, u32[]{:S(2)}, u32[]{:S(2)}) collective-permute-start(bf16[256,512]{1,0:T(8,128)(2,1)S(1)} %get-tuple-element.41), channel_id=1, source_target_pairs={{0,4},{4,0},{8,12},{12,8},{16,20},{20,16},{24,28},{28,24},{32,36},... | collective-permute-start | bytes 786440 | tf_op jit(solution)/shard_map/ppermute | solution.py:293
  76.6 10.6 %collective-permute-start.17 = (bf16[128,512]{1,0:T(8,128)(2,1)S(1)}, bf16[128,512]{1,0:T(8,128)(2,1)S(1)}, u32[]{:S(2)}, u32[]{:S(2)}) collective-permute-start(bf16[128,512]{1,0:T(8,128)(2,1)S(1)} %get-tuple-element.43), channel_id=1, source_target_pairs={{8,0},{12,4},{16,8},{20,12},{24,16},{28,20},{32,24},{36,28},{40,32... | collective-permute-start | bytes 393224 | tf_op jit(solution)/shard_map/ppermute | solution.py:288
  87.2 2.1 %collective-permute-start.18 = (bf16[128,512]{1,0:T(8,128)(2,1)S(1)}, bf16[128,512]{1,0:T(8,128)(2,1)S(1)}, u32[]{:S(2)}, u32[]{:S(2)}) collective-permute-start(bf16[128,512]{1,0:T(8,128)(2,1)S(1)} %get-tuple-element.44), channel_id=1, source_target_pairs={{16,0},{20,4},{24,8},{28,12},{32,16},{36,20},{40,24},{44,28},{48,3... | collective-permute-start | bytes 393224 | tf_op jit(solution)/shard_map/ppermute | solution.py:288
  89.3 2.3 %collective-permute-done.17.two_ref = bf16[128,512]{1,0:T(8,128)(2,1)S(1)} collective-permute-done((bf16[128,512]{1,0:T(8,128)(2,1)S(1)}, bf16[128,512]{1,0:T(8,128)(2,1)S(1)}, u32[]{:S(2)}, u32[]{:S(2)}) %collective-permute-start.17) | collective-permute-done | bytes 131104 | tf_op jit(solution)/shard_map/ppermute | solution.py:288
  91.5 4.3 %collective-permute-done.18.four_ref = bf16[128,512]{1,0:T(8,128)(2,1)S(1)} collective-permute-done((bf16[128,512]{1,0:T(8,128)(2,1)S(1)}, bf16[128,512]{1,0:T(8,128)(2,1)S(1)}, u32[]{:S(2)}, u32[]{:S(2)}) %collective-permute-start.18) | collective-permute-done | bytes 131104 | tf_op jit(solution)/shard_map/ppermute | solution.py:288
  98.2 3.8 %all-to-all-start.1 = ((bf16[4,688,128]{2,1,0:T(8,128)(2,1)}), bf16[4,688,128]{2,1,0:T(8,128)(2,1)S(1)}, u32[]{:S(2)}, u32[]{:S(2)}) async-start(bf16[4,688,128]{2,1,0:T(8,128)(2,1)} %copy-done.7), calls=%async_computation.1 | async-start | bytes 1409024 | tf_op jit(solution)/shard_map/all_to_all | solution.py:411
  102.0 4.9 %collective-permute-start.6 = (bf16[128,512]{1,0:T(8,128)(2,1)S(1)}, bf16[128,512]{1,0:T(8,128)(2,1)S(1)}, u32[]{:S(2)}, u32[]{:S(2)}) collective-permute-start(bf16[128,512]{1,0:T(8,128)(2,1)S(1)} %get-tuple-element.28.kv_ref.own), channel_id=1, source_target_pairs={{0,16},{4,20},{8,24},{12,28},{16,32},{20,36},{24,40},{28,44},{32,4... | collective-permute-start | bytes 393224 | tf_op jit(solution)/shard_map/ppermute | solution.py:288
  106.9 10.1 %collective-permute-start.5 = (bf16[128,512]{1,0:T(8,128)(2,1)S(1)}, bf16[128,512]{1,0:T(8,128)(2,1)S(1)}, u32[]{:S(2)}, u32[]{:S(2)}) collective-permute-start(bf16[128,512]{1,0:T(8,128)(2,1)S(1)} %get-tuple-element.28.kv_ref.own), channel_id=1, source_target_pairs={{0,8},{4,12},{8,16},{12,20},{16,24},{20,28},{24,32},{28,36},{32,40... | collective-permute-start | bytes 393224 | tf_op jit(solution)/shard_map/ppermute | solution.py:288
  117.6 1.9 %collective-permute-start.7 = (bf16[128,512]{1,0:T(8,128)(2,1)S(1)}, bf16[128,512]{1,0:T(8,128)(2,1)S(1)}, u32[]{:S(2)}, u32[]{:S(2)}) collective-permute-start(bf16[128,512]{1,0:T(8,128)(2,1)S(1)} %shard_map.133), channel_id=1, source_target_pairs={{0,4},{4,0},{8,12},{12,8},{16,20},{20,16},{24,28},{28,24},{32,36},... | collective-permute-start | bytes 393224 | tf_op jit(solution)/shard_map/ppermute | solution.py:293
  119.5 7.5 %collective-permute-done.5.two = bf16[128,512]{1,0:T(8,128)(2,1)S(1)} collective-permute-done((bf16[128,512]{1,0:T(8,128)(2,1)S(1)}, bf16[128,512]{1,0:T(8,128)(2,1)S(1)}, u32[]{:S(2)}, u32[]{:S(2)}) %collective-permute-start.5) | collective-permute-done | bytes 131104 | tf_op jit(solution)/shard_map/ppermute | solution.py:288
  127.1 1.9 %collective-permute-start.8 = (bf16[128,512]{1,0:T(8,128)(2,1)S(1)}, bf16[128,512]{1,0:T(8,128)(2,1)S(1)}, u32[]{:S(2)}, u32[]{:S(2)}) collective-permute-start(bf16[128,512]{1,0:T(8,128)(2,1)S(1)} %collective-permute-done.5.two), channel_id=1, source_target_pairs={{0,4},{4,0},{8,12},{12,8},{16,20},{20,16},{24,28},{28,24},{32,36},... | collective-permute-start | bytes 393224 | tf_op jit(solution)/shard_map/ppermute | solution.py:293
  130.3 1.8 %copy-done.6 = bf16[1,512,2688]{2,1,0:T(8,128)(2,1)S(1)} copy-done((bf16[1,512,2688]{2,1,0:T(8,128)(2,1)S(1)}, bf16[1,512,2688]{2,1,0:T(8,128)(2,1)}, u32[]{:S(2)}) %copy-start.6) | copy-done | bytes 2752536
  132.1 2.9 %shard_map.134 = (bf16[672,128]{1,0:T(8,128)(2,1)S(1)}, bf16[672,128]{1,0:T(8,128)(2,1)S(1)}, bf16[672,128]{1,0:T(8,128)(2,1)S(1)}, bf16[672,128]{1,0:T(8,128)(2,1)S(1)}) custom-call(s32[5]{0:T(128)S(1)} %stack.31.info_ref, s32[32,128]{1,0:T(8,128)S(1)} %bitcast.44, bf16[128,512]{1,0:T(8,128)(2,1)S(1)} %get-tuple-element.27.q_ref, ...), custom_call_target="tpu_custom_call" | custom-call | bytes 13200000 | tf_op jit(solution)/shard_map/pallas_call | solution.py:398
  135.0 3.6 %collective-permute-start.9 = (bf16[672,128]{1,0:T(8,128)(2,1)S(1)}, bf16[672,128]{1,0:T(8,128)(2,1)S(1)}, u32[]{:S(2)}, u32[]{:S(2)}) collective-permute-start(bf16[672,128]{1,0:T(8,128)(2,1)S(1)} %get-tuple-element.30), channel_id=1, source_target_pairs={{0,1},{1,2},{2,3},{3,0},{4,5},{5,6},{6,7},{7,4},{8,9},{9,10},{10,1... | collective-permute-start | bytes 516104 | tf_op jit(solution)/shard_map/ppermute | solution.py:307
  138.6 3.5 %collective-permute-start.10 = (bf16[672,128]{1,0:T(8,128)(2,1)S(1)}, bf16[672,128]{1,0:T(8,128)(2,1)S(1)}, u32[]{:S(2)}, u32[]{:S(2)}) collective-permute-start(bf16[672,128]{1,0:T(8,128)(2,1)S(1)} %get-tuple-element.31), channel_id=1, source_target_pairs={{0,3},{1,0},{2,1},{3,2},{4,7},{5,4},{6,5},{7,6},{8,11},{9,8},{10,9... | collective-permute-start | bytes 516104 | tf_op jit(solution)/shard_map/ppermute | solution.py:307
  142.0 3.9 %collective-permute-start.11 = (bf16[672,128]{1,0:T(8,128)(2,1)S(1)}, bf16[672,128]{1,0:T(8,128)(2,1)S(1)}, u32[]{:S(2)}, u32[]{:S(2)}) collective-permute-start(bf16[672,128]{1,0:T(8,128)(2,1)S(1)} %get-tuple-element.32), channel_id=1, source_target_pairs={{0,2},{1,3},{2,0},{3,1},{4,6},{5,7},{6,4},{7,5},{8,10},{9,11},{10,... | collective-permute-start | bytes 516104 | tf_op jit(solution)/shard_map/ppermute | solution.py:307
  147.0 4.3 %collective-permute-done.11.far = bf16[672,128]{1,0:T(8,128)(2,1)S(1)} collective-permute-done((bf16[672,128]{1,0:T(8,128)(2,1)S(1)}, bf16[672,128]{1,0:T(8,128)(2,1)S(1)}, u32[]{:S(2)}, u32[]{:S(2)}) %collective-permute-start.11) | collective-permute-done | bytes 172064 | tf_op jit(solution)/shard_map/ppermute | solution.py:307
  (60 shorter events, 20.3 us)
Async XLA Ops:
  0.6 32.6 %copy-start = (bf16[1,2688,512]{2,1,0:T(8,128)(2,1)S(1)}, bf16[1,2688,512]{2,1,0:T(8,128)(2,1)}, u32[]{:S(2)}) copy-start(bf16[1,2688,512]{2,1,0:T(8,128)(2,1)} %param.18) | copy-start | bytes 8257540
  2.7 30.5 %all-to-all-start = ((bf16[4,672,128]{2,1,0:T(8,128)(2,1)}), bf16[4,672,128]{2,1,0:T(8,128)(2,1)}, u32[]{:S(2)}, u32[]{:S(2)}) async-start(bf16[4,672,128]{2,1,0:T(8,128)(2,1)} %spread.1), calls=%async_computation | async-start | bytes 1376256 | tf_op jit(solution)/shard_map/all_to_all | solution.py:360
  7.0 8.1 %collective-permute-start = (bf16[672,128]{1,0:T(8,128)(2,1)}, bf16[672,128]{1,0:T(8,128)(2,1)S(1)}, u32[]{:S(2)}, u32[]{:S(2)}) collective-permute-start(bf16[672,128]{1,0:T(8,128)(2,1)} %bitcast.47), channel_id=1, source_target_pairs={{0,128},{128,256},{256,384},{384,512},{512,640},{1,129},{129,257},... | collective-permute-start | bytes 516104 | tf_op jit(solution)/shard_map/ppermute | solution.py:299
  11.3 8.5 %collective-permute-start.1 = (bf16[672,128]{1,0:T(8,128)(2,1)}, bf16[672,128]{1,0:T(8,128)(2,1)S(1)}, u32[]{:S(2)}, u32[]{:S(2)}) collective-permute-start(bf16[672,128]{1,0:T(8,128)(2,1)} %bitcast.48), channel_id=1, source_target_pairs={{128,0},{256,128},{384,256},{512,384},{640,512},{129,1},{257,129},... | collective-permute-start | bytes 516104 | tf_op jit(solution)/shard_map/ppermute | solution.py:299
  22.3 42.0 %collective-permute-start.2 = (bf16[1344,128]{1,0:T(8,128)(2,1)S(1)}, bf16[1344,128]{1,0:T(8,128)(2,1)S(1)}, u32[]{:S(2)}, u32[]{:S(2)}) collective-permute-start(bf16[1344,128]{1,0:T(8,128)(2,1)S(1)} %shard_map.131.own.both_ref), channel_id=1, source_target_pairs={{0,1},{1,2},{2,3},{3,0},{4,5},{5,6},{6,7},{7,4},{8,9},{9,10},{10,1... | collective-permute-start | bytes 1032200 | tf_op jit(solution)/shard_map/ppermute | solution.py:307
  25.9 39.2 %collective-permute-start.3 = (bf16[1344,128]{1,0:T(8,128)(2,1)S(1)}, bf16[1344,128]{1,0:T(8,128)(2,1)}, u32[]{:S(2)}, u32[]{:S(2)}) collective-permute-start(bf16[1344,128]{1,0:T(8,128)(2,1)S(1)} %shard_map.131.own.both_ref), channel_id=1, source_target_pairs={{0,3},{1,0},{2,1},{3,2},{4,7},{5,4},{6,5},{7,6},{8,11},{9,8},{10,9... | collective-permute-start | bytes 1032200 | tf_op jit(solution)/shard_map/ppermute | solution.py:307
  29.3 35.7 %collective-permute-start.4 = (bf16[1344,128]{1,0:T(8,128)(2,1)S(1)}, bf16[1344,128]{1,0:T(8,128)(2,1)}, u32[]{:S(2)}, u32[]{:S(2)}) collective-permute-start(bf16[1344,128]{1,0:T(8,128)(2,1)S(1)} %shard_map.131.own.both_ref), channel_id=1, source_target_pairs={{0,2},{1,3},{2,0},{3,1},{4,6},{5,7},{6,4},{7,5},{8,10},{9,11},{10,... | collective-permute-start | bytes 1032200 | tf_op jit(solution)/shard_map/ppermute | solution.py:307
  33.3 1.3 copy-start.1
  34.6 1.3 copy-start.3
  36.6 28.4 %copy-start.2 = (bf16[1,2688,256]{2,1,0:T(8,128)(2,1)S(1)}, bf16[1,2688,256]{2,1,0:T(8,128)(2,1)}, u32[]{:S(2)}) copy-start(bf16[1,2688,256]{2,1,0:T(8,128)(2,1)} %param.19) | copy-start | bytes 4128772
  36.6 28.4 %copy-start.4 = (bf16[1,2688,256]{2,1,0:T(8,128)(2,1)S(1)}, bf16[1,2688,256]{2,1,0:T(8,128)(2,1)}, u32[]{:S(2)}) copy-start(bf16[1,2688,256]{2,1,0:T(8,128)(2,1)} %param.20) | copy-start | bytes 4128772
  36.6 28.4 %copy-start.5 = (bf16[1,512,2688]{2,1,0:T(8,128)(2,1)S(1)}, bf16[1,512,2688]{2,1,0:T(8,128)(2,1)}, u32[]{:S(2)}) copy-start(bf16[1,512,2688]{2,1,0:T(8,128)(2,1)} %param.21) | copy-start | bytes 8257540
  39.1 18.9 %collective-permute-start.13 = (bf16[128,512]{1,0:T(8,128)(2,1)S(1)}, bf16[128,512]{1,0:T(8,128)(2,1)S(1)}, u32[]{:S(2)}, u32[]{:S(2)}) collective-permute-start(bf16[128,512]{1,0:T(8,128)(2,1)S(1)} %get-tuple-element.36.kv_ref.own), channel_id=1, source_target_pairs={{0,16},{4,20},{8,24},{12,28},{16,32},{20,36},{24,40},{28,44},{32,4... | collective-permute-start | bytes 393224 | tf_op jit(solution)/shard_map/ppermute | solution.py:288
  43.8 18.6 %collective-permute-start.12 = (bf16[128,512]{1,0:T(8,128)(2,1)S(1)}, bf16[128,512]{1,0:T(8,128)(2,1)S(1)}, u32[]{:S(2)}, u32[]{:S(2)}) collective-permute-start(bf16[128,512]{1,0:T(8,128)(2,1)S(1)} %get-tuple-element.36.kv_ref.own), channel_id=1, source_target_pairs={{0,8},{4,12},{8,16},{12,20},{16,24},{20,28},{24,32},{28,36},{32,40... | collective-permute-start | bytes 393224 | tf_op jit(solution)/shard_map/ppermute | solution.py:288
  58.6 10.6 %collective-permute-start.14 = (bf16[128,512]{1,0:T(8,128)(2,1)S(1)}, bf16[128,512]{1,0:T(8,128)(2,1)S(1)}, u32[]{:S(2)}, u32[]{:S(2)}) collective-permute-start(bf16[128,512]{1,0:T(8,128)(2,1)S(1)} %shard_map.137), channel_id=1, source_target_pairs={{0,4},{4,0},{8,12},{12,8},{16,20},{20,16},{24,28},{28,24},{32,36},... | collective-permute-start | bytes 393224 | tf_op jit(solution)/shard_map/ppermute | solution.py:293
  62.4 6.9 %collective-permute-start.15 = (bf16[128,512]{1,0:T(8,128)(2,1)S(1)}, bf16[128,512]{1,0:T(8,128)(2,1)S(1)}, u32[]{:S(2)}, u32[]{:S(2)}) collective-permute-start(bf16[128,512]{1,0:T(8,128)(2,1)S(1)} %collective-permute-done.12.two), channel_id=1, source_target_pairs={{0,4},{4,0},{8,12},{12,8},{16,20},{20,16},{24,28},{28,24},{32,36},... | collective-permute-start | bytes 393224 | tf_op jit(solution)/shard_map/ppermute | solution.py:293
  66.1 3.3 %copy-start.16 = (s32[1,4096]{1,0:T(1,128)S(1)}, s32[1,4096]{1,0:T(1,128)}, u32[]{:S(2)}) copy-start(s32[1,4096]{1,0:T(1,128)} %param.23) | copy-start | bytes 49156
  72.4 3.6 %collective-permute-start.16 = (bf16[256,512]{1,0:T(8,128)(2,1)S(1)}, bf16[256,512]{1,0:T(8,128)(2,1)S(1)}, u32[]{:S(2)}, u32[]{:S(2)}) collective-permute-start(bf16[256,512]{1,0:T(8,128)(2,1)S(1)} %get-tuple-element.41), channel_id=1, source_target_pairs={{0,4},{4,0},{8,12},{12,8},{16,20},{20,16},{24,28},{28,24},{32,36},... | collective-permute-start | bytes 786440 | tf_op jit(solution)/shard_map/ppermute | solution.py:293
  76.6 14.9 %collective-permute-start.17 = (bf16[128,512]{1,0:T(8,128)(2,1)S(1)}, bf16[128,512]{1,0:T(8,128)(2,1)S(1)}, u32[]{:S(2)}, u32[]{:S(2)}) collective-permute-start(bf16[128,512]{1,0:T(8,128)(2,1)S(1)} %get-tuple-element.43), channel_id=1, source_target_pairs={{8,0},{12,4},{16,8},{20,12},{24,16},{28,20},{32,24},{36,28},{40,32... | collective-permute-start | bytes 393224 | tf_op jit(solution)/shard_map/ppermute | solution.py:288
  87.2 8.6 %collective-permute-start.18 = (bf16[128,512]{1,0:T(8,128)(2,1)S(1)}, bf16[128,512]{1,0:T(8,128)(2,1)S(1)}, u32[]{:S(2)}, u32[]{:S(2)}) collective-permute-start(bf16[128,512]{1,0:T(8,128)(2,1)S(1)} %get-tuple-element.44), channel_id=1, source_target_pairs={{16,0},{20,4},{24,8},{28,12},{32,16},{36,20},{40,24},{44,28},{48,3... | collective-permute-start | bytes 393224 | tf_op jit(solution)/shard_map/ppermute | solution.py:288
  95.8 34.5 %copy-start.17 = (s32[1,4096]{1,0:T(1,128)S(1)}, s32[1,4096]{1,0:T(1,128)}, u32[]{:S(2)}) copy-start(s32[1,4096]{1,0:T(1,128)} %param.22) | copy-start | bytes 49156
  98.2 47.7 %copy-start.15 = (f32[1,2688]{1,0:T(1,128)S(1)}, f32[1,2688]{1,0:T(1,128)}, u32[]{:S(2)}) copy-start(f32[1,2688]{1,0:T(1,128)} %gain_ref.5) | copy-start | bytes 32260
  98.2 53.8 %all-to-all-start.1 = ((bf16[4,688,128]{2,1,0:T(8,128)(2,1)}), bf16[4,688,128]{2,1,0:T(8,128)(2,1)S(1)}, u32[]{:S(2)}, u32[]{:S(2)}) async-start(bf16[4,688,128]{2,1,0:T(8,128)(2,1)} %copy-done.7), calls=%async_computation.1 | async-start | bytes 1409024 | tf_op jit(solution)/shard_map/all_to_all | solution.py:411
  102.0 50.1 %copy-start.9 = (bf16[1,128,672]{1,2,0:T(8,128)(2,1)S(1)}, bf16[1,128,672]{1,2,0:T(8,128)(2,1)}, u32[]{:S(2)}) copy-start(bf16[1,128,672]{1,2,0:T(8,128)(2,1)} %param.14) | copy-start | bytes 516100
  102.0 15.0 %collective-permute-start.6 = (bf16[128,512]{1,0:T(8,128)(2,1)S(1)}, bf16[128,512]{1,0:T(8,128)(2,1)S(1)}, u32[]{:S(2)}, u32[]{:S(2)}) collective-permute-start(bf16[128,512]{1,0:T(8,128)(2,1)S(1)} %get-tuple-element.28.kv_ref.own), channel_id=1, source_target_pairs={{0,16},{4,20},{8,24},{12,28},{16,32},{20,36},{24,40},{28,44},{32,4... | collective-permute-start | bytes 393224 | tf_op jit(solution)/shard_map/ppermute | solution.py:288
  106.9 20.2 %collective-permute-start.5 = (bf16[128,512]{1,0:T(8,128)(2,1)S(1)}, bf16[128,512]{1,0:T(8,128)(2,1)S(1)}, u32[]{:S(2)}, u32[]{:S(2)}) collective-permute-start(bf16[128,512]{1,0:T(8,128)(2,1)S(1)} %get-tuple-element.28.kv_ref.own), channel_id=1, source_target_pairs={{0,8},{4,12},{8,16},{12,20},{16,24},{20,28},{24,32},{28,36},{32,40... | collective-permute-start | bytes 393224 | tf_op jit(solution)/shard_map/ppermute | solution.py:288
  117.6 11.4 %collective-permute-start.7 = (bf16[128,512]{1,0:T(8,128)(2,1)S(1)}, bf16[128,512]{1,0:T(8,128)(2,1)S(1)}, u32[]{:S(2)}, u32[]{:S(2)}) collective-permute-start(bf16[128,512]{1,0:T(8,128)(2,1)S(1)} %shard_map.133), channel_id=1, source_target_pairs={{0,4},{4,0},{8,12},{12,8},{16,20},{20,16},{24,28},{28,24},{32,36},... | collective-permute-start | bytes 393224 | tf_op jit(solution)/shard_map/ppermute | solution.py:293
  127.1 3.2 %collective-permute-start.8 = (bf16[128,512]{1,0:T(8,128)(2,1)S(1)}, bf16[128,512]{1,0:T(8,128)(2,1)S(1)}, u32[]{:S(2)}, u32[]{:S(2)}) collective-permute-start(bf16[128,512]{1,0:T(8,128)(2,1)S(1)} %collective-permute-done.5.two), channel_id=1, source_target_pairs={{0,4},{4,0},{8,12},{12,8},{16,20},{20,16},{24,28},{28,24},{32,36},... | collective-permute-start | bytes 393224 | tf_op jit(solution)/shard_map/ppermute | solution.py:293
  130.3 1.8 %copy-start.6 = (bf16[1,512,2688]{2,1,0:T(8,128)(2,1)S(1)}, bf16[1,512,2688]{2,1,0:T(8,128)(2,1)}, u32[]{:S(2)}) copy-start(bf16[1,512,2688]{2,1,0:T(8,128)(2,1)} %param.21) | copy-start | bytes 8257540
  135.0 12.0 %collective-permute-start.9 = (bf16[672,128]{1,0:T(8,128)(2,1)S(1)}, bf16[672,128]{1,0:T(8,128)(2,1)S(1)}, u32[]{:S(2)}, u32[]{:S(2)}) collective-permute-start(bf16[672,128]{1,0:T(8,128)(2,1)S(1)} %get-tuple-element.30), channel_id=1, source_target_pairs={{0,1},{1,2},{2,3},{3,0},{4,5},{5,6},{6,7},{7,4},{8,9},{9,10},{10,1... | collective-permute-start | bytes 516104 | tf_op jit(solution)/shard_map/ppermute | solution.py:307
  138.6 8.4 %collective-permute-start.10 = (bf16[672,128]{1,0:T(8,128)(2,1)S(1)}, bf16[672,128]{1,0:T(8,128)(2,1)S(1)}, u32[]{:S(2)}, u32[]{:S(2)}) collective-permute-start(bf16[672,128]{1,0:T(8,128)(2,1)S(1)} %get-tuple-element.31), channel_id=1, source_target_pairs={{0,3},{1,0},{2,1},{3,2},{4,7},{5,4},{6,5},{7,6},{8,11},{9,8},{10,9... | collective-permute-start | bytes 516104 | tf_op jit(solution)/shard_map/ppermute | solution.py:307
  142.0 9.3 %collective-permute-start.11 = (bf16[672,128]{1,0:T(8,128)(2,1)S(1)}, bf16[672,128]{1,0:T(8,128)(2,1)S(1)}, u32[]{:S(2)}, u32[]{:S(2)}) collective-permute-start(bf16[672,128]{1,0:T(8,128)(2,1)S(1)} %get-tuple-element.32), channel_id=1, source_target_pairs={{0,2},{1,3},{2,0},{3,1},{4,6},{5,7},{6,4},{7,5},{8,10},{9,11},{10,... | collective-permute-start | bytes 516104 | tf_op jit(solution)/shard_map/ppermute | solution.py:307
  (7 other events, 6.2 us)

commit v5 on v4

--- a/solution.py
+++ b/solution.py
@@ -176,9 +176,8 @@
     return jnp.concatenate([block[:, start : start + HEAD] for block in blocks], axis=0)
 
 
-def attend_body(info_ref, docs_ref, q_ref, own, two, four, mid, late, wo_ref, *outs):
+def attend_body(info_ref, docs_ref, q_ref, own, two, four, mid, late, wo_ref, out_ref):
     length = q_ref.shape[0]
-    hold_ref = outs[4]
     kv_heads = own.shape[1] // (2 * HEAD)
     groups = q_ref.shape[1] // HEAD // kv_heads
     bias = window_mask(info_ref, docs_ref, length)
@@ -194,10 +193,7 @@
             heads.append(dot_nn(probs, values).astype(BF))
     mixed = jnp.concatenate(heads, axis=1)
     whole = jnp.transpose(dot_nn(mixed, wo_ref[...]).astype(BF))
-    hold_ref[...] = whole.reshape(hold_ref.shape)
-    parts = hold_ref.shape[0]
-    for out_ref, offset in zip(outs, SENDS):
-        out_ref[...] = hold_ref[lax.rem(info_ref[2] + offset, parts)]
+    out_ref[...] = whole.reshape(out_ref.shape)
 
 
 def attend_back_body(
@@ -236,10 +232,11 @@
 
 
 def input_terms_body(
-    dq_ref, own_ref, two_ref, four_ref, q_ref, kv_ref, wk_ref, wv_ref, wq_ref, out_ref
+    dq_ref, own_ref, two_ref, four_ref, q_ref, kv_ref, front_ref, wk_ref, wv_ref, wq_ref, out_ref
 ):
     parts, rows, length = out_ref.shape
     share = wq_ref.shape[0] // parts
+    out_ref[:, :share, :] = front_ref[...]
     half = own_ref.shape[1] // 2
     total = own_ref[...] + two_ref[...].astype(F32) + four_ref[...].astype(F32)
     d_key = (total[:, :half] * SCALE).astype(BF)
@@ -248,38 +245,30 @@
     row = jnp.sum(q_ref[...].astype(F32) * d_query.astype(F32), axis=1, keepdims=True)
     keys = kv_ref[:, :half].astype(F32) * d_key.astype(F32)
     values = kv_ref[:, half:].astype(F32) * d_value.astype(F32)
-    row = across(row + jnp.sum(keys + values, axis=1, keepdims=True))[: rows - share]
+    row = across(row + jnp.sum(keys + values, axis=1, keepdims=True))[: rows - 2 * share]
     high = row.astype(BF).astype(F32)
-    first = lax.broadcasted_iota(jnp.int32, (rows - share, length), 0) == 0
+    first = lax.broadcasted_iota(jnp.int32, (rows - 2 * share, length), 0) == 0
     pair = jnp.where(first, high, row - high).astype(BF)
     for part in range(parts):
         span = slice(part * share, (part + 1) * share)
         d_norm = dot_nt(wq_ref[span], d_query)
         d_norm = d_norm + dot_nt(wk_ref[span], d_key)
         d_norm = d_norm + dot_nt(wv_ref[span], d_value)
-        out_ref[part, :share] = d_norm.astype(BF)
-        out_ref[part, share:] = pair
-
-
-def total_of(refs):
-    return sum(ref[...].astype(F32) for ref in refs)
-
-
-def finish_front_body(own, one, minus, far, both_ref, out_ref):
-    share = out_ref.shape[0]
-    total = total_of((own, one, minus, far))
-    out_ref[...] = (both_ref[:share].astype(F32) + total).astype(BF)
-
-
-def finish_body(sums_ref, x_ref, both_ref, gain_ref, r_ref, out_ref):
+        out_ref[part, share : 2 * share] = d_norm.astype(BF)
+        out_ref[part, 2 * share :] = pair
+
+
+def finish_body(sums_ref, x_ref, both_ref, gain_ref, r_ref, front_ref, back_ref):
     share = x_ref.shape[0]
     parts = sums_ref.shape[0]
     total = sum(sums_ref[part].astype(F32) for part in range(parts))
-    row = (total[share : share + 1] + total[share + 1 : share + 2]) / (parts * share)
+    front_ref[...] = (both_ref[:share].astype(F32) + total[:share]).astype(BF)
+    last = 2 * share
+    row = (total[last : last + 1] + total[last + 1 : last + 2]) / (parts * share)
     factor = jnp.transpose(r_ref[...])[:1]
-    d_input = factor * gain_ref[...] * total[:share]
+    d_input = factor * gain_ref[...] * total[share:last]
     d_input = d_input - x_ref[...].astype(F32) * (factor * factor * row)
-    out_ref[...] = (both_ref[share:].astype(F32) + d_input).astype(BF)
+    back_ref[...] = (both_ref[share:].astype(F32) + d_input).astype(BF)
 
 
 def shifted(value, steps):
@@ -396,22 +385,17 @@
     back_four = shifted(send_four, -4)
 
     partial_out = kernel(
-        attend_body, LIMIT, (rows(share, length),) * 4, [smem()] + vmem(8),
-        scratch=[pieces(share)],
+        attend_body, LIMIT, jax.ShapeDtypeStruct((parts, share, length), BF),
+        [smem()] + vmem(8),
     )(info, docs_front, q_front, *blocks_front, wo)
-    sums = exchanged(partial_out[1:])
-    forward_out = kernel(finish_front_body, 8, rows(share, length), vmem(5), 1.0)(
-        partial_out[0], *sums, sent
-    )
-
-    d_parts = kernel(
+    partial_sums = kernel(
         input_terms_body, LIMIT,
-        jax.ShapeDtypeStruct((parts, share + 16, length), BF), vmem(9),
-    )(d_query, t_own, back_two, back_four, q_back, kv_back, wk, wv, wq)
-    d_parts = lax.all_to_all(d_parts, "fsdp", 0, 0)
-    input_grad = kernel(finish_body, 8, rows(share, length), vmem(5), 1.0)(
-        d_parts, stash, sent, own_gain, factor
-    )
+        jax.ShapeDtypeStruct((parts, 2 * share + 16, length), BF), vmem(10),
+    )(d_query, t_own, back_two, back_four, q_back, kv_back, partial_out, wk, wv, wq)
+    partial_sums = lax.all_to_all(partial_sums, "fsdp", 0, 0)
+    forward_out, input_grad = kernel(
+        finish_body, 8, (rows(share, length), rows(share, length)), vmem(5), 1.0
+    )(partial_sums, stash, sent, own_gain, factor)
     return (forward_out.T[None], input_grad.T[None])
 
 

time: 154 us -> 143 us (0.929)
  the two profiles are of different devices: /device:TPU:24 before, /device:TPU:32 now
where the time goes in v5:
time: 143 us
  starting transfers between devices  81.3 us (57%)
  waiting for transfers between devices  34.9 us (24%)
  Pallas kernels  18.7 us (13%)
  local copies, waits for them, and re-layouts  6.67 us (5%)
    ppermute x6, starting transfers between devices, shifted(): return lax.ppermute(value, 'seq', pairs)  46.6 us
    all_to_all x1, waiting for transfers between devices, step(): partial_sums = lax.all_to_all(partial_sums, 'fsdp', 0, 0)  18 us
    ppermute x3, starting transfers between devices, exchanged(): received.append(lax.ppermute(value, 'fsdp', pairs))  10.9 us
    ppermute x5, starting transfers between devices, swapped(): return lax.ppermute(value, 'seq', [(s, s ^ 1) for s in range(count)])  10.1 us
    ppermute x6, waiting for transfers between devices, shifted(): return lax.ppermute(value, 'seq', pairs)  9.67 us
    ppermute x2, waiting for transfers between devices, next_section(): return lax.ppermute(value, 'pipe', pairs)  7.17 us
    unnamed x28, local copies, waits for them, and re-layouts  6.58 us
    ppermute x2, starting transfers between devices, next_section(): return lax.ppermute(value, 'pipe', pairs)  5.57 us
  transfers between devices with their start and end apart: 18, of which 6 were waited for; matrix products, arithmetic and copies ran while one was open for 0% of the time, Pallas kernels for 8%

profile of v5, /device:TPU:32, one launch (start us, length us, event | category | flops | bytes accessed | tf_op | source)
XLA Modules:
  0.0 142.6 jit_solution(2859393370880456429)
XLA Ops:
  2.6 4.4 %all-to-all-start = ((bf16[4,672,128]{2,1,0:T(8,128)(2,1)}), bf16[4,672,128]{2,1,0:T(8,128)(2,1)}, u32[]{:S(2)}, u32[]{:S(2)}) async-start(bf16[4,672,128]{2,1,0:T(8,128)(2,1)} %spread.1), calls=%async_computation | async-start | bytes 1376256 | tf_op jit(solution)/shard_map/all_to_all | solution.py:349
  7.0 4.3 %collective-permute-start = (bf16[672,128]{1,0:T(8,128)(2,1)}, bf16[672,128]{1,0:T(8,128)(2,1)S(1)}, u32[]{:S(2)}, u32[]{:S(2)}) collective-permute-start(bf16[672,128]{1,0:T(8,128)(2,1)} %bitcast.45), channel_id=1, source_target_pairs={{0,128},{128,256},{256,384},{384,512},{512,640},{1,129},{129,257},... | collective-permute-start | bytes 516104 | tf_op jit(solution)/shard_map/ppermute | solution.py:288
  11.3 1.3 collective-permute-start.1
  12.6 2.5 %collective-permute-done.arr_ref = bf16[672,128]{1,0:T(8,128)(2,1)S(1)} collective-permute-done((bf16[672,128]{1,0:T(8,128)(2,1)}, bf16[672,128]{1,0:T(8,128)(2,1)S(1)}, u32[]{:S(2)}, u32[]{:S(2)}) %collective-permute-start) | collective-permute-done | bytes 172064 | tf_op jit(solution)/shard_map/ppermute | solution.py:288
  15.1 4.7 %collective-permute-done.1.ret_ref = bf16[672,128]{1,0:T(8,128)(2,1)S(1)} collective-permute-done((bf16[672,128]{1,0:T(8,128)(2,1)}, bf16[672,128]{1,0:T(8,128)(2,1)S(1)}, u32[]{:S(2)}, u32[]{:S(2)}) %collective-permute-start.1) | collective-permute-done | bytes 172064 | tf_op jit(solution)/shard_map/ppermute | solution.py:288
  22.3 3.6 %collective-permute-start.2 = (bf16[1344,128]{1,0:T(8,128)(2,1)S(1)}, bf16[1344,128]{1,0:T(8,128)(2,1)S(1)}, u32[]{:S(2)}, u32[]{:S(2)}) collective-permute-start(bf16[1344,128]{1,0:T(8,128)(2,1)S(1)} %shard_map.132.own.both_ref), channel_id=1, source_target_pairs={{0,1},{1,2},{2,3},{3,0},{4,5},{5,6},{6,7},{7,4},{8,9},{9,10},{10,1... | collective-permute-start | bytes 1032200 | tf_op jit(solution)/shard_map/ppermute | solution.py:296
  25.9 3.5 %collective-permute-start.3 = (bf16[1344,128]{1,0:T(8,128)(2,1)S(1)}, bf16[1344,128]{1,0:T(8,128)(2,1)}, u32[]{:S(2)}, u32[]{:S(2)}) collective-permute-start(bf16[1344,128]{1,0:T(8,128)(2,1)S(1)} %shard_map.132.own.both_ref), channel_id=1, source_target_pairs={{0,3},{1,0},{2,1},{3,2},{4,7},{5,4},{6,5},{7,6},{8,11},{9,8},{10,9... | collective-permute-start | bytes 1032200 | tf_op jit(solution)/shard_map/ppermute | solution.py:296
  29.3 3.9 %collective-permute-start.4 = (bf16[1344,128]{1,0:T(8,128)(2,1)S(1)}, bf16[1344,128]{1,0:T(8,128)(2,1)}, u32[]{:S(2)}, u32[]{:S(2)}) collective-permute-start(bf16[1344,128]{1,0:T(8,128)(2,1)S(1)} %shard_map.132.own.both_ref), channel_id=1, source_target_pairs={{0,2},{1,3},{2,0},{3,1},{4,6},{5,7},{6,4},{7,5},{8,10},{9,11},{10,... | collective-permute-start | bytes 1032200 | tf_op jit(solution)/shard_map/ppermute | solution.py:296
  33.3 1.3 copy-done.1
  34.6 1.3 copy-done.3
  36.0 2.5 %shard_map.131 = (bf16[128,512]{1,0:T(8,128)(2,1)S(1)}, bf16[128,512]{1,0:T(8,128)(2,1)S(1)}, f32[128,128]{1,0:T(8,128)S(1)}) custom-call(bf16[4,672,128]{2,1,0:T(8,128)(2,1)} %all-to-all-done.x_ref, f32[1,2688]{1,0:T(1,128)S(1)} %copy-done.11, bf16[2688,256]{1,0:T(8,128)(2,1)S(1)} %bitcast.31, bf16[2688,256]{1,0:T(8,128)(2,1)S(1)} %bitcast.34, ...), custom_call_target="tpu_custom_call" | custom-call | bytes 13200000 | tf_op jit(solution)/shard_map/pallas_call | solution.py:355
  38.4 2.6 %collective-permute-start.6 = (bf16[128,512]{1,0:T(8,128)(2,1)S(1)}, bf16[128,512]{1,0:T(8,128)(2,1)S(1)}, u32[]{:S(2)}, u32[]{:S(2)}) collective-permute-start(bf16[128,512]{1,0:T(8,128)(2,1)S(1)} %get-tuple-element.28.kv_ref.own), channel_id=1, source_target_pairs={{0,16},{4,20},{8,24},{12,28},{16,32},{20,36},{24,40},{28,44},{32,4... | collective-permute-start | bytes 393224 | tf_op jit(solution)/shard_map/ppermute | solution.py:277
  41.0 14.2 %collective-permute-start.5 = (bf16[128,512]{1,0:T(8,128)(2,1)S(1)}, bf16[128,512]{1,0:T(8,128)(2,1)S(1)}, u32[]{:S(2)}, u32[]{:S(2)}) collective-permute-start(bf16[128,512]{1,0:T(8,128)(2,1)S(1)} %get-tuple-element.28.kv_ref.own), channel_id=1, source_target_pairs={{0,8},{4,12},{8,16},{12,20},{16,24},{20,28},{24,32},{28,36},{32,40... | collective-permute-start | bytes 393224 | tf_op jit(solution)/shard_map/ppermute | solution.py:277
  55.8 1.9 %collective-permute-start.7 = (bf16[128,512]{1,0:T(8,128)(2,1)S(1)}, bf16[128,512]{1,0:T(8,128)(2,1)S(1)}, u32[]{:S(2)}, u32[]{:S(2)}) collective-permute-start(bf16[128,512]{1,0:T(8,128)(2,1)S(1)} %shard_map.134), channel_id=1, source_target_pairs={{0,4},{4,0},{8,12},{12,8},{16,20},{20,16},{24,28},{28,24},{32,36},... | collective-permute-start | bytes 393224 | tf_op jit(solution)/shard_map/ppermute | solution.py:282
  57.8 2.6 %collective-permute-done.5.two = bf16[128,512]{1,0:T(8,128)(2,1)S(1)} collective-permute-done((bf16[128,512]{1,0:T(8,128)(2,1)S(1)}, bf16[128,512]{1,0:T(8,128)(2,1)S(1)}, u32[]{:S(2)}, u32[]{:S(2)}) %collective-permute-start.5) | collective-permute-done | bytes 131104 | tf_op jit(solution)/shard_map/ppermute | solution.py:277
  60.4 1.9 %collective-permute-start.8 = (bf16[128,512]{1,0:T(8,128)(2,1)S(1)}, bf16[128,512]{1,0:T(8,128)(2,1)S(1)}, u32[]{:S(2)}, u32[]{:S(2)}) collective-permute-start(bf16[128,512]{1,0:T(8,128)(2,1)S(1)} %collective-permute-done.5.two), channel_id=1, source_target_pairs={{0,4},{4,0},{8,12},{12,8},{16,20},{20,16},{24,28},{28,24},{32,36},... | collective-permute-start | bytes 393224 | tf_op jit(solution)/shard_map/ppermute | solution.py:282
  62.4 3.2 %shard_map.133 = (bf16[128,512]{1,0:T(8,128)(2,1)S(1)}, bf16[128,512]{1,0:T(8,128)(2,1)S(1)}, bf16[128,512]{1,0:T(8,128)(2,1)S(1)}) custom-call(s32[5]{0:T(128)S(1)} %stack.31.info_ref, bf16[1344,128]{1,0:T(8,128)(2,1)S(1)} %shard_map.132.own.both_ref, bf16[1344,128]{1,0:T(8,128)(2,1)S(1)} %collective-permute-done.2.one, ...), custom_call_target="tpu_custom_call" | custom-call | bytes 13200000 | tf_op jit(solution)/shard_map/pallas_call | solution.py:366
  65.7 3.1 %shard_map.135 = (bf16[128,512]{1,0:T(8,128)(2,1)S(1)}, f32[128,512]{1,0:T(8,128)S(1)}, f32[128,512]{1,0:T(8,128)S(1)}, f32[128,512]{1,0:T(8,128)S(1)}, bf16[256,512]{1,0:T(8,128)(2,1)S(1)}) custom-call(s32[5]{0:T(128)S(1)} %stack.31.info_ref, s32[32,128]{1,0:T(8,128)S(1)} %bitcast.43, bf16[128,512]{1,0:T(8,128)(2,1)S(1)} %get-tuple-element.24.q_ref, ...), custom_call_target="tpu_custom_call" | custom-call | bytes 13200000 | tf_op jit(solution)/shard_map/pallas_call | solution.py:374
  68.8 2.4 %collective-permute-start.9 = (bf16[256,512]{1,0:T(8,128)(2,1)S(1)}, bf16[256,512]{1,0:T(8,128)(2,1)S(1)}, u32[]{:S(2)}, u32[]{:S(2)}) collective-permute-start(bf16[256,512]{1,0:T(8,128)(2,1)S(1)} %get-tuple-element.33), channel_id=1, source_target_pairs={{0,4},{4,0},{8,12},{12,8},{16,20},{20,16},{24,28},{28,24},{32,36},... | collective-permute-start | bytes 786440 | tf_op jit(solution)/shard_map/ppermute | solution.py:282
  71.2 1.9 %collective-permute-start.13 = (bf16[128,512]{1,0:T(8,128)(2,1)S(1)}, bf16[128,512]{1,0:T(8,128)(2,1)S(1)}, u32[]{:S(2)}, u32[]{:S(2)}) collective-permute-start(bf16[128,512]{1,0:T(8,128)(2,1)S(1)} %get-tuple-element.38.kv_ref.own), channel_id=1, source_target_pairs={{0,16},{4,20},{8,24},{12,28},{16,32},{20,36},{24,40},{28,44},{32,4... | collective-permute-start | bytes 393224 | tf_op jit(solution)/shard_map/ppermute | solution.py:277
  73.1 10.6 %collective-permute-start.12 = (bf16[128,512]{1,0:T(8,128)(2,1)S(1)}, bf16[128,512]{1,0:T(8,128)(2,1)S(1)}, u32[]{:S(2)}, u32[]{:S(2)}) collective-permute-start(bf16[128,512]{1,0:T(8,128)(2,1)S(1)} %get-tuple-element.38.kv_ref.own), channel_id=1, source_target_pairs={{0,8},{4,12},{8,16},{12,20},{16,24},{20,28},{24,32},{28,36},{32,40... | collective-permute-start | bytes 393224 | tf_op jit(solution)/shard_map/ppermute | solution.py:277
  84.3 1.9 %collective-permute-start.14 = (bf16[128,512]{1,0:T(8,128)(2,1)S(1)}, bf16[128,512]{1,0:T(8,128)(2,1)S(1)}, u32[]{:S(2)}, u32[]{:S(2)}) collective-permute-start(bf16[128,512]{1,0:T(8,128)(2,1)S(1)} %shard_map.137), channel_id=1, source_target_pairs={{0,4},{4,0},{8,12},{12,8},{16,20},{20,16},{24,28},{28,24},{32,36},... | collective-permute-start | bytes 393224 | tf_op jit(solution)/shard_map/ppermute | solution.py:282
  86.2 3.1 %collective-permute-done.12.two = bf16[128,512]{1,0:T(8,128)(2,1)S(1)} collective-permute-done((bf16[128,512]{1,0:T(8,128)(2,1)S(1)}, bf16[128,512]{1,0:T(8,128)(2,1)S(1)}, u32[]{:S(2)}, u32[]{:S(2)}) %collective-permute-start.12) | collective-permute-done | bytes 131104 | tf_op jit(solution)/shard_map/ppermute | solution.py:277
  89.2 1.9 %collective-permute-start.15 = (bf16[128,512]{1,0:T(8,128)(2,1)S(1)}, bf16[128,512]{1,0:T(8,128)(2,1)S(1)}, u32[]{:S(2)}, u32[]{:S(2)}) collective-permute-start(bf16[128,512]{1,0:T(8,128)(2,1)S(1)} %collective-permute-done.12.two), channel_id=1, source_target_pairs={{0,4},{4,0},{8,12},{12,8},{16,20},{20,16},{24,28},{28,24},{32,36},... | collective-permute-start | bytes 393224 | tf_op jit(solution)/shard_map/ppermute | solution.py:282
  91.8 15.4 %collective-permute-start.10 = (bf16[128,512]{1,0:T(8,128)(2,1)S(1)}, bf16[128,512]{1,0:T(8,128)(2,1)S(1)}, u32[]{:S(2)}, u32[]{:S(2)}) collective-permute-start(bf16[128,512]{1,0:T(8,128)(2,1)S(1)} %get-tuple-element.35), channel_id=1, source_target_pairs={{8,0},{12,4},{16,8},{20,12},{24,16},{28,20},{32,24},{36,28},{40,32... | collective-permute-start | bytes 393224 | tf_op jit(solution)/shard_map/ppermute | solution.py:277
  107.2 1.9 %collective-permute-start.11 = (bf16[128,512]{1,0:T(8,128)(2,1)S(1)}, bf16[128,512]{1,0:T(8,128)(2,1)S(1)}, u32[]{:S(2)}, u32[]{:S(2)}) collective-permute-start(bf16[128,512]{1,0:T(8,128)(2,1)S(1)} %get-tuple-element.36), channel_id=1, source_target_pairs={{16,0},{20,4},{24,8},{28,12},{32,16},{36,20},{40,24},{44,28},{48,3... | collective-permute-start | bytes 393224 | tf_op jit(solution)/shard_map/ppermute | solution.py:277
  109.1 2.8 %shard_map.138.front_ref = bf16[4,672,128]{2,1,0:T(8,128)(2,1)S(1)} custom-call(s32[5]{0:T(128)S(1)} %stack.31.info_ref, s32[32,128]{1,0:T(8,128)S(1)} %bitcast.44, bf16[128,512]{1,0:T(8,128)(2,1)S(1)} %get-tuple-element.37.q_ref, bf16[128,512]{1,0:T(8,128)(2,1)S(1)} %get-tuple-element.38.kv_ref.own, bf16[128,512]{1,0:T(8,128)(2,1)S(1)} %collective-permute-done.12.two, ...), custom_call_target="tpu_custom_call" | custom-call | bytes 13200000 | tf_op jit(solution)/shard_map/pallas_call | solution.py:387
  112.0 4.0 %collective-permute-done.10.two_ref = bf16[128,512]{1,0:T(8,128)(2,1)S(1)} collective-permute-done((bf16[128,512]{1,0:T(8,128)(2,1)S(1)}, bf16[128,512]{1,0:T(8,128)(2,1)S(1)}, u32[]{:S(2)}, u32[]{:S(2)}) %collective-permute-start.10) | collective-permute-done | bytes 131104 | tf_op jit(solution)/shard_map/ppermute | solution.py:277
  116.0 1.6 %shard_map.139 = bf16[4,1360,128]{2,1,0:T(8,128)(2,1)S(1)} custom-call(bf16[128,512]{1,0:T(8,128)(2,1)S(1)} %get-tuple-element.29.dq_ref, f32[128,512]{1,0:T(8,128)S(1)} %get-tuple-element.34.own_ref, bf16[128,512]{1,0:T(8,128)(2,1)S(1)} %collective-permute-done.10.two_ref, bf16[128,512]{1,0:T(8,128)(2,1)S(1)} %collective-permute-done.11.four_ref, ...), custom_call_target="tpu_custom_call" | custom-call | bytes 13200000 | tf_op jit(solution)/shard_map/pallas_call | solution.py:391
  118.7 3.7 %all-to-all-start.1 = ((bf16[4,1360,128]{2,1,0:T(8,128)(2,1)}), bf16[4,1360,128]{2,1,0:T(8,128)(2,1)S(1)}, u32[]{:S(2)}, u32[]{:S(2)}) async-start(bf16[4,1360,128]{2,1,0:T(8,128)(2,1)} %copy-done.6), calls=%async_computation.1 | async-start | bytes 2785280 | tf_op jit(solution)/shard_map/all_to_all | solution.py:395
  123.4 18.0 %all-to-all-done.1.sums_ref = bf16[4,1360,128]{2,1,0:T(8,128)(2,1)S(1)} async-done(((bf16[4,1360,128]{2,1,0:T(8,128)(2,1)}), bf16[4,1360,128]{2,1,0:T(8,128)(2,1)S(1)}, u32[]{:S(2)}, u32[]{:S(2)}) %all-to-all-start.1) | async-done | bytes 1392672 | tf_op jit(solution)/shard_map/all_to_all | solution.py:395
  141.4 1.1 shard_map.141
  (45 shorter events, 8.3 us)
Async XLA Ops:
  0.6 32.6 %copy-start.11 = (f32[1,2688]{1,0:T(1,128)S(1)}, f32[1,2688]{1,0:T(1,128)}, u32[]{:S(2)}) copy-start(f32[1,2688]{1,0:T(1,128)} %gain_ref.5) | copy-start | bytes 32260
  0.7 0.9 copy-start.7
  1.7 31.6 %copy-start = (bf16[1,2688,512]{2,1,0:T(8,128)(2,1)S(1)}, bf16[1,2688,512]{2,1,0:T(8,128)(2,1)}, u32[]{:S(2)}) copy-start(bf16[1,2688,512]{2,1,0:T(8,128)(2,1)} %param.18) | copy-start | bytes 8257540
  2.6 30.6 %all-to-all-start = ((bf16[4,672,128]{2,1,0:T(8,128)(2,1)}), bf16[4,672,128]{2,1,0:T(8,128)(2,1)}, u32[]{:S(2)}, u32[]{:S(2)}) async-start(bf16[4,672,128]{2,1,0:T(8,128)(2,1)} %spread.1), calls=%async_computation | async-start | bytes 1376256 | tf_op jit(solution)/shard_map/all_to_all | solution.py:349
  7.0 8.1 %collective-permute-start = (bf16[672,128]{1,0:T(8,128)(2,1)}, bf16[672,128]{1,0:T(8,128)(2,1)S(1)}, u32[]{:S(2)}, u32[]{:S(2)}) collective-permute-start(bf16[672,128]{1,0:T(8,128)(2,1)} %bitcast.45), channel_id=1, source_target_pairs={{0,128},{128,256},{256,384},{384,512},{512,640},{1,129},{129,257},... | collective-permute-start | bytes 516104 | tf_op jit(solution)/shard_map/ppermute | solution.py:288
  11.3 8.5 %collective-permute-start.1 = (bf16[672,128]{1,0:T(8,128)(2,1)}, bf16[672,128]{1,0:T(8,128)(2,1)S(1)}, u32[]{:S(2)}, u32[]{:S(2)}) collective-permute-start(bf16[672,128]{1,0:T(8,128)(2,1)} %bitcast.46), channel_id=1, source_target_pairs={{128,0},{256,128},{384,256},{512,384},{640,512},{129,1},{257,129},... | collective-permute-start | bytes 516104 | tf_op jit(solution)/shard_map/ppermute | solution.py:288
  19.8 0.9 copy-start.9
  20.7 0.9 copy-start.10
  22.3 40.1 %collective-permute-start.2 = (bf16[1344,128]{1,0:T(8,128)(2,1)S(1)}, bf16[1344,128]{1,0:T(8,128)(2,1)S(1)}, u32[]{:S(2)}, u32[]{:S(2)}) collective-permute-start(bf16[1344,128]{1,0:T(8,128)(2,1)S(1)} %shard_map.132.own.both_ref), channel_id=1, source_target_pairs={{0,1},{1,2},{2,3},{3,0},{4,5},{5,6},{6,7},{7,4},{8,9},{9,10},{10,1... | collective-permute-start | bytes 1032200 | tf_op jit(solution)/shard_map/ppermute | solution.py:296
  25.9 36.5 %collective-permute-start.3 = (bf16[1344,128]{1,0:T(8,128)(2,1)S(1)}, bf16[1344,128]{1,0:T(8,128)(2,1)}, u32[]{:S(2)}, u32[]{:S(2)}) collective-permute-start(bf16[1344,128]{1,0:T(8,128)(2,1)S(1)} %shard_map.132.own.both_ref), channel_id=1, source_target_pairs={{0,3},{1,0},{2,1},{3,2},{4,7},{5,4},{6,5},{7,6},{8,11},{9,8},{10,9... | collective-permute-start | bytes 1032200 | tf_op jit(solution)/shard_map/ppermute | solution.py:296
  29.3 33.0 %collective-permute-start.4 = (bf16[1344,128]{1,0:T(8,128)(2,1)S(1)}, bf16[1344,128]{1,0:T(8,128)(2,1)}, u32[]{:S(2)}, u32[]{:S(2)}) collective-permute-start(bf16[1344,128]{1,0:T(8,128)(2,1)S(1)} %shard_map.132.own.both_ref), channel_id=1, source_target_pairs={{0,2},{1,3},{2,0},{3,1},{4,6},{5,7},{6,4},{7,5},{8,10},{9,11},{10,... | collective-permute-start | bytes 1032200 | tf_op jit(solution)/shard_map/ppermute | solution.py:296
  33.3 1.3 copy-start.1
  34.6 1.3 copy-start.3
  36.0 26.4 %copy-start.2 = (bf16[1,2688,256]{2,1,0:T(8,128)(2,1)S(1)}, bf16[1,2688,256]{2,1,0:T(8,128)(2,1)}, u32[]{:S(2)}) copy-start(bf16[1,2688,256]{2,1,0:T(8,128)(2,1)} %param.19) | copy-start | bytes 4128772
  36.0 26.4 %copy-start.4 = (bf16[1,2688,256]{2,1,0:T(8,128)(2,1)S(1)}, bf16[1,2688,256]{2,1,0:T(8,128)(2,1)}, u32[]{:S(2)}) copy-start(bf16[1,2688,256]{2,1,0:T(8,128)(2,1)} %param.20) | copy-start | bytes 4128772
  36.0 26.4 %copy-start.5 = (bf16[1,512,2688]{2,1,0:T(8,128)(2,1)S(1)}, bf16[1,512,2688]{2,1,0:T(8,128)(2,1)}, u32[]{:S(2)}) copy-start(bf16[1,512,2688]{2,1,0:T(8,128)(2,1)} %param.21) | copy-start | bytes 8257540
  38.4 16.8 %collective-permute-start.6 = (bf16[128,512]{1,0:T(8,128)(2,1)S(1)}, bf16[128,512]{1,0:T(8,128)(2,1)S(1)}, u32[]{:S(2)}, u32[]{:S(2)}) collective-permute-start(bf16[128,512]{1,0:T(8,128)(2,1)S(1)} %get-tuple-element.28.kv_ref.own), channel_id=1, source_target_pairs={{0,16},{4,20},{8,24},{12,28},{16,32},{20,36},{24,40},{28,44},{32,4... | collective-permute-start | bytes 393224 | tf_op jit(solution)/shard_map/ppermute | solution.py:277
  41.0 19.4 %collective-permute-start.5 = (bf16[128,512]{1,0:T(8,128)(2,1)S(1)}, bf16[128,512]{1,0:T(8,128)(2,1)S(1)}, u32[]{:S(2)}, u32[]{:S(2)}) collective-permute-start(bf16[128,512]{1,0:T(8,128)(2,1)S(1)} %get-tuple-element.28.kv_ref.own), channel_id=1, source_target_pairs={{0,8},{4,12},{8,16},{12,20},{16,24},{20,28},{24,32},{28,36},{32,40... | collective-permute-start | bytes 393224 | tf_op jit(solution)/shard_map/ppermute | solution.py:277
  55.8 9.8 %collective-permute-start.7 = (bf16[128,512]{1,0:T(8,128)(2,1)S(1)}, bf16[128,512]{1,0:T(8,128)(2,1)S(1)}, u32[]{:S(2)}, u32[]{:S(2)}) collective-permute-start(bf16[128,512]{1,0:T(8,128)(2,1)S(1)} %shard_map.134), channel_id=1, source_target_pairs={{0,4},{4,0},{8,12},{12,8},{16,20},{20,16},{24,28},{28,24},{32,36},... | collective-permute-start | bytes 393224 | tf_op jit(solution)/shard_map/ppermute | solution.py:282
  60.4 5.2 %collective-permute-start.8 = (bf16[128,512]{1,0:T(8,128)(2,1)S(1)}, bf16[128,512]{1,0:T(8,128)(2,1)S(1)}, u32[]{:S(2)}, u32[]{:S(2)}) collective-permute-start(bf16[128,512]{1,0:T(8,128)(2,1)S(1)} %collective-permute-done.5.two), channel_id=1, source_target_pairs={{0,4},{4,0},{8,12},{12,8},{16,20},{20,16},{24,28},{28,24},{32,36},... | collective-permute-start | bytes 393224 | tf_op jit(solution)/shard_map/ppermute | solution.py:282
  62.4 3.3 %copy-start.12 = (s32[1,4096]{1,0:T(1,128)S(1)}, s32[1,4096]{1,0:T(1,128)}, u32[]{:S(2)}) copy-start(s32[1,4096]{1,0:T(1,128)} %param.23) | copy-start | bytes 49156
  65.6 43.5 %copy-start.13 = (s32[1,4096]{1,0:T(1,128)S(1)}, s32[1,4096]{1,0:T(1,128)}, u32[]{:S(2)}) copy-start(s32[1,4096]{1,0:T(1,128)} %param.22) | copy-start | bytes 49156
  68.8 22.4 %collective-permute-start.9 = (bf16[256,512]{1,0:T(8,128)(2,1)S(1)}, bf16[256,512]{1,0:T(8,128)(2,1)S(1)}, u32[]{:S(2)}, u32[]{:S(2)}) collective-permute-start(bf16[256,512]{1,0:T(8,128)(2,1)S(1)} %get-tuple-element.33), channel_id=1, source_target_pairs={{0,4},{4,0},{8,12},{12,8},{16,20},{20,16},{24,28},{28,24},{32,36},... | collective-permute-start | bytes 786440 | tf_op jit(solution)/shard_map/ppermute | solution.py:282
  71.2 12.5 %collective-permute-start.13 = (bf16[128,512]{1,0:T(8,128)(2,1)S(1)}, bf16[128,512]{1,0:T(8,128)(2,1)S(1)}, u32[]{:S(2)}, u32[]{:S(2)}) collective-permute-start(bf16[128,512]{1,0:T(8,128)(2,1)S(1)} %get-tuple-element.38.kv_ref.own), channel_id=1, source_target_pairs={{0,16},{4,20},{8,24},{12,28},{16,32},{20,36},{24,40},{28,44},{32,4... | collective-permute-start | bytes 393224 | tf_op jit(solution)/shard_map/ppermute | solution.py:277
  73.1 16.1 %collective-permute-start.12 = (bf16[128,512]{1,0:T(8,128)(2,1)S(1)}, bf16[128,512]{1,0:T(8,128)(2,1)S(1)}, u32[]{:S(2)}, u32[]{:S(2)}) collective-permute-start(bf16[128,512]{1,0:T(8,128)(2,1)S(1)} %get-tuple-element.38.kv_ref.own), channel_id=1, source_target_pairs={{0,8},{4,12},{8,16},{12,20},{16,24},{20,28},{24,32},{28,36},{32,40... | collective-permute-start | bytes 393224 | tf_op jit(solution)/shard_map/ppermute | solution.py:277
  84.3 24.9 %collective-permute-start.14 = (bf16[128,512]{1,0:T(8,128)(2,1)S(1)}, bf16[128,512]{1,0:T(8,128)(2,1)S(1)}, u32[]{:S(2)}, u32[]{:S(2)}) collective-permute-start(bf16[128,512]{1,0:T(8,128)(2,1)S(1)} %shard_map.137), channel_id=1, source_target_pairs={{0,4},{4,0},{8,12},{12,8},{16,20},{20,16},{24,28},{28,24},{32,36},... | collective-permute-start | bytes 393224 | tf_op jit(solution)/shard_map/ppermute | solution.py:282
  89.2 19.9 %collective-permute-start.15 = (bf16[128,512]{1,0:T(8,128)(2,1)S(1)}, bf16[128,512]{1,0:T(8,128)(2,1)S(1)}, u32[]{:S(2)}, u32[]{:S(2)}) collective-permute-start(bf16[128,512]{1,0:T(8,128)(2,1)S(1)} %collective-permute-done.12.two), channel_id=1, source_target_pairs={{0,4},{4,0},{8,12},{12,8},{16,20},{20,16},{24,28},{28,24},{32,36},... | collective-permute-start | bytes 393224 | tf_op jit(solution)/shard_map/ppermute | solution.py:282
  91.8 24.2 %collective-permute-start.10 = (bf16[128,512]{1,0:T(8,128)(2,1)S(1)}, bf16[128,512]{1,0:T(8,128)(2,1)S(1)}, u32[]{:S(2)}, u32[]{:S(2)}) collective-permute-start(bf16[128,512]{1,0:T(8,128)(2,1)S(1)} %get-tuple-element.35), channel_id=1, source_target_pairs={{8,0},{12,4},{16,8},{20,12},{24,16},{28,20},{32,24},{36,28},{40,32... | collective-permute-start | bytes 393224 | tf_op jit(solution)/shard_map/ppermute | solution.py:277
  107.2 8.8 %collective-permute-start.11 = (bf16[128,512]{1,0:T(8,128)(2,1)S(1)}, bf16[128,512]{1,0:T(8,128)(2,1)S(1)}, u32[]{:S(2)}, u32[]{:S(2)}) collective-permute-start(bf16[128,512]{1,0:T(8,128)(2,1)S(1)} %get-tuple-element.36), channel_id=1, source_target_pairs={{16,0},{20,4},{24,8},{28,12},{32,16},{36,20},{40,24},{44,28},{48,3... | collective-permute-start | bytes 393224 | tf_op jit(solution)/shard_map/ppermute | solution.py:277
  117.6 1.1 copy-start.6
  118.7 22.7 %copy-start.8 = (bf16[1,128,672]{1,2,0:T(8,128)(2,1)S(1)}, bf16[1,128,672]{1,2,0:T(8,128)(2,1)}, u32[]{:S(2)}) copy-start(bf16[1,128,672]{1,2,0:T(8,128)(2,1)} %param.14) | copy-start | bytes 516100
  118.7 22.7 %all-to-all-start.1 = ((bf16[4,1360,128]{2,1,0:T(8,128)(2,1)}), bf16[4,1360,128]{2,1,0:T(8,128)(2,1)S(1)}, u32[]{:S(2)}, u32[]{:S(2)}) async-start(bf16[4,1360,128]{2,1,0:T(8,128)(2,1)} %copy-done.6), calls=%async_computation.1 | async-start | bytes 2785280 | tf_op jit(solution)/shard_map/all_to_all | solution.py:395
